TPU v7x, 128 devices: a whole 4x4x4 slice. The times are simulated.
128 devices in a mesh: blk: 16 (over y_lo, x, core), mp: 8 (over z, y_hi).
Axes of the slice: x: 4, y: 4 (y_hi: 2, y_lo: 2; y = y_hi * 2 + y_lo), z: 4, core: 2. Of those that a mesh axis runs over, the one named last changes fastest.
Arguments:
- features: bfloat16 [32768, 768], P('blk', 'mp'), may hold values from -9 to 9
- edge_dst: int32 [1024], P('blk'), may hold values from 0 to 15
- edge_src: int32 [1024], P('blk'), may hold values from 0 to 255
- edge_mask: int32 [1024, 128, 128], P('blk'), may hold values 0 or 1
- gin_in: bfloat16 [768, 768], P(None, 'mp'), may hold values from -0.21875 to 0.21875
- gin_out: bfloat16 [768, 768], P('mp'), may hold values from -0.21875 to 0.21875
- w_query: bfloat16 [768, 512], P(None, 'mp'), may hold values from -1 to 1
- w_key: bfloat16 [768, 512], P(None, 'mp'), may hold values from -1 to 1
- w_value: bfloat16 [768, 512], P(None, 'mp'), may hold values from -0.21875 to 0.21875
- w_attn_out: bfloat16 [512, 768], P('mp'), may hold values from -4 to 4
- ffn_in: bfloat16 [768, 1536], P(None, 'mp'), may hold values from -0.21875 to 0.21875
- ffn_out: bfloat16 [1536, 768], P('mp'), may hold values from -0.15625 to 0.15625
Outputs:
- layer_out: bfloat16 [32768, 768], P('blk', 'mp')
Inputs may be any that keep to these rules, and one draw needn't show every extreme that they name: `edge_dst`: local destination block of an edge block. `edge_src`: source block over the whole batch; several edge blocks may share a pair.
All inputs are finite; a program needn't handle non-finite values. No bound on the sum of `edge_mask` on one device may be relied on, other than what follows from the above.
Results may differ from a plain program's by a relative error of at most 0.011.
Values may be sent and summed in bfloat16 or wider, within the bound.
A program may use at most 128 MiB of HBM per device.

v0:
```python
import math

import jax
import jax.numpy as jnp
from jax import lax
from jax.sharding import PartitionSpec as P

HEAD_DIM = 64
BLOCK = 128


def neighbour_parts(features, edge_dst, edge_src, edge_mask):
    rows, cols = features.shape
    local_blocks = rows // BLOCK
    edge_count = edge_src.shape[0]

    def collect(pulled_all, piece, start):
        count = piece.shape[0] // BLOCK
        blocks = piece.reshape(count, BLOCK, cols)
        inside = jnp.logical_and(edge_src >= 0, edge_src < count)
        pulled = jnp.take(blocks, jnp.clip(edge_src, 0, count - 1), axis=0)
        return jnp.where(inside[:, None, None], pulled, pulled_all)

    def neighbour_finish(pulled_all):
        summand_terms = jnp.einsum(
            "ers,esf->erf",
            edge_mask.astype(jnp.bfloat16),
            pulled_all,
            preferred_element_type=jnp.float32,
        )
        target_nodes = (
            edge_dst[:, None] == jnp.arange(local_blocks, dtype=jnp.int32)[None, :]
        ).astype(jnp.float32)
        running_total = jnp.einsum(
            "cy,cla->yla", target_nodes, summand_terms, precision=lax.Precision.HIGHEST
        )
        return running_total.reshape(rows, cols)

    empty = jnp.zeros((edge_count, BLOCK, cols), features.dtype)
    return (collect, neighbour_finish, empty)


def attention_parts(whole, w_query, w_key, w_value):
    rows = whole.shape[0]
    heads = w_query.shape[1] // HEAD_DIM
    scale = 1.0 / math.sqrt(HEAD_DIM)
    queries = jnp.dot(whole, w_query, preferred_element_type=jnp.float32).astype(jnp.bfloat16)
    keys = jnp.dot(whole, w_key, preferred_element_type=jnp.float32).astype(jnp.bfloat16)
    values = jnp.dot(whole, w_value, preferred_element_type=jnp.float32).astype(jnp.bfloat16)
    query_heads = queries.reshape(rows, heads, HEAD_DIM)

    def add_keys(state, pieces, start):
        key_row_matrix, value_rows = pieces
        count = key_row_matrix.shape[0] // rows
        key_blocks = key_row_matrix.reshape(count, rows, heads, HEAD_DIM)
        value_blocks = value_rows.reshape(count, rows, heads, HEAD_DIM)

        def one_block(carry, operands):
            best, running_total, summed = carry
            key_block, value_block = operands
            scores = (
                jnp.einsum(
                    "qhd,khd->hqk", query_heads, key_block, preferred_element_type=jnp.float32
                )
                * scale
            )
            newest = jnp.maximum(best, jnp.max(scores, axis=-1))
            fade = jnp.exp(best - newest)
            expo = jnp.exp(scores - newest[..., None])
            running_total = running_total * fade + jnp.sum(expo, axis=-1)
            summed = summed * fade[..., None] + jnp.einsum(
                "hqk,khd->hqd",
                expo.astype(jnp.bfloat16),
                value_block,
                preferred_element_type=jnp.float32,
            )
            return ((newest, running_total, summed), None)

        state, _ = lax.scan(one_block, state, (key_blocks, value_blocks))
        return state

    def attention_finish(state):
        best, running_total, summed = state
        attended = (summed / running_total[..., None]).astype(jnp.bfloat16)
        return attended.transpose(1, 0, 2).reshape(rows, heads * HEAD_DIM)

    start_state = (
        jnp.full((heads, rows), -1e30, jnp.float32),
        jnp.zeros((heads, rows), jnp.float32),
        jnp.zeros((heads, rows, HEAD_DIM), jnp.float32),
    )
    return (add_keys, attention_finish, start_state, keys, values)


def per_device(
    features,
    edge_dst,
    edge_src,
    edge_mask,
    gin_in,
    gin_out,
    w_query,
    w_key,
    w_value,
    w_attn_out,
    ffn_in,
    ffn_out,
):
    rows, cols = features.shape
    width = cols * lax.axis_size("mp")
    whole = lax.all_gather(features, "mp", axis=1, tiled=True)
    collect, completed_rows, empty = neighbour_parts(features, edge_dst, edge_src, edge_mask)
    add_keys, finish_keys, start_state, keys, values = attention_parts(
        whole, w_query, w_key, w_value
    )
    pulled_all = collect(empty, lax.all_gather(features, "blk", axis=0, tiled=True), jnp.int32(0))
    state = add_keys(
        start_state,
        (
            lax.all_gather(keys, "blk", axis=0, tiled=True),
            lax.all_gather(values, "blk", axis=0, tiled=True),
        ),
        jnp.int32(0),
    )
    gathered = completed_rows(pulled_all)
    attended = finish_keys(state)
    local_share = (features.astype(jnp.float32) + gathered * 0.25).astype(jnp.bfloat16)
    local_in = lax.all_gather(local_share, "mp", axis=1, tiled=True)
    local_hidden = jax.nn.relu(
        jnp.dot(local_in, gin_in, preferred_element_type=jnp.float32)
    ).astype(jnp.bfloat16)
    partial_sum = jnp.dot(local_hidden, gin_out, preferred_element_type=jnp.float32) + jnp.dot(
        attended, w_attn_out, preferred_element_type=jnp.float32
    )
    mixed = lax.psum(partial_sum, "mp") + whole.astype(jnp.float32)
    row_average = jnp.sum(mixed, axis=1, keepdims=True) / width
    square_row = jnp.sum(mixed * mixed, axis=1, keepdims=True) / width
    normed = (
        (mixed - row_average) * lax.rsqrt(square_row - row_average * row_average + 1e-05)
    ).astype(jnp.bfloat16)
    mixed_share = lax.dynamic_slice_in_dim(mixed, lax.axis_index("mp") * cols, cols, 1)
    ffn_hidden = jax.nn.relu(jnp.dot(normed, ffn_in, preferred_element_type=jnp.float32)).astype(
        jnp.bfloat16
    )
    ffn_terms = jnp.dot(ffn_hidden, ffn_out, preferred_element_type=jnp.float32)
    return (
        mixed_share + lax.psum_scatter(ffn_terms, "mp", scatter_dimension=1, tiled=True)
    ).astype(jnp.bfloat16)


def solution(mesh):
    return jax.shard_map(
        per_device,
        mesh=mesh,
        in_specs=(
            P("blk", "mp"),
            P("blk"),
            P("blk"),
            P("blk", None, None),
            P(None, "mp"),
            P("mp", None),
            P(None, "mp"),
            P(None, "mp"),
            P(None, "mp"),
            P("mp", None),
            P(None, "mp"),
            P("mp", None),
        ),
        out_specs=P("blk", "mp"),
        check_vma=False,
    )
```

profile of v0, /device:TPU:0, one launch (start us, length us, event | category | flops | bytes accessed | tf_op | source)
XLA Modules:
  0.0 1044.9 jit_solution(14462335083314807584)
XLA Ops:
  8.1 67.0 %all-gather.10.cloned.1.call-done = bf16[2048,768]{0,1:T(8,128)(2,1)} async-done(((bf16[2048,96]{0,1:T(8,128)(2,1)}), bf16[2048,768]{0,1:T(8,128)(2,1)}) %all-gather.10.cloned.1.call-update) | async-done | bytes 3145744 | tf_op jit(solution)/shard_map/all_gather | solution.py:111
  82.4 34.4 %all-gather.6.cloned.1.call-done = bf16[32768,96]{0,1:T(8,128)(2,1)} async-done(((bf16[2048,96]{0,1:T(8,128)(2,1)}), bf16[32768,96]{0,1:T(8,128)(2,1)}) %all-gather.6.cloned.1.call-update) | async-done | bytes 6291472 | tf_op jit(solution)/shard_map/all_gather | solution.py:116
  136.5 20.1 %all-gather.12.cloned.1.call-done = bf16[32768,64]{0,1:T(8,128)(2,1)} async-done(((bf16[2048,64]{0,1:T(8,128)(2,1)}), bf16[32768,64]{0,1:T(8,128)(2,1)}) %all-gather.12.cloned.1.call-update) | async-done | bytes 4194320 | tf_op jit(solution)/shard_map/all_gather | solution.py:120
  165.4 30.1 %all-gather.14.cloned.1.call-done = bf16[32768,64]{0,1:T(8,128)(2,1)} async-done(((bf16[2048,64]{0,1:T(8,128)(2,1)}), bf16[32768,64]{0,1:T(8,128)(2,1)}) %all-gather.14.cloned.1.call-update) | async-done | bytes 4194320 | tf_op jit(solution)/shard_map/all_gather | solution.py:121
  204.3 440.0 %while.15 = (s32[]{:T(128)}, f32[1,2048]{1,0:T(1,128)S(1)}, f32[1,2048]{1,0:T(1,128)S(1)}, f32[1,2048,64]{1,2,0:T(8,128)}, bf16[16,2048,1,64]{1,3,2,0:T(8,128)(2...) while((s32[]{:T(128)}, f32[1,2048]{1,0:T(1,128)S(1)}, ...), condition=%wide.region_3.4_spmd.clone, body=%wide.region_0.0_spmd.clone.sunk | while | flops 1107699712 | bytes 52298852 | solution.py:79
  204.3 9.2 multiply_reduce_fusion.3
  222.2 9.6 fusion.82
  231.9 9.2 multiply_reduce_fusion.3
  249.7 9.8 fusion.82
  259.5 9.2 multiply_reduce_fusion.3
  277.3 9.7 fusion.82
  287.0 9.2 multiply_reduce_fusion.3
  304.8 9.7 fusion.82
  314.5 9.2 multiply_reduce_fusion.3
  332.3 9.7 fusion.82
  342.0 9.2 multiply_reduce_fusion.3
  359.8 9.7 fusion.82
  369.5 9.2 multiply_reduce_fusion.3
  387.3 9.7 fusion.82
  396.9 9.2 multiply_reduce_fusion.3
  414.8 9.7 fusion.82
  424.4 9.2 multiply_reduce_fusion.3
  442.2 9.7 fusion.82
  469.7 9.7 fusion.82
  497.2 9.7 fusion.82
  524.7 9.7 fusion.82
  552.2 9.7 fusion.82
  579.7 9.7 fusion.82
  607.2 9.7 fusion.82
  634.7 9.7 fusion.82
  660.3 260.5 %all-reduce.2.cloned.1.call-done = f32[2048,768]{1,0:T(8,128)} async-done(((f32[2048,768]{1,0:T(8,128)}), f32[2048,768]{1,0:T(8,128)}) %all-reduce.2.cloned.1.call-update) | async-done | bytes 6291472 | tf_op jit(solution)/shard_map/psum | solution.py:135
  935.4 98.3 %reduce-scatter.4.cloned.1.call-done = f32[96,2048]{1,0:T(8,128)} async-done(((f32[768,2048]{1,0:T(8,128)}), f32[96,2048]{1,0:T(8,128)}) %reduce-scatter.4.cloned.1.call-update) | async-done | bytes 786448
  (126 shorter events, 283.2 us)
Async XLA Ops:
  6.5 921.3 %copy-start = (bf16[192,768]{1,0:T(8,128)(2,1)S(1)}, bf16[192,768]{1,0:T(8,128)(2,1)}, u32[]{:S(2)}) copy-start(bf16[192,768]{1,0:T(8,128)(2,1)} %param.25) | copy-start | bytes 884740
  6.5 72.0 %copy-start.4 = (bf16[768,64]{0,1:T(8,128)(2,1)S(1)}, bf16[768,64]{0,1:T(8,128)(2,1)}, u32[]{:S(2)}) copy-start(bf16[768,64]{0,1:T(8,128)(2,1)} %param.22) | copy-start | bytes 294916
  6.5 73.5 %copy-start.6 = (s32[64]{0:T(128)S(1)}, s32[64]{0:T(128)}, u32[]{:S(2)}) copy-start(s32[64]{0:T(128)} %param.16) | copy-start | bytes 772
  6.5 68.5 %all-gather.10.cloned.1.call-start = ((), (), s32[]{:S(2)}) async-start(), calls=%async_computation.3 | async-start | bytes 3538944 | tf_op jit(solution)/shard_map/all_gather | solution.py:111
  7.3 109.5 %all-gather.6.cloned.1.call-start = ((), (), s32[]{:S(2)}) async-start(), calls=%async_computation.1 | async-start | bytes 6684672 | tf_op jit(solution)/shard_map/all_gather | solution.py:116
  8.0 148.6 %all-gather.12.cloned.1.call-start = ((), (), s32[]{:S(2)}) async-start(), calls=%async_computation.4 | async-start | bytes 4456448 | tf_op jit(solution)/shard_map/all_gather | solution.py:120
  75.0 3.5 copy-start.1
  78.5 117.0 %all-gather.14.cloned.1.call-start = ((), (), s32[]{:S(2)}) async-start(), calls=%async_computation.5 | async-start | bytes 4456448 | tf_op jit(solution)/shard_map/all_gather | solution.py:121
  80.0 564.3 %all-gather.8.cloned.1.call-start = ((), (), s32[]{:S(2)}) async-start(), calls=%async_computation.2 | async-start | bytes 3538944 | tf_op jit(solution)/shard_map/all_gather | solution.py:128
  127.9 4.3 copy-start.5
  132.3 2.9 copy-start.2
  136.2 784.6 %all-reduce.2.cloned.1.call-start = ((), (), s32[]{:S(2)}) async-start(), calls=%async_computation.6 | async-start | bytes 12582912 | tf_op jit(solution)/shard_map/psum | solution.py:135
  657.1 376.6 %reduce-scatter.4.cloned.1.call-start = ((), (), s32[]{:S(2)}) async-start(), calls=%async_computation.7 | async-start | bytes 7077888
  660.3 267.5 %copy-start.3 = (bf16[768,192]{0,1:T(8,128)(2,1)S(1)}, bf16[768,192]{0,1:T(8,128)(2,1)}, u32[]{:S(2)}) copy-start(bf16[768,192]{0,1:T(8,128)(2,1)} %param.24) | copy-start | bytes 884740
Sparse Core Ops, SparseCore 0:
  9.7 65.3 all-gather.9
  76.7 39.9 all-gather.5
  118.4 38.1 all-gather.11
  158.1 37.3 all-gather.13
  197.6 62.9 all-gather.7
  657.2 263.5 all-reduce.1
  935.5 98.1 reduce-scatter.3
where the time goes:
time: 1050 us; the launch traced here: 1040 us
  waiting for transfers between devices  512 us (49%)
  matrix products  337 us (32%)
  other arithmetic  148 us (14%)
  local copies, waits for them, and re-layouts  34.5 us (3%)
  between operations  13.6 us (1%)
    psum x1, waiting for transfers between devices, per_device(): mixed = lax.psum(partial_sum, 'mp') + whole.astype(jnp.float32)  261 us
    dot_general x16, matrix products, one_block(): jnp.einsum('hqk,khd->hqd', expo.astype(jnp.bfloat16), value_block, prefer...  155 us
    dot_general x16, matrix products, one_block(): jnp.einsum('qhd,khd->hqk', query_heads, key_block, preferred_element_type...  147 us
    reduce_sum x16, other arithmetic, one_block(): running_total = running_total * fade + jnp.sum(expo, axis=-1)  137 us
    unnamed x8, waiting for transfers between devices  99.8 us
    all_gather x1, waiting for transfers between devices, per_device(): whole = lax.all_gather(features, 'mp', axis=1, tiled=True)  67 us
    all_gather x1, waiting for transfers between devices, per_device(): lax.all_gather(features, 'blk', axis=0, tiled=True)  34.4 us
    all_gather x1, waiting for transfers between devices, per_device(): lax.all_gather(values, 'blk', axis=0, tiled=True)  30.1 us
  transfers between devices with their start and end apart: 7, of which 6 were waited for; matrix products, arithmetic and copies ran while one was open for 47% of the time, Pallas kernels for 0%

commit v1 on v0

v1 whole, which is shorter than its diff:
```python
import functools
import math

import jax
import jax.numpy as jnp
from jax import lax
from jax.experimental import pallas as pl
from jax.experimental.pallas import tpu as pltpu
from jax.sharding import PartitionSpec as P

HEAD_DIM = 64
BLOCK = 128
Q_TILE = 1024
K_TILE = 1024


def neighbour_sum(features, edge_dst, edge_src, edge_mask, all_features):
    rows, cols = features.shape
    local_blocks = rows // BLOCK
    count = all_features.shape[0] // BLOCK
    blocks = all_features.reshape(count, BLOCK, cols)
    pulled = jnp.take(blocks, jnp.clip(edge_src, 0, count - 1), axis=0)
    summand_terms = jnp.einsum(
        "ers,esf->erf",
        edge_mask.astype(jnp.bfloat16),
        pulled,
        preferred_element_type=jnp.float32,
    )
    target_nodes = (
        edge_dst[:, None] == jnp.arange(local_blocks, dtype=jnp.int32)[None, :]
    ).astype(jnp.float32)
    running_total = jnp.einsum(
        "cy,cla->yla", target_nodes, summand_terms, precision=lax.Precision.HIGHEST
    )
    return running_total.reshape(rows, cols)


def flash_kernel(q_ref, k_ref, v_ref, o_ref, m_ref, l_ref, acc_ref):
    j = pl.program_id(1)

    @pl.when(j == 0)
    def _():
        m_ref[...] = jnp.full(m_ref.shape, -jnp.inf, jnp.float32)
        l_ref[...] = jnp.zeros(l_ref.shape, jnp.float32)
        acc_ref[...] = jnp.zeros(acc_ref.shape, jnp.float32)

    s = lax.dot_general(
        q_ref[...], k_ref[...], (((1,), (1,)), ((), ())), preferred_element_type=jnp.float32
    )
    m_prev = m_ref[...]
    m_new = jnp.maximum(m_prev, jnp.max(s, axis=1, keepdims=True))
    alpha = jnp.exp(m_prev - m_new)
    p = jnp.exp(s - m_new)
    l_ref[...] = alpha * l_ref[...] + jnp.sum(p, axis=1, keepdims=True)
    acc_ref[...] = alpha * acc_ref[...] + jnp.dot(
        p.astype(jnp.bfloat16), v_ref[...], preferred_element_type=jnp.float32
    )
    m_ref[...] = m_new

    @pl.when(j == pl.num_programs(1) - 1)
    def _():
        o_ref[...] = (acc_ref[...] / l_ref[...]).astype(o_ref.dtype)


def flash_attention(q, k, v):
    rows, dim = q.shape
    keys_n = k.shape[0]
    tq = min(Q_TILE, rows)
    tk = min(K_TILE, keys_n)
    grid = (rows // tq, keys_n // tk)
    return pl.pallas_call(
        flash_kernel,
        grid=grid,
        in_specs=[
            pl.BlockSpec((tq, dim), lambda i, j: (i, 0)),
            pl.BlockSpec((tk, dim), lambda i, j: (j, 0)),
            pl.BlockSpec((tk, dim), lambda i, j: (j, 0)),
        ],
        out_specs=pl.BlockSpec((tq, dim), lambda i, j: (i, 0)),
        out_shape=jax.ShapeDtypeStruct((rows, dim), jnp.bfloat16),
        scratch_shapes=[
            pltpu.VMEM((tq, 1), jnp.float32),
            pltpu.VMEM((tq, 1), jnp.float32),
            pltpu.VMEM((tq, dim), jnp.float32),
        ],
        compiler_params=pltpu.CompilerParams(
            dimension_semantics=("arbitrary", "arbitrary")
        ),
        cost_estimate=pl.CostEstimate(
            flops=4 * rows * keys_n * dim,
            transcendentals=rows * keys_n,
            bytes_accessed=2 * (rows * dim * 2 + grid[0] * keys_n * dim * 2),
        ),
    )(q, k, v)


def per_device(
    features,
    edge_dst,
    edge_src,
    edge_mask,
    gin_in,
    gin_out,
    w_query,
    w_key,
    w_value,
    w_attn_out,
    ffn_in,
    ffn_out,
):
    rows, cols = features.shape
    n_mp = lax.axis_size("mp")
    width = cols * n_mp
    share = rows // n_mp
    me = lax.axis_index("mp")
    heads = w_query.shape[1] // HEAD_DIM
    scale = 1.0 / math.sqrt(HEAD_DIM)

    whole = lax.all_gather(features, "mp", axis=1, tiled=True)
    all_features = lax.all_gather(features, "blk", axis=0, tiled=True)
    gin_in_full = lax.all_gather(gin_in, "mp", axis=1, tiled=True)
    gin_out_full = lax.all_gather(gin_out, "mp", axis=0, tiled=True)
    w_attn_out_full = lax.all_gather(w_attn_out, "mp", axis=0, tiled=True)
    ffn_in_full = lax.all_gather(ffn_in, "mp", axis=1, tiled=True)
    ffn_out_full = lax.all_gather(ffn_out, "mp", axis=0, tiled=True)

    queries = jnp.dot(whole, w_query, preferred_element_type=jnp.float32).astype(jnp.bfloat16)
    keys = jnp.dot(whole, w_key, preferred_element_type=jnp.float32).astype(jnp.bfloat16)
    values = jnp.dot(whole, w_value, preferred_element_type=jnp.float32).astype(jnp.bfloat16)
    queries = queries * jnp.bfloat16(scale)
    keys_all = lax.all_gather(keys, "blk", axis=0, tiled=True)
    values_all = lax.all_gather(values, "blk", axis=0, tiled=True)

    gathered = neighbour_sum(features, edge_dst, edge_src, edge_mask, all_features)
    local_share = (features.astype(jnp.float32) + gathered * 0.25).astype(jnp.bfloat16)

    attended = jnp.concatenate(
        [
            flash_attention(
                queries[:, h * HEAD_DIM : (h + 1) * HEAD_DIM],
                keys_all[:, h * HEAD_DIM : (h + 1) * HEAD_DIM],
                values_all[:, h * HEAD_DIM : (h + 1) * HEAD_DIM],
            )
            for h in range(heads)
        ],
        axis=1,
    )

    local_in = lax.all_to_all(local_share, "mp", 0, 1, tiled=True)
    attended_rows = lax.all_to_all(attended, "mp", 0, 1, tiled=True)
    own_rows = lax.dynamic_slice_in_dim(whole, me * share, share, 0).astype(jnp.float32)

    local_hidden = jax.nn.relu(
        jnp.dot(local_in, gin_in_full, preferred_element_type=jnp.float32)
    ).astype(jnp.bfloat16)
    mixed = (
        own_rows
        + jnp.dot(local_hidden, gin_out_full, preferred_element_type=jnp.float32)
        + jnp.dot(attended_rows, w_attn_out_full, preferred_element_type=jnp.float32)
    )
    row_average = jnp.sum(mixed, axis=1, keepdims=True) / width
    square_row = jnp.sum(mixed * mixed, axis=1, keepdims=True) / width
    normed = (
        (mixed - row_average) * lax.rsqrt(square_row - row_average * row_average + 1e-05)
    ).astype(jnp.bfloat16)
    ffn_hidden = jax.nn.relu(
        jnp.dot(normed, ffn_in_full, preferred_element_type=jnp.float32)
    ).astype(jnp.bfloat16)
    out_rows = (
        mixed + jnp.dot(ffn_hidden, ffn_out_full, preferred_element_type=jnp.float32)
    ).astype(jnp.bfloat16)
    return lax.all_to_all(out_rows, "mp", 1, 0, tiled=True)


def solution(mesh):
    return jax.shard_map(
        per_device,
        mesh=mesh,
        in_specs=(
            P("blk", "mp"),
            P("blk"),
            P("blk"),
            P("blk", None, None),
            P(None, "mp"),
            P("mp", None),
            P(None, "mp"),
            P(None, "mp"),
            P(None, "mp"),
            P("mp", None),
            P(None, "mp"),
            P("mp", None),
        ),
        out_specs=P("blk", "mp"),
        check_vma=False,
    )
```

time: 1050 us -> 483 us (0.46)
  matrix products: 337 us -> 19.5 us
  waiting for transfers between devices: 512 us -> 198 us
  Pallas kernels: 0 us -> 163 us
  other arithmetic: 148 us -> 1.17 us
  blocking collectives: 0 us -> 56.3 us
  local copies, waits for them, and re-layouts: 34.5 us -> 18.9 us
  starting transfers between devices: 0.43 us -> 12 us
    dot_general x39 -> x8, matrix products: 329 us -> 19.5 us  [the longest x1 3.93 us: per_device(): jnp.dot(ffn_hidden, ffn_out_full, preferred_element_type=jnp.float32)]
    psum x1 -> x0, waiting for transfers between devices: 261 us -> none  [per_device(): mixed = lax.psum(partial_sum, 'mp') + whole.astype(jnp.float32)]
    pallas_call x0 -> x1, Pallas kernels: none -> 163 us  [flash_attention(): pl.pallas_call(flash_kernel, grid=grid, in_specs=[pl.BlockSpec((tq, dim),...]
    reduce_sum x17 -> x0, other arithmetic: 144 us -> none  [the longest x16 137 us: one_block(): running_total = running_total * fade + jnp.sum(expo, axis=-1)]
    unnamed x8, waiting for transfers between devices: 99.8 us -> 3.89 us
    all_gather x0 -> x1, blocking collectives: none -> 43.8 us  [per_device(): w_attn_out_full = lax.all_gather(w_attn_out, 'mp', axis=0, tiled=True)]
    all_gather x4 -> x7, waiting for transfers between devices: 84.5 us -> 120 us  [the longest x1 54.3 us: per_device(): values_all = lax.all_gather(values, 'blk', axis=0, tiled=True)]
    unnamed x19 -> x15, local copies, waits for them, and re-layouts: 19.2 us -> 1.95 us
  transfers between devices with their start and end apart: 7 -> 10, of which waited for: 6 -> 5; matrix products, arithmetic and copies ran while one was open for 47% -> 7% of each run, Pallas kernels for 0% -> 34%
where the time goes in v1:
time: 483 us
  waiting for transfers between devices  198 us (41%)
  Pallas kernels  163 us (34%)
  blocking collectives  56.3 us (12%)
  matrix products  19.5 us (4%)
  local copies, waits for them, and re-layouts  18.9 us (4%)
  between operations  13.7 us (3%)
  starting transfers between devices  12 us (2%)
    pallas_call x1, Pallas kernels, flash_attention(): pl.pallas_call(flash_kernel, grid=grid, in_specs=[pl.BlockSpec((tq, dim),...  163 us
    all_gather x1, waiting for transfers between devices, per_device(): whole = lax.all_gather(features, 'mp', axis=1, tiled=True)  67 us
    all_gather x1, waiting for transfers between devices, per_device(): values_all = lax.all_gather(values, 'blk', axis=0, tiled=True)  54.3 us
    all_gather x1, blocking collectives, per_device(): w_attn_out_full = lax.all_gather(w_attn_out, 'mp', axis=0, tiled=True)  43.8 us
    all_gather x1, waiting for transfers between devices, per_device(): keys_all = lax.all_gather(keys, 'blk', axis=0, tiled=True)  33.9 us
    all_gather x1, waiting for transfers between devices, per_device(): ffn_out_full = lax.all_gather(ffn_out, 'mp', axis=0, tiled=True)  31.9 us
    all_to_all x1, blocking collectives, per_device(): return lax.all_to_all(out_rows, 'mp', 1, 0, tiled=True)  12.6 us
  transfers between devices with their start and end apart: 10, of which 5 were waited for; matrix products, arithmetic and copies ran while one was open for 7% of the time, Pallas kernels for 34%

profile of v1, /device:TPU:0, one launch (start us, length us, event | category | flops | bytes accessed | tf_op | source)
XLA Modules:
  0.0 482.5 jit_solution(17813781783775939871)
XLA Ops:
  6.5 0.7 all-gather.9.cloned.1.call-update
  7.3 0.7 all-gather.11.cloned.1.call-update
  8.1 67.0 %all-gather.9.cloned.1.call-done = bf16[2048,768]{0,1:T(8,128)(2,1)} async-done(((bf16[2048,96]{0,1:T(8,128)(2,1)}), bf16[2048,768]{0,1:T(8,128)(2,1)}) %all-gather.9.cloned.1.call-update) | async-done | bytes 3145744 | tf_op jit(solution)/shard_map/all_gather | solution.py:119
  75.0 2.7 convolution_convert_fusion.1
  77.7 1.0 copy.49
  78.8 1.6 convolution_convert_fusion
  80.4 1.0 copy.50
  81.5 0.5 all-gather.13.cloned.1.call-update
  82.7 0.7 all-gather.21.cloned.1.call-update
  83.4 0.7 all-gather.23.cloned.1.call-update
  84.2 43.8 %all_gather.33 = bf16[512,768]{1,0:T(8,128)(2,1)} all-gather(bf16[64,768]{1,0:T(8,128)(2,1)} %param.21), channel_id=1, replica_groups=mesh['blk'=16,'mp'=8] {'mp'}, dimensions={0}, use_global_device_ids=true | all-gather | bytes 884736 | tf_op jit(solution)/shard_map/all_gather | solution.py:123
  127.9 0.8 constant_dynamic-slice_fusion
  128.8 1.9 copy.54
  130.7 1.6 convolution_convert_fusion.2
  132.5 0.8 broadcast_multiply_fusion.q_ref
  133.3 6.5 %copy_bitcast_fusion = bf16[256,128,96]{1,2,0:T(8,128)(2,1)} fusion(bf16[32768,96]{0,1:T(8,128)(2,1)} %all-gather.11.cloned.1.call-done), kind=kLoop, calls=%fused_computation.1 | loop fusion | bytes 12582912 | tf_op jit(solution)/shard_map/reshape | solution.py:21
  139.8 3.6 gather_fusion
  143.5 3.8 fusion.5
  147.3 2.9 fusion.10
  150.6 0.8 copy.66
  151.3 4.8 %all-to-all-start = ((bf16[8,256,96]{1,2,0:T(8,128)(2,1)}), bf16[8,256,96]{1,2,0:T(8,128)(2,1)S(1)}, u32[]{:S(2)}, u32[]{:S(2)}) async-start(bf16[8,256,96]{1,2,0:T(8,128)(2,1)} %bitcast.44), calls=%async_computation | async-start | bytes 786432 | tf_op jit(solution)/shard_map/all_to_all | solution.py:149
  156.2 33.9 %all-gather.17.cloned.1.call-done.k_ref = bf16[32768,64]{1,0:T(8,128)(2,1)} async-done(((bf16[2048,64]{1,0:T(8,128)(2,1)}), bf16[32768,64]{1,0:T(8,128)(2,1)}) %all-gather.17.cloned.1.call-update) | async-done | bytes 4194320 | tf_op jit(solution)/shard_map/all_gather | solution.py:131
  190.1 54.3 %all-gather.19.cloned.1.call-done.v_ref = bf16[32768,64]{1,0:T(8,128)(2,1)} async-done(((bf16[2048,64]{1,0:T(8,128)(2,1)}), bf16[32768,64]{1,0:T(8,128)(2,1)}) %all-gather.19.cloned.1.call-update) | async-done | bytes 4194320 | tf_op jit(solution)/shard_map/all_gather | solution.py:132
  244.4 163.3 %shard_map.118 = bf16[2048,64]{1,0:T(8,128)(2,1)} custom-call(bf16[2048,64]{1,0:T(8,128)(2,1)} %broadcast_multiply_fusion.q_ref, bf16[32768,64]{1,0:T(8,128)(2,1)} %all-gather.17.cloned.1.call-done.k_ref, bf16[32768,64]{1,0:T(8,128)(2,1)} %all-gather.19.cloned.1.call-done.v_ref), custom_call_target="tpu_custom_call" | custom-call | flops 17179869184 | bytes 17301504 | tf_op jit(solution)/shard_map/pallas_call | solution.py:71
  407.6 1.9 copy.51
  409.6 6.9 %all-to-all-start.1 = ((bf16[8,256,64]{1,2,0:T(8,128)(2,1)}), bf16[8,256,64]{1,2,0:T(8,128)(2,1)S(1)}, u32[]{:S(2)}, u32[]{:S(2)}) async-start(bf16[8,256,64]{1,2,0:T(8,128)(2,1)} %copy.51), calls=%async_computation.1 | async-start | bytes 524288 | tf_op jit(solution)/shard_map/all_to_all | solution.py:150
  416.5 2.6 convolution_add_fusion.2
  419.1 6.6 %all-to-all-done.1 = bf16[8,256,64]{1,2,0:T(8,128)(2,1)S(1)} async-done(((bf16[8,256,64]{1,2,0:T(8,128)(2,1)}), bf16[8,256,64]{1,2,0:T(8,128)(2,1)S(1)}, u32[]{:S(2)}, u32[]{:S(2)}) %all-to-all-start.1) | async-done | bytes 262176 | tf_op jit(solution)/shard_map/all_to_all | solution.py:150
  426.3 31.9 %all-gather.23.cloned.1.call-done = bf16[1536,768]{1,0:T(8,128)(2,1)} async-done(((bf16[192,768]{1,0:T(8,128)(2,1)}), bf16[1536,768]{1,0:T(8,128)(2,1)}) %all-gather.23.cloned.1.call-update) | async-done | bytes 2359312 | tf_op jit(solution)/shard_map/all_gather | solution.py:125
  458.2 3.9 fusion.14
  462.3 12.6 %all_to_all.57 = bf16[256,8,96]{0,2,1:T(8,128)(2,1)S(1)} all-to-all(bf16[256,8,96]{0,2,1:T(8,128)(2,1)S(1)} %bitcast.46), channel_id=1, replica_groups=mesh['blk'=16,'mp'=8] {'mp'}, dimensions={1} | all-to-all | bytes 786432 | tf_op jit(solution)/shard_map/all_to_all | solution.py:172
  474.9 0.8 copy.57
  (37 shorter events, 2.2 us)
Async XLA Ops:
  6.5 68.5 %copy-start = (bf16[768,64]{0,1:T(8,128)(2,1)S(1)}, bf16[768,64]{0,1:T(8,128)(2,1)}, u32[]{:S(2)}) copy-start(bf16[768,64]{0,1:T(8,128)(2,1)} %param.19) | copy-start | bytes 294916
  6.5 68.5 %all-gather.9.cloned.1.call-start = ((), (), s32[]{:S(2)}) async-start(), calls=%async_computation.3 | async-start | bytes 3538944 | tf_op jit(solution)/shard_map/all_gather | solution.py:119
  7.3 126.1 %all-gather.11.cloned.1.call-start = ((), (), s32[]{:S(2)}) async-start(), calls=%async_computation.4 | async-start | bytes 6684672 | tf_op jit(solution)/shard_map/all_gather | solution.py:120
  8.0 182.1 %all-gather.17.cloned.1.call-start = ((), (), s32[]{:S(2)}) async-start(), calls=%async_computation.7 | async-start | bytes 8912896 | tf_op jit(solution)/shard_map/all_gather | solution.py:131
  75.0 3.8 copy-start.1
  78.8 5.3 %copy-start.6 = (s32[64]{0:T(128)S(1)}, s32[64]{0:T(128)}, u32[]{:S(2)}) copy-start(s32[64]{0:T(128)} %param.14) | copy-start | bytes 772
  78.8 165.6 %all-gather.19.cloned.1.call-start = ((), (), s32[]{:S(2)}) async-start(), calls=%async_computation.8 | async-start | bytes 8912896 | tf_op jit(solution)/shard_map/all_gather | solution.py:132
  81.4 335.1 %all-gather.13.cloned.1.call-start = ((), (), s32[]{:S(2)}) async-start(), calls=%async_computation.5 | async-start | bytes 1327104 | tf_op jit(solution)/shard_map/all_gather | solution.py:121
  82.0 334.5 %all-gather.15.cloned.1.call-start = ((), (), s32[]{:S(2)}) async-start(), calls=%async_computation.6 | async-start | bytes 1327104 | tf_op jit(solution)/shard_map/all_gather | solution.py:122
  82.6 343.6 %all-gather.21.cloned.1.call-start = ((), (), s32[]{:S(2)}) async-start(), calls=%async_computation.9 | async-start | bytes 2654208 | tf_op jit(solution)/shard_map/all_gather | solution.py:124
  83.4 374.8 %all-gather.23.cloned.1.call-start = ((), (), s32[]{:S(2)}) async-start(), calls=%async_computation.10 | async-start | bytes 2654208 | tf_op jit(solution)/shard_map/all_gather | solution.py:125
  143.5 3.8 copy-start.5
  147.3 2.9 copy-start.2
  151.3 258.2 %all-to-all-start = ((bf16[8,256,96]{1,2,0:T(8,128)(2,1)}), bf16[8,256,96]{1,2,0:T(8,128)(2,1)S(1)}, u32[]{:S(2)}, u32[]{:S(2)}) async-start(bf16[8,256,96]{1,2,0:T(8,128)(2,1)} %bitcast.44), calls=%async_computation | async-start | bytes 786432 | tf_op jit(solution)/shard_map/all_to_all | solution.py:149
  156.2 260.4 %copy-start.4 = (bf16[256,768]{1,0:T(8,128)(2,1)S(1)}, bf16[256,768]{1,0:T(8,128)(2,1)}, u32[]{:S(2)}) copy-start(bf16[256,768]{1,0:T(8,128)(2,1)} %copy.54) | copy-start | bytes 1179652
  409.6 16.1 %copy-start.3 = (bf16[512,768]{1,0:T(8,128)(2,1)S(1)}, bf16[512,768]{1,0:T(8,128)(2,1)}, u32[]{:S(2)}) copy-start(bf16[512,768]{1,0:T(8,128)(2,1)} %all_gather.33) | copy-start | bytes 2359300
  409.6 16.1 %all-to-all-start.1 = ((bf16[8,256,64]{1,2,0:T(8,128)(2,1)}), bf16[8,256,64]{1,2,0:T(8,128)(2,1)S(1)}, u32[]{:S(2)}, u32[]{:S(2)}) async-start(bf16[8,256,64]{1,2,0:T(8,128)(2,1)} %copy.51), calls=%async_computation.1 | async-start | bytes 524288 | tf_op jit(solution)/shard_map/all_to_all | solution.py:150
Sparse Core Ops, SparseCore 0:
  9.7 65.3 all-gather.8
  76.7 54.6 all-gather.10
  133.1 56.9 all-gather.16
  191.6 52.6 all-gather.18
  246.5 48.1 all-gather.12
  296.9 46.0 all-gather.14
  345.2 55.1 all-gather.20
  402.7 55.4 all-gather.22

commit v2 on v1

--- a/solution.py
+++ b/solution.py
@@ -35,7 +35,7 @@
     return running_total.reshape(rows, cols)
 
 
-def flash_kernel(q_ref, k_ref, v_ref, o_ref, m_ref, l_ref, acc_ref):
+def flash_kernel(dim, q_ref, kv_ref, o_ref, m_ref, l_ref, acc_ref):
     j = pl.program_id(1)
 
     @pl.when(j == 0)
@@ -44,8 +44,9 @@
         l_ref[...] = jnp.zeros(l_ref.shape, jnp.float32)
         acc_ref[...] = jnp.zeros(acc_ref.shape, jnp.float32)
 
+    kv = kv_ref[...]
     s = lax.dot_general(
-        q_ref[...], k_ref[...], (((1,), (1,)), ((), ())), preferred_element_type=jnp.float32
+        q_ref[...], kv, (((1,), (1,)), ((), ())), preferred_element_type=jnp.float32
     )
     m_prev = m_ref[...]
     m_new = jnp.maximum(m_prev, jnp.max(s, axis=1, keepdims=True))
@@ -53,45 +54,47 @@
     p = jnp.exp(s - m_new)
     l_ref[...] = alpha * l_ref[...] + jnp.sum(p, axis=1, keepdims=True)
     acc_ref[...] = alpha * acc_ref[...] + jnp.dot(
-        p.astype(jnp.bfloat16), v_ref[...], preferred_element_type=jnp.float32
+        p.astype(jnp.bfloat16), kv, preferred_element_type=jnp.float32
     )
     m_ref[...] = m_new
 
     @pl.when(j == pl.num_programs(1) - 1)
     def _():
-        o_ref[...] = (acc_ref[...] / l_ref[...]).astype(o_ref.dtype)
-
-
-def flash_attention(q, k, v):
+        o_ref[...] = (acc_ref[:, dim : 2 * dim] / l_ref[...]).astype(o_ref.dtype)
+
+
+def flash_attention(q, packed_all, head, heads):
     rows, dim = q.shape
-    keys_n = k.shape[0]
+    keys_n = packed_all.shape[0]
     tq = min(Q_TILE, rows)
     tk = min(K_TILE, keys_n)
     grid = (rows // tq, keys_n // tk)
+    assert heads == 1
+    lanes = 2 * dim
+    q_pad = jnp.concatenate([q, jnp.zeros((rows, lanes - dim), q.dtype)], axis=1)
     return pl.pallas_call(
-        flash_kernel,
+        functools.partial(flash_kernel, dim),
         grid=grid,
         in_specs=[
-            pl.BlockSpec((tq, dim), lambda i, j: (i, 0)),
-            pl.BlockSpec((tk, dim), lambda i, j: (j, 0)),
-            pl.BlockSpec((tk, dim), lambda i, j: (j, 0)),
+            pl.BlockSpec((tq, lanes), lambda i, j: (i, 0)),
+            pl.BlockSpec((tk, lanes), lambda i, j: (j, 0)),
         ],
         out_specs=pl.BlockSpec((tq, dim), lambda i, j: (i, 0)),
         out_shape=jax.ShapeDtypeStruct((rows, dim), jnp.bfloat16),
         scratch_shapes=[
             pltpu.VMEM((tq, 1), jnp.float32),
             pltpu.VMEM((tq, 1), jnp.float32),
-            pltpu.VMEM((tq, dim), jnp.float32),
+            pltpu.VMEM((tq, lanes), jnp.float32),
         ],
         compiler_params=pltpu.CompilerParams(
             dimension_semantics=("arbitrary", "arbitrary")
         ),
         cost_estimate=pl.CostEstimate(
-            flops=4 * rows * keys_n * dim,
+            flops=4 * rows * keys_n * lanes,
             transcendentals=rows * keys_n,
-            bytes_accessed=2 * (rows * dim * 2 + grid[0] * keys_n * dim * 2),
+            bytes_accessed=rows * lanes * 2 + grid[0] * keys_n * lanes * 2 + rows * dim * 2,
         ),
-    )(q, k, v)
+    )(q_pad, packed_all)
 
 
 def per_device(
@@ -116,20 +119,43 @@
     heads = w_query.shape[1] // HEAD_DIM
     scale = 1.0 / math.sqrt(HEAD_DIM)
 
-    whole = lax.all_gather(features, "mp", axis=1, tiled=True)
-    all_features = lax.all_gather(features, "blk", axis=0, tiled=True)
-    gin_in_full = lax.all_gather(gin_in, "mp", axis=1, tiled=True)
-    gin_out_full = lax.all_gather(gin_out, "mp", axis=0, tiled=True)
-    w_attn_out_full = lax.all_gather(w_attn_out, "mp", axis=0, tiled=True)
-    ffn_in_full = lax.all_gather(ffn_in, "mp", axis=1, tiled=True)
-    ffn_out_full = lax.all_gather(ffn_out, "mp", axis=0, tiled=True)
+    pieces = (features, gin_in, ffn_in, gin_out, w_attn_out, ffn_out)
+    flat = jnp.concatenate([x.reshape(-1) for x in pieces])
+    flat_all = lax.all_gather(flat, "mp", axis=0, tiled=False)
+    unpacked = []
+    offset = 0
+    for x in pieces:
+        size = x.size
+        unpacked.append(flat_all[:, offset : offset + size].reshape((n_mp,) + x.shape))
+        offset += size
+    feats_parts, gin_in_parts, ffn_in_parts, gin_out_parts, attn_out_parts, ffn_out_parts = unpacked
+
+    def join_columns(parts):
+        count, r, c = parts.shape
+        return parts.transpose(1, 0, 2).reshape(r, count * c)
+
+    def join_rows(parts):
+        count, r, c = parts.shape
+        return parts.reshape(count * r, c)
+
+    whole = join_columns(feats_parts)
+    gin_in_full = join_columns(gin_in_parts)
+    ffn_in_full = join_columns(ffn_in_parts)
+    gin_out_full = join_rows(gin_out_parts)
+    w_attn_out_full = join_rows(attn_out_parts)
+    ffn_out_full = join_rows(ffn_out_parts)
 
     queries = jnp.dot(whole, w_query, preferred_element_type=jnp.float32).astype(jnp.bfloat16)
     keys = jnp.dot(whole, w_key, preferred_element_type=jnp.float32).astype(jnp.bfloat16)
     values = jnp.dot(whole, w_value, preferred_element_type=jnp.float32).astype(jnp.bfloat16)
     queries = queries * jnp.bfloat16(scale)
-    keys_all = lax.all_gather(keys, "blk", axis=0, tiled=True)
-    values_all = lax.all_gather(values, "blk", axis=0, tiled=True)
+    kv_width = 2 * HEAD_DIM * heads
+    lane_pad = (-(kv_width + cols)) % 128
+    packed = jnp.concatenate(
+        [keys, values, features, jnp.zeros((rows, lane_pad), jnp.bfloat16)], axis=1
+    )
+    packed_all = lax.all_gather(packed, "blk", axis=0, tiled=True)
+    all_features = packed_all[:, kv_width : kv_width + cols]
 
     gathered = neighbour_sum(features, edge_dst, edge_src, edge_mask, all_features)
     local_share = (features.astype(jnp.float32) + gathered * 0.25).astype(jnp.bfloat16)
@@ -138,16 +164,19 @@
         [
             flash_attention(
                 queries[:, h * HEAD_DIM : (h + 1) * HEAD_DIM],
-                keys_all[:, h * HEAD_DIM : (h + 1) * HEAD_DIM],
-                values_all[:, h * HEAD_DIM : (h + 1) * HEAD_DIM],
+                packed_all,
+                h,
+                heads,
             )
             for h in range(heads)
         ],
         axis=1,
     )
 
-    local_in = lax.all_to_all(local_share, "mp", 0, 1, tiled=True)
-    attended_rows = lax.all_to_all(attended, "mp", 0, 1, tiled=True)
+    mixed_in = jnp.concatenate([local_share, attended], axis=1).reshape(n_mp, share, -1)
+    received = lax.all_to_all(mixed_in, "mp", 0, 0, tiled=False)
+    local_in = join_columns(received[:, :, :cols])
+    attended_rows = join_columns(received[:, :, cols:])
     own_rows = lax.dynamic_slice_in_dim(whole, me * share, share, 0).astype(jnp.float32)
 
     local_hidden = jax.nn.relu(
@@ -169,7 +198,8 @@
     out_rows = (
         mixed + jnp.dot(ffn_hidden, ffn_out_full, preferred_element_type=jnp.float32)
     ).astype(jnp.bfloat16)
-    return lax.all_to_all(out_rows, "mp", 1, 0, tiled=True)
+    out_parts = out_rows.reshape(share, n_mp, cols).transpose(1, 0, 2)
+    return lax.all_to_all(out_parts, "mp", 0, 0, tiled=False).reshape(rows, cols)
 
 
 def solution(mesh):

time: 483 us -> 556 us (1.15)
  local copies, waits for them, and re-layouts: 18.9 us -> 114 us
  blocking collectives: 56.3 us -> 17.2 us
  waiting for transfers between devices: 198 us -> 215 us
    all_gather x1 -> x0, blocking collectives: 43.8 us -> none  [per_device(): w_attn_out_full = lax.all_gather(w_attn_out, 'mp', axis=0, tiled=True)]
    all_gather x8 -> x2, waiting for transfers between devices: 187 us -> 215 us  [the longest x1 133 us: per_device(): flat_all = lax.all_gather(flat, 'mp', axis=0, tiled=False)]
    reshape x0 -> x11, local copies, waits for them, and re-layouts: none -> 23.2 us  [the longest x3 16.7 us: per_device(): flat_all[:, offset:offset + size].reshape((n_mp,) + x.shape)]
    slice x0 -> x8, local copies, waits for them, and re-layouts: none -> 21 us  [the longest x5 11.2 us: per_device(): flat_all[:, offset:offset + size].reshape((n_mp,) + x.shape)]
    unnamed x15 -> x32, local copies, waits for them, and re-layouts: 1.95 us -> 15.8 us
    all_gather x0 -> x1, local copies, waits for them, and re-layouts: none -> 12.9 us  [per_device(): flat_all = lax.all_gather(flat, 'mp', axis=0, tiled=False)]
    transpose x0 -> x3, local copies, waits for them, and re-layouts: none -> 11.8 us  [join_columns(): return parts.transpose(1, 0, 2).reshape(r, count * c)]
    another operation x0 -> x3, local copies, waits for them, and re-layouts: none -> 8 us  [join_rows(): return parts.reshape(count * r, c)]
  transfers between devices with their start and end apart: 10 -> 3, of which waited for: 5 -> 2; matrix products, arithmetic and copies ran while one was open for 7% -> 9% of each run, Pallas kernels for 34% -> 0%
where the time goes in v2:
time: 556 us; the launch traced here: 554 us
  waiting for transfers between devices  215 us (39%)
  Pallas kernels  163 us (29%)
  local copies, waits for them, and re-layouts  114 us (21%)
  matrix products  19.9 us (4%)
  blocking collectives  17.2 us (3%)
  between operations  13.7 us (2%)
  starting transfers between devices  6.75 us (1%)
    pallas_call x1, Pallas kernels, flash_attention(): pl.pallas_call(functools.partial(flash_kernel, dim), grid=grid, in_specs=...  163 us
    all_gather x1, waiting for transfers between devices, per_device(): flat_all = lax.all_gather(flat, 'mp', axis=0, tiled=False)  133 us
    all_gather x1, waiting for transfers between devices, per_device(): packed_all = lax.all_gather(packed, 'blk', axis=0, tiled=True)  81.7 us
    all_to_all x1, blocking collectives, per_device(): lax.all_to_all(out_parts, 'mp', 0, 0, tiled=False).reshape(rows, cols)  17.2 us
    reshape x3, local copies, waits for them, and re-layouts, per_device(): flat_all[:, offset:offset + size].reshape((n_mp,) + x.shape)  16.7 us
    unnamed x32, local copies, waits for them, and re-layouts  15.8 us
    all_gather x1, local copies, waits for them, and re-layouts, per_device(): flat_all = lax.all_gather(flat, 'mp', axis=0, tiled=False)  12.9 us
    transpose x3, local copies, waits for them, and re-layouts, join_columns(): return parts.transpose(1, 0, 2).reshape(r, count * c)  11.8 us
  transfers between devices with their start and end apart: 3, of which 2 were waited for; matrix products, arithmetic and copies ran while one was open for 9% of the time, Pallas kernels for 0%

profile of v2, /device:TPU:0, one launch (start us, length us, event | category | flops | bytes accessed | tf_op | source)
XLA Modules:
  0.0 554.0 jit_solution(11466413117100277284)
XLA Ops:
  15.3 133.4 %all-gather.6.cloned.1.call-done = bf16[5505024]{0:T(1024)(128)(2,1)} async-done(((bf16[688128]{0:T(1024)(128)(2,1)}), bf16[5505024]{0:T(1024)(128)(2,1)}) %all-gather.6.cloned.1.call-update) | async-done | bytes 11010064 | tf_op jit(solution)/shard_map/all_gather | solution.py:124
  148.7 12.9 %reshape.107 = bf16[8,688128]{1,0:T(8,128)(2,1)} reshape(bf16[5505024]{0:T(1024)(128)(2,1)} %all-gather.6.cloned.1.call-done) | data formatting | bytes 22020096 | tf_op jit(solution)/shard_map/all_gather | solution.py:124
  161.6 1.9 slice-done
  163.5 3.1 reshape.110
  166.6 7.4 %reshape.87 = bf16[8,2048,96]{2,1,0:T(8,128)(2,1)} reshape(bf16[1572864]{0:T(1024)(128)(2,1)} %reshape.110) | data formatting | bytes 6291456 | tf_op jit(solution)/shard_map/reshape | solution.py:129
  174.1 4.8 copy.87
  183.1 2.9 maximum_maximum_fusion
  189.8 4.0 fusion.30
  193.8 81.7 %all-gather.4.cloned.1.call-done.kv_ref = bf16[32768,256]{1,0:T(8,128)(2,1)} async-done(((bf16[2048,256]{1,0:T(8,128)(2,1)}), bf16[32768,256]{1,0:T(8,128)(2,1)}) %all-gather.4.cloned.1.call-update) | async-done | bytes 16777232 | tf_op jit(solution)/shard_map/all_gather | solution.py:157
  275.6 163.2 %shard_map.118 = bf16[2048,64]{1,0:T(8,128)(2,1)} custom-call(bf16[2048,128]{1,0:T(8,128)(2,1)} %concatenate.14.q_ref, bf16[32768,256]{1,0:T(8,128)(2,1)} %all-gather.4.cloned.1.call-done.kv_ref), custom_call_target="tpu_custom_call" | custom-call | flops 34359738368 | bytes 17563648 | tf_op jit(solution)/shard_map/pallas_call | solution.py:75
  440.0 7.1 %slice.39 = bf16[32768,96]{1,0:T(8,128)(2,1)} slice(bf16[32768,256]{1,0:T(8,128)(2,1)} %all-gather.4.cloned.1.call-done.kv_ref), slice={[0:32768], [128:224]} | slice | bytes 12582912 | tf_op jit(solution)/shard_map/slice | solution.py:158
  447.1 10.1 %copy.92 = bf16[256,128,96]{1,2,0:T(8,128)(2,1)} copy(bf16[256,128,96]{2,1,0:T(8,128)(2,1)} %bitcast.51) | data formatting | bytes 12582912 | tf_op jit(solution)/shard_map/reshape | solution.py:21
  457.2 4.7 gather_fusion
  461.9 4.3 fusion.5
  466.2 2.9 fusion.10
  470.4 6.7 %all-to-all-start = ((bf16[8,256,160]{1,2,0:T(8,128)(2,1)}), bf16[8,256,160]{1,2,0:T(8,128)(2,1)}, u32[]{:S(2)}, u32[]{:S(2)}) async-start(bf16[8,256,160]{1,2,0:T(8,128)(2,1)} %bitcast.56), calls=%async_computation | async-start | bytes 1310720 | tf_op jit(solution)/shard_map/all_to_all | solution.py:177
  477.1 3.2 fusion.31
  480.3 2.1 slice.44
  482.3 2.4 reshape_reshape.10
  484.8 2.8 reshape.112
  487.6 3.7 reshape.92
  491.3 2.5 copy.97
  493.8 2.8 reshape_reshape.9
  496.6 4.2 reshape.114
  500.8 5.6 %reshape.95 = bf16[8,768,192]{2,1,0:T(8,128)(2,1)} reshape(bf16[1179648]{0:T(1024)(128)(2,1)} %reshape.114) | data formatting | bytes 4718592 | tf_op jit(solution)/shard_map/reshape | solution.py:129
  506.5 4.5 copy.98
  511.7 1.9 copy.101
  513.7 2.7 reshape_reshape.11
  518.2 3.7 convolution_add_fusion.2
  522.9 2.4 fusion.29
  525.3 3.7 fusion.14
  529.2 17.2 %all_to_all.10 = bf16[8,256,96]{1,2,0:T(8,128)(2,1)S(1)} all-to-all(bf16[8,256,96]{1,2,0:T(8,128)(2,1)S(1)} %bitcast.59), channel_id=1, replica_groups=mesh['blk'=16,'mp'=8] {'mp'}, dimensions={0} | all-to-all | bytes 786432 | tf_op jit(solution)/shard_map/all_to_all | solution.py:202
  (63 shorter events, 23.6 us)
Async XLA Ops:
  6.5 172.3 %copy-start = (bf16[768,64]{0,1:T(8,128)(2,1)S(1)}, bf16[768,64]{0,1:T(8,128)(2,1)}, u32[]{:S(2)}) copy-start(bf16[768,64]{0,1:T(8,128)(2,1)} %param.19) | copy-start | bytes 294916
  6.5 6.3 %copy-start.5 = (bf16[2048,96]{0,1:T(8,128)(2,1)S(1)}, bf16[2048,96]{0,1:T(8,128)(2,1)}, u32[]{:S(2)}) copy-start(bf16[2048,96]{0,1:T(8,128)(2,1)} %param.12) | copy-start | bytes 1179652
  6.5 142.2 %all-gather.6.cloned.1.call-start = ((), (), s32[]{:S(2)}) async-start(), calls=%async_computation.3 | async-start | bytes 12386304 | tf_op jit(solution)/shard_map/all_gather | solution.py:124
  13.2 2.0 copy-start.2
  13.9 1.4 copy-start.9
  14.0 1.1 copy-start.4
  15.2 260.4 %all-gather.4.cloned.1.call-start = ((), (), s32[]{:S(2)}) async-start(), calls=%async_computation.2 | async-start | bytes 17825792 | tf_op jit(solution)/shard_map/all_gather | solution.py:157
  161.6 1.9 slice-start
  182.1 4.0 copy-start.7
  461.9 4.3 copy-start.8
  466.2 2.9 copy-start.6
  470.4 46.1 %all-to-all-start = ((bf16[8,256,160]{1,2,0:T(8,128)(2,1)}), bf16[8,256,160]{1,2,0:T(8,128)(2,1)}, u32[]{:S(2)}, u32[]{:S(2)}) async-start(bf16[8,256,160]{1,2,0:T(8,128)(2,1)} %bitcast.56), calls=%async_computation | async-start | bytes 1310720 | tf_op jit(solution)/shard_map/all_to_all | solution.py:177
  518.2 4.7 copy-start.3
  525.3 21.8 %copy-start.1 = (bf16[768,64]{0,1:T(8,128)(2,1)S(1)}, bf16[768,64]{0,1:T(8,128)(2,1)}, u32[]{:S(2)}) copy-start(bf16[768,64]{0,1:T(8,128)(2,1)} %param.19) | copy-start | bytes 294916
Sparse Core Ops, SparseCore 0:
  15.3 133.3 all-gather.5
  186.2 89.2 all-gather.3

commit v3 on v2

--- a/solution.py
+++ b/solution.py
@@ -119,8 +119,16 @@
     heads = w_query.shape[1] // HEAD_DIM
     scale = 1.0 / math.sqrt(HEAD_DIM)
 
-    pieces = (features, gin_in, ffn_in, gin_out, w_attn_out, ffn_out)
+    whole = lax.all_gather(features, "mp", axis=1, tiled=True)
+    queries = jnp.dot(whole, w_query, preferred_element_type=jnp.float32).astype(jnp.bfloat16)
+    keys = jnp.dot(whole, w_key, preferred_element_type=jnp.float32).astype(jnp.bfloat16)
+    values = jnp.dot(whole, w_value, preferred_element_type=jnp.float32).astype(jnp.bfloat16)
+    queries = queries * jnp.bfloat16(scale)
+    kv_all = lax.all_gather(jnp.concatenate([keys, values], axis=1), "blk", axis=0, tiled=True)
+    pieces = (gin_in, ffn_in, gin_out, w_attn_out, ffn_out)
     flat = jnp.concatenate([x.reshape(-1) for x in pieces])
+    kv_all, late_features, flat = lax.optimization_barrier((kv_all, features, flat))
+    all_features = lax.all_gather(late_features, "blk", axis=0, tiled=True)
     flat_all = lax.all_gather(flat, "mp", axis=0, tiled=False)
     unpacked = []
     offset = 0
@@ -128,64 +136,33 @@
         size = x.size
         unpacked.append(flat_all[:, offset : offset + size].reshape((n_mp,) + x.shape))
         offset += size
-    feats_parts, gin_in_parts, ffn_in_parts, gin_out_parts, attn_out_parts, ffn_out_parts = unpacked
+    gin_in_parts, ffn_in_parts, gin_out_parts, attn_out_parts, ffn_out_parts = unpacked
 
     def join_columns(parts):
         count, r, c = parts.shape
         return parts.transpose(1, 0, 2).reshape(r, count * c)
 
-    def join_rows(parts):
-        count, r, c = parts.shape
-        return parts.reshape(count * r, c)
-
-    whole = join_columns(feats_parts)
-    gin_in_full = join_columns(gin_in_parts)
+    gin_in_full = join_columns(gin_in_parts).reshape(n_mp, cols, width)
     ffn_in_full = join_columns(ffn_in_parts)
-    gin_out_full = join_rows(gin_out_parts)
-    w_attn_out_full = join_rows(attn_out_parts)
-    ffn_out_full = join_rows(ffn_out_parts)
-
-    queries = jnp.dot(whole, w_query, preferred_element_type=jnp.float32).astype(jnp.bfloat16)
-    keys = jnp.dot(whole, w_key, preferred_element_type=jnp.float32).astype(jnp.bfloat16)
-    values = jnp.dot(whole, w_value, preferred_element_type=jnp.float32).astype(jnp.bfloat16)
-    queries = queries * jnp.bfloat16(scale)
-    kv_width = 2 * HEAD_DIM * heads
-    lane_pad = (-(kv_width + cols)) % 128
-    packed = jnp.concatenate(
-        [keys, values, features, jnp.zeros((rows, lane_pad), jnp.bfloat16)], axis=1
-    )
-    packed_all = lax.all_gather(packed, "blk", axis=0, tiled=True)
-    all_features = packed_all[:, kv_width : kv_width + cols]
+    gin_out_full = gin_out_parts.reshape(width, width)
+    ffn_out_full = ffn_out_parts.reshape(-1, width)
 
     gathered = neighbour_sum(features, edge_dst, edge_src, edge_mask, all_features)
     local_share = (features.astype(jnp.float32) + gathered * 0.25).astype(jnp.bfloat16)
 
-    attended = jnp.concatenate(
-        [
-            flash_attention(
-                queries[:, h * HEAD_DIM : (h + 1) * HEAD_DIM],
-                packed_all,
-                h,
-                heads,
-            )
-            for h in range(heads)
-        ],
-        axis=1,
-    )
+    attended = flash_attention(queries, kv_all, 0, heads)
 
     mixed_in = jnp.concatenate([local_share, attended], axis=1).reshape(n_mp, share, -1)
     received = lax.all_to_all(mixed_in, "mp", 0, 0, tiled=False)
-    local_in = join_columns(received[:, :, :cols])
-    attended_rows = join_columns(received[:, :, cols:])
     own_rows = lax.dynamic_slice_in_dim(whole, me * share, share, 0).astype(jnp.float32)
 
     local_hidden = jax.nn.relu(
-        jnp.dot(local_in, gin_in_full, preferred_element_type=jnp.float32)
+        jnp.einsum("jrc,jcd->rd", received[:, :, :cols], gin_in_full, preferred_element_type=jnp.float32)
     ).astype(jnp.bfloat16)
     mixed = (
         own_rows
         + jnp.dot(local_hidden, gin_out_full, preferred_element_type=jnp.float32)
-        + jnp.dot(attended_rows, w_attn_out_full, preferred_element_type=jnp.float32)
+        + jnp.einsum("jrd,jde->re", received[:, :, cols:], attn_out_parts, preferred_element_type=jnp.float32)
     )
     row_average = jnp.sum(mixed, axis=1, keepdims=True) / width
     square_row = jnp.sum(mixed * mixed, axis=1, keepdims=True) / width

time: 556 us -> 403 us (0.72)
  waiting for transfers between devices: 215 us -> 103 us
  local copies, waits for them, and re-layouts: 114 us -> 72.4 us
    all_gather x1, waiting for transfers between devices: 133 us -> 0.01 us  [per_device(): flat_all = lax.all_gather(flat, 'mp', axis=0, tiled=False)]
    all_gather x1 -> x3, waiting for transfers between devices: 81.7 us -> 102 us  [the longest x1 67.7 us: per_device(): whole = lax.all_gather(features, 'mp', axis=1, tiled=True)]
    reshape x3 -> x2, local copies, waits for them, and re-layouts: 16.7 us -> 5.47 us  [per_device(): flat_all[:, offset:offset + size].reshape((n_mp,) + x.shape)]
    slice x3 -> x0, local copies, waits for them, and re-layouts: 9.83 us -> none  [the longest x1 7.09 us: per_device(): all_features = packed_all[:, kv_width:kv_width + cols]]
    transpose x3 -> x2, local copies, waits for them, and re-layouts: 11.8 us -> 3.7 us  [join_columns(): return parts.transpose(1, 0, 2).reshape(r, count * c)]
    slice x5 -> x4, local copies, waits for them, and re-layouts: 11.2 us -> 5.26 us  [per_device(): flat_all[:, offset:offset + size].reshape((n_mp,) + x.shape)]
    unnamed x32 -> x31, local copies, waits for them, and re-layouts: 15.8 us -> 16.6 us
  transfers between devices with their start and end apart: 3 -> 5, of which waited for: 2 -> 2; matrix products, arithmetic and copies ran while one was open for 9% -> 19% of each run, Pallas kernels for 0% -> 41%
where the time goes in v3:
time: 403 us; the launch traced here: 402 us
  Pallas kernels  163 us (40%)
  waiting for transfers between devices  103 us (26%)
  local copies, waits for them, and re-layouts  72.4 us (18%)
  matrix products  22.5 us (6%)
  blocking collectives  17.1 us (4%)
  between operations  13.4 us (3%)
  starting transfers between devices  7.08 us (2%)
    pallas_call x1, Pallas kernels, flash_attention(): pl.pallas_call(functools.partial(flash_kernel, dim), grid=grid, in_specs=...  163 us
    all_gather x1, waiting for transfers between devices, per_device(): whole = lax.all_gather(features, 'mp', axis=1, tiled=True)  67.7 us
    all_gather x1, waiting for transfers between devices, per_device(): lax.all_gather(jnp.concatenate([keys, values], axis=1), 'blk', axis=0, ti...  34.5 us
    all_to_all x1, blocking collectives, per_device(): lax.all_to_all(out_parts, 'mp', 0, 0, tiled=False).reshape(rows, cols)  17.1 us
    unnamed x31, local copies, waits for them, and re-layouts  16.6 us
    all_gather x1, local copies, waits for them, and re-layouts, per_device(): flat_all = lax.all_gather(flat, 'mp', axis=0, tiled=False)  9.58 us
  transfers between devices with their start and end apart: 5, of which 2 were waited for; matrix products, arithmetic and copies ran while one was open for 19% of the time, Pallas kernels for 41%

profile of v3, /device:TPU:0, one launch (start us, length us, event | category | flops | bytes accessed | tf_op | source)
XLA Modules:
  0.0 401.7 jit_solution(14239860694242225540)
XLA Ops:
  7.3 67.7 %all-gather.6.cloned.1.call-done = bf16[2048,768]{0,1:T(8,128)(2,1)} async-done(((bf16[2048,96]{0,1:T(8,128)(2,1)}), bf16[2048,768]{0,1:T(8,128)(2,1)}) %all-gather.6.cloned.1.call-update) | async-done | bytes 3145744 | tf_op jit(solution)/shard_map/all_gather | solution.py:122
  75.0 2.7 convolution_convert_fusion.2
  78.7 1.6 convolution_convert_fusion.1
  81.3 2.4 pad_maximum_fusion.1
  88.9 1.9 copy.62
  90.7 2.2 reshape.67
  92.9 1.6 constant_dynamic-update-slice_fusion.4
  94.5 1.7 constant_dynamic-update-slice_fusion.3
  96.2 1.6 constant_dynamic-update-slice_fusion.2
  99.2 34.5 %all-gather.8.cloned.1.call-done.kv_ref = bf16[32768,128]{1,0:T(8,128)(2,1)} async-done(((bf16[2048,128]{1,0:T(8,128)(2,1)}), bf16[32768,128]{1,0:T(8,128)(2,1)}) %all-gather.8.cloned.1.call-update) | async-done | bytes 8388624 | tf_op jit(solution)/shard_map/all_gather | solution.py:127
  135.1 2.0 copy.72
  139.9 163.2 %shard_map.118 = bf16[2048,64]{1,0:T(8,128)(2,1)} custom-call(bf16[2048,128]{1,0:T(8,128)(2,1)} %concatenate.14.q_ref, bf16[32768,128]{1,0:T(8,128)(2,1)} %all-gather.8.cloned.1.call-done.kv_ref), custom_call_target="tpu_custom_call" | custom-call | flops 34359738368 | bytes 17563648 | tf_op jit(solution)/shard_map/pallas_call | solution.py:75
  304.3 6.5 %copy_bitcast_fusion = bf16[256,128,96]{1,2,0:T(8,128)(2,1)} fusion(bf16[32768,96]{0,1:T(8,128)(2,1)} %all-gather.10.cloned.1.call-done), kind=kLoop, calls=%fused_computation.1 | loop fusion | bytes 12582912 | tf_op jit(solution)/shard_map/reshape | solution.py:21
  310.8 3.6 gather_fusion
  314.5 3.8 fusion.5
  318.3 2.9 fusion.11
  322.5 6.8 %all-to-all-start = ((bf16[8,256,160]{1,2,0:T(8,128)(2,1)}), bf16[8,256,160]{1,2,0:T(8,128)(2,1)}, u32[]{:S(2)}, u32[]{:S(2)}) async-start(bf16[8,256,160]{1,2,0:T(8,128)(2,1)} %bitcast.54), calls=%async_computation | async-start | bytes 1310720 | tf_op jit(solution)/shard_map/all_to_all | solution.py:156
  329.3 9.6 %reshape.87 = bf16[8,491520]{1,0:T(8,128)(2,1)} reshape(bf16[3932160]{0:T(1024)(128)(2,1)} %all-gather.12.cloned.1.call-done) | data formatting | bytes 15728640 | tf_op jit(solution)/shard_map/all_gather | solution.py:132
  338.9 3.7 fusion.37
  342.6 1.8 copy-done.2
  344.4 1.6 fusion.38
  345.9 2.5 reshape.94
  348.5 1.8 reshape.92
  352.3 2.1 reshape_reshape.9
  354.5 4.4 %reshape.75 = bf16[8,768,192]{2,1,0:T(8,128)(2,1)S(1)} reshape(bf16[1179648]{0:T(1024)(128)(2,1)} %reshape.94) | data formatting | bytes 4718592 | tf_op jit(solution)/shard_map/reshape | solution.py:137
  358.9 2.7 copy.69
  361.6 3.0 reshape_reshape.10
  364.6 2.5 reshape_reshape.11
  367.1 2.3 convolution_bitcast_fusion
  369.4 4.0 fusion.36
  373.4 3.7 fusion.15
  377.3 17.1 %all_to_all.10 = bf16[8,256,96]{1,2,0:T(8,128)(2,1)S(1)} all-to-all(bf16[8,256,96]{1,2,0:T(8,128)(2,1)S(1)} %bitcast.61), channel_id=1, replica_groups=mesh['blk'=16,'mp'=8] {'mp'}, dimensions={0} | all-to-all | bytes 786432 | tf_op jit(solution)/shard_map/all_to_all | solution.py:179
  (59 shorter events, 19.0 us)
Async XLA Ops:
  6.5 68.5 %copy-start = (bf16[768,64]{0,1:T(8,128)(2,1)S(1)}, bf16[768,64]{0,1:T(8,128)(2,1)}, u32[]{:S(2)}) copy-start(bf16[768,64]{0,1:T(8,128)(2,1)} %param.19) | copy-start | bytes 294916
  6.5 68.5 %all-gather.6.cloned.1.call-start = ((), (), s32[]{:S(2)}) async-start(), calls=%async_computation.2 | async-start | bytes 3538944 | tf_op jit(solution)/shard_map/all_gather | solution.py:122
  7.3 126.4 %all-gather.8.cloned.1.call-start = ((), (), s32[]{:S(2)}) async-start(), calls=%async_computation.3 | async-start | bytes 8912896 | tf_op jit(solution)/shard_map/all_gather | solution.py:127
  75.0 3.7 copy-start.3
  81.3 3.5 copy-start.8
  83.7 220.6 %all-gather.10.cloned.1.call-start = ((), (), s32[]{:S(2)}) async-start(), calls=%async_computation.4 | async-start | bytes 6684672 | tf_op jit(solution)/shard_map/all_gather | solution.py:131
  88.8 45.4 %copy-start.10 = (s32[64]{0:T(128)S(1)}, s32[64]{0:T(128)}, u32[]{:S(2)}) copy-start(s32[64]{0:T(128)} %param.14) | copy-start | bytes 772
  133.7 195.6 %all-gather.12.cloned.1.call-start = ((), (), s32[]{:S(2)}) async-start(), calls=%async_computation.5 | async-start | bytes 8847360 | tf_op jit(solution)/shard_map/all_gather | solution.py:132
  314.5 3.8 copy-start.9
  318.3 2.9 copy-start.5
  322.5 44.6 %all-to-all-start = ((bf16[8,256,160]{1,2,0:T(8,128)(2,1)}), bf16[8,256,160]{1,2,0:T(8,128)(2,1)}, u32[]{:S(2)}, u32[]{:S(2)}) async-start(bf16[8,256,160]{1,2,0:T(8,128)(2,1)} %bitcast.54), calls=%async_computation | async-start | bytes 1310720 | tf_op jit(solution)/shard_map/all_to_all | solution.py:156
  338.9 5.5 %copy-start.2 = (bf16[8,491520]{1,0:T(8,128)(2,1)S(1)}, bf16[8,491520]{1,0:T(8,128)(2,1)}, u32[]{:S(2)}) copy-start(bf16[8,491520]{1,0:T(8,128)(2,1)} %reshape.87) | copy-start | bytes 23592964
  361.6 3.0 copy-start.4
  364.6 2.5 slice-start
  367.1 2.3 copy-start.7
  369.4 4.0 %copy-start.6 = (bf16[1536,768]{1,0:T(8,128)(2,1)S(1)}, bf16[1536,768]{1,0:T(8,128)(2,1)}, u32[]{:S(2)}) copy-start(bf16[1536,768]{1,0:T(8,128)(2,1)} %reshape_reshape.11) | copy-start | bytes 7077892
  373.4 21.8 %copy-start.1 = (bf16[768,64]{0,1:T(8,128)(2,1)S(1)}, bf16[768,64]{0,1:T(8,128)(2,1)}, u32[]{:S(2)}) copy-start(bf16[768,64]{0,1:T(8,128)(2,1)} %param.19) | copy-start | bytes 294916
Sparse Core Ops, SparseCore 0:
  9.7 65.3 all-gather.5
  83.8 49.7 all-gather.7
  135.3 43.1 all-gather.9
  180.7 103.3 all-gather.11

commit v4 on v3

--- a/solution.py
+++ b/solution.py
@@ -10,8 +10,8 @@
 
 HEAD_DIM = 64
 BLOCK = 128
-Q_TILE = 1024
-K_TILE = 1024
+Q_TILE = 512
+K_TILE = 4096
 
 
 def neighbour_sum(features, edge_dst, edge_src, edge_mask, all_features):

time: 403 us -> 357 us (0.89)
  Pallas kernels: 163 us -> 118 us
    pallas_call x1, Pallas kernels: 163 us -> 118 us  [flash_attention(): pl.pallas_call(functools.partial(flash_kernel, dim), grid=grid, in_specs=...]
  transfers between devices with their start and end apart: 5 -> 5, of which waited for: 2 -> 3; matrix products, arithmetic and copies ran while one was open for 19% -> 21% of each run, Pallas kernels for 41% -> 33%
where the time goes in v4:
time: 357 us; the launch traced here: 356 us
  Pallas kernels  118 us (33%)
  waiting for transfers between devices  104 us (29%)
  local copies, waits for them, and re-layouts  72.4 us (20%)
  matrix products  22.8 us (6%)
  blocking collectives  17 us (5%)
  between operations  13.4 us (4%)
  starting transfers between devices  6.77 us (2%)
    pallas_call x1, Pallas kernels, flash_attention(): pl.pallas_call(functools.partial(flash_kernel, dim), grid=grid, in_specs=...  118 us
    all_gather x1, waiting for transfers between devices, per_device(): whole = lax.all_gather(features, 'mp', axis=1, tiled=True)  67.7 us
    all_gather x1, waiting for transfers between devices, per_device(): lax.all_gather(jnp.concatenate([keys, values], axis=1), 'blk', axis=0, ti...  34.5 us
    all_to_all x1, blocking collectives, per_device(): lax.all_to_all(out_parts, 'mp', 0, 0, tiled=False).reshape(rows, cols)  17 us
    unnamed x31, local copies, waits for them, and re-layouts  16.6 us
    all_gather x1, local copies, waits for them, and re-layouts, per_device(): flat_all = lax.all_gather(flat, 'mp', axis=0, tiled=False)  9.57 us
  transfers between devices with their start and end apart: 5, of which 3 were waited for; matrix products, arithmetic and copies ran while one was open for 21% of the time, Pallas kernels for 33%

profile of v4, /device:TPU:0, one launch (start us, length us, event | category | flops | bytes accessed | tf_op | source)
XLA Modules:
  0.0 356.5 jit_solution(11576359966125960240)
XLA Ops:
  7.3 67.7 %all-gather.6.cloned.1.call-done = bf16[2048,768]{0,1:T(8,128)(2,1)} async-done(((bf16[2048,96]{0,1:T(8,128)(2,1)}), bf16[2048,768]{0,1:T(8,128)(2,1)}) %all-gather.6.cloned.1.call-update) | async-done | bytes 3145744 | tf_op jit(solution)/shard_map/all_gather | solution.py:122
  75.0 2.7 convolution_convert_fusion.2
  78.7 1.6 convolution_convert_fusion.1
  81.3 2.4 pad_maximum_fusion.1
  88.9 1.9 copy.62
  90.7 2.2 reshape.67
  92.9 1.6 constant_dynamic-update-slice_fusion.4
  94.5 1.7 constant_dynamic-update-slice_fusion.3
  96.2 1.6 constant_dynamic-update-slice_fusion.2
  99.2 34.5 %all-gather.8.cloned.1.call-done.kv_ref = bf16[32768,128]{1,0:T(8,128)(2,1)} async-done(((bf16[2048,128]{1,0:T(8,128)(2,1)}), bf16[32768,128]{1,0:T(8,128)(2,1)}) %all-gather.8.cloned.1.call-update) | async-done | bytes 8388624 | tf_op jit(solution)/shard_map/all_gather | solution.py:127
  135.1 2.0 copy.72
  139.9 117.8 %shard_map.118 = bf16[2048,64]{1,0:T(8,128)(2,1)} custom-call(bf16[2048,128]{1,0:T(8,128)(2,1)} %concatenate.14.q_ref, bf16[32768,128]{1,0:T(8,128)(2,1)} %all-gather.8.cloned.1.call-done.kv_ref), custom_call_target="tpu_custom_call" | custom-call | flops 34359738368 | bytes 34340864 | tf_op jit(solution)/shard_map/pallas_call | solution.py:75
  258.9 6.6 %copy_bitcast_fusion = bf16[256,128,96]{1,2,0:T(8,128)(2,1)} fusion(bf16[32768,96]{0,1:T(8,128)(2,1)} %all-gather.10.cloned.1.call-done), kind=kLoop, calls=%fused_computation.1 | loop fusion | bytes 12582912 | tf_op jit(solution)/shard_map/reshape | solution.py:21
  265.5 3.6 %gather_fusion = bf16[64,128,96]{1,2,0:T(8,128)(2,1)S(1)} fusion(bf16[256,128,96]{1,2,0:T(8,128)(2,1)} %copy_bitcast_fusion, s32[1024]{0:T(1024)S(1)} %pad_clamp_fusion), kind=kCustom, calls=%fused_computation | custom fusion | bytes 3145984 | tf_op jit(solution)/shard_map/jit(_take)/gather | solution.py:22
  269.2 4.1 %fusion.5 = f32[64,128,96]{1,2,0:T(8,128)S(1)} fusion(s32[64,128,128]{2,1,0:T(8,128)} %param.15, bf16[64,128,96]{1,2,0:T(8,128)(2,1)S(1)} %gather_fusion, pred[64]{0:T(512)(128)(4,1)S(1)} %get-tuple-element.13), kind=kOutput, calls=%fused_computation.11 | convolution fusion | flops 203161600 | bytes 8912960 | tf_op jit(solution)/shard_map/ers,esf->erf/dot_general | solution.py:23
  273.3 2.9 fusion.11
  277.4 6.5 %all-to-all-start = ((bf16[8,256,160]{1,2,0:T(8,128)(2,1)}), bf16[8,256,160]{1,2,0:T(8,128)(2,1)}, u32[]{:S(2)}, u32[]{:S(2)}) async-start(bf16[8,256,160]{1,2,0:T(8,128)(2,1)} %bitcast.54), calls=%async_computation | async-start | bytes 1310720 | tf_op jit(solution)/shard_map/all_to_all | solution.py:156
  284.1 9.6 %reshape.87 = bf16[8,491520]{1,0:T(8,128)(2,1)} reshape(bf16[3932160]{0:T(1024)(128)(2,1)} %all-gather.12.cloned.1.call-done) | data formatting | bytes 15728640 | tf_op jit(solution)/shard_map/all_gather | solution.py:132
  293.7 3.7 %fusion.37 = (bf16[8,147456]{1,0:T(8,128)(2,1)S(1)}, bf16[8,147456]{1,0:T(8,128)(2,1)}) fusion(bf16[8,491520]{1,0:T(8,128)(2,1)} %reshape.87), kind=kLoop, calls=%fused_computation.58 | loop fusion | bytes 9437184 | tf_op jit(solution)/shard_map/slice | solution.py:137
  297.4 1.8 copy-done.2
  299.2 1.6 fusion.38
  300.8 2.5 reshape.94
  303.3 1.8 reshape.92
  307.2 2.1 reshape_reshape.9
  309.3 4.4 %reshape.75 = bf16[8,768,192]{2,1,0:T(8,128)(2,1)S(1)} reshape(bf16[1179648]{0:T(1024)(128)(2,1)} %reshape.94) | data formatting | bytes 4718592 | tf_op jit(solution)/shard_map/reshape | solution.py:137
  313.8 2.7 copy.69
  316.5 3.0 reshape_reshape.10
  319.4 2.5 reshape_reshape.11
  321.9 2.3 convolution_bitcast_fusion
  324.2 4.0 %fusion.36 = (f32[256]{0:T(256)S(1)}, f32[256]{0:T(256)S(1)}, f32[256,768]{1,0:T(8,128)}) fusion(f32[256,768]{1,0:T(8,128)} %convolution_bitcast_fusion, bf16[768,768]{1,0:T(8,128)(2,1)} %reshape_reshape.10, bf16[8,96,768]{2,1,0:T(8,128)(2,1)} %reshape_reshape.9, bf16[8,256,160]{1,2,0:T(8,128)(2,1)} %all-to-all-done, bf16[256,768]{1,0:T(8,128)(2,1)S(1)} %copy-done.7), kind=kOutput, calls=%fused_computation.57 | convolution fusion | flops 605552128 | bytes 4720640 | tf_op jit(solution)/shard_map/dot_general | solution.py:164
  328.3 3.7 %fusion.15 = bf16[256,768]{1,0:T(8,128)(2,1)S(1)} fusion(f32[256,768]{1,0:T(8,128)} %get-tuple-element.21, bf16[1536,768]{1,0:T(8,128)(2,1)S(1)} %copy-done.6, bf16[768,1536]{0,1:T(8,128)(2,1)} %bitcast.60, f32[256]{0:T(256)S(1)} %get-tuple-element.20, f32[256]{0:T(256)S(1)} %get-tuple-element.19), kind=kOutput, calls=%fused_computation.21 | convolution fusion | flops 1209729024 | bytes 5900288 | tf_op jit(solution)/shard_map/dot_general | solution.py:176
  332.1 17.0 %all_to_all.10 = bf16[8,256,96]{1,2,0:T(8,128)(2,1)S(1)} all-to-all(bf16[8,256,96]{1,2,0:T(8,128)(2,1)S(1)} %bitcast.61), channel_id=1, replica_groups=mesh['blk'=16,'mp'=8] {'mp'}, dimensions={0} | all-to-all | bytes 786432 | tf_op jit(solution)/shard_map/all_to_all | solution.py:179
  (59 shorter events, 19.2 us)
Async XLA Ops:
  6.5 68.5 %copy-start = (bf16[768,64]{0,1:T(8,128)(2,1)S(1)}, bf16[768,64]{0,1:T(8,128)(2,1)}, u32[]{:S(2)}) copy-start(bf16[768,64]{0,1:T(8,128)(2,1)} %param.19) | copy-start | bytes 294916
  6.5 68.5 %all-gather.6.cloned.1.call-start = ((), (), s32[]{:S(2)}) async-start(), calls=%async_computation.2 | async-start | bytes 3538944 | tf_op jit(solution)/shard_map/all_gather | solution.py:122
  7.3 126.4 %all-gather.8.cloned.1.call-start = ((), (), s32[]{:S(2)}) async-start(), calls=%async_computation.3 | async-start | bytes 8912896 | tf_op jit(solution)/shard_map/all_gather | solution.py:127
  75.0 3.7 %copy-start.3 = (bf16[2048,768]{0,1:T(8,128)(2,1)S(1)}, bf16[2048,768]{0,1:T(8,128)(2,1)}, u32[]{:S(2)}) copy-start(bf16[2048,768]{0,1:T(8,128)(2,1)} %all-gather.6.cloned.1.call-done) | copy-start | bytes 9437188
  81.3 3.5 copy-start.8
  83.7 175.2 %all-gather.10.cloned.1.call-start = ((), (), s32[]{:S(2)}) async-start(), calls=%async_computation.4 | async-start | bytes 6684672 | tf_op jit(solution)/shard_map/all_gather | solution.py:131
  88.8 45.4 %copy-start.10 = (s32[64]{0:T(128)S(1)}, s32[64]{0:T(128)}, u32[]{:S(2)}) copy-start(s32[64]{0:T(128)} %param.14) | copy-start | bytes 772
  133.7 150.4 %all-gather.12.cloned.1.call-start = ((), (), s32[]{:S(2)}) async-start(), calls=%async_computation.5 | async-start | bytes 8847360 | tf_op jit(solution)/shard_map/all_gather | solution.py:132
  269.2 4.1 %copy-start.9 = (s32[64]{0:T(128)S(1)}, s32[64]{0:T(128)}, u32[]{:S(2)}) copy-start(s32[64]{0:T(128)} %param.13) | copy-start | bytes 772
  273.3 2.9 copy-start.5
  277.4 44.5 %all-to-all-start = ((bf16[8,256,160]{1,2,0:T(8,128)(2,1)}), bf16[8,256,160]{1,2,0:T(8,128)(2,1)}, u32[]{:S(2)}, u32[]{:S(2)}) async-start(bf16[8,256,160]{1,2,0:T(8,128)(2,1)} %bitcast.54), calls=%async_computation | async-start | bytes 1310720 | tf_op jit(solution)/shard_map/all_to_all | solution.py:156
  293.7 5.5 %copy-start.2 = (bf16[8,491520]{1,0:T(8,128)(2,1)S(1)}, bf16[8,491520]{1,0:T(8,128)(2,1)}, u32[]{:S(2)}) copy-start(bf16[8,491520]{1,0:T(8,128)(2,1)} %reshape.87) | copy-start | bytes 23592964
  316.5 3.0 copy-start.4
  319.4 2.5 slice-start
  321.9 2.3 copy-start.7
  324.2 4.0 %copy-start.6 = (bf16[1536,768]{1,0:T(8,128)(2,1)S(1)}, bf16[1536,768]{1,0:T(8,128)(2,1)}, u32[]{:S(2)}) copy-start(bf16[1536,768]{1,0:T(8,128)(2,1)} %reshape_reshape.11) | copy-start | bytes 7077892
  328.3 21.7 %copy-start.1 = (bf16[768,64]{0,1:T(8,128)(2,1)S(1)}, bf16[768,64]{0,1:T(8,128)(2,1)}, u32[]{:S(2)}) copy-start(bf16[768,64]{0,1:T(8,128)(2,1)} %param.19) | copy-start | bytes 294916
Sparse Core Ops, SparseCore 0:
  9.7 65.3 all-gather.5
  83.8 49.7 all-gather.7
  135.3 43.1 all-gather.9
  180.7 103.3 all-gather.11

commit v5 on v4

--- a/solution.py
+++ b/solution.py
@@ -97,6 +97,61 @@
     )(q_pad, packed_all)
 
 
+def gather_kernel(axis, n, x_ref, out_ref, send_sem, recv_sem, local_sem):
+    me = lax.axis_index(axis)
+    mesh_id = pl.DeviceIdType.MESH
+    barrier = pltpu.get_barrier_semaphore()
+    for k in range(1, n):
+        pl.semaphore_signal(
+            barrier, inc=1, device_id={axis: lax.rem(me + k, n)}, device_id_type=mesh_id
+        )
+    pl.semaphore_wait(barrier, n - 1)
+    local = pltpu.make_async_copy(x_ref, out_ref.at[me], local_sem)
+    local.start()
+    sends = []
+    for k in range(1, n):
+        copy = pltpu.make_async_remote_copy(
+            src_ref=x_ref,
+            dst_ref=out_ref.at[me],
+            send_sem=send_sem.at[k],
+            recv_sem=recv_sem.at[k],
+            device_id={axis: lax.rem(me + k, n)},
+            device_id_type=mesh_id,
+        )
+        copy.start()
+        sends.append(copy)
+    for k in range(1, n):
+        source = lax.rem(me + n - k, n)
+        arriving = pltpu.make_async_remote_copy(
+            src_ref=x_ref,
+            dst_ref=out_ref.at[source],
+            send_sem=send_sem.at[k],
+            recv_sem=recv_sem.at[k],
+            device_id={axis: source},
+            device_id_type=mesh_id,
+        )
+        arriving.wait_recv()
+    for copy in sends:
+        copy.wait_send()
+    local.wait()
+
+
+def dma_all_gather(x, axis, collective_id):
+    n = lax.axis_size(axis)
+    return pl.pallas_call(
+        functools.partial(gather_kernel, axis, n),
+        in_specs=[pl.BlockSpec(memory_space=pl.ANY)],
+        out_specs=pl.BlockSpec(memory_space=pl.ANY),
+        out_shape=jax.ShapeDtypeStruct((n,) + x.shape, x.dtype),
+        scratch_shapes=[
+            pltpu.SemaphoreType.DMA((n,)),
+            pltpu.SemaphoreType.DMA((n,)),
+            pltpu.SemaphoreType.DMA,
+        ],
+        compiler_params=pltpu.CompilerParams(collective_id=collective_id, has_side_effects=True),
+    )(x)
+
+
 def per_device(
     features,
     edge_dst,
@@ -119,7 +174,7 @@
     heads = w_query.shape[1] // HEAD_DIM
     scale = 1.0 / math.sqrt(HEAD_DIM)
 
-    whole = lax.all_gather(features, "mp", axis=1, tiled=True)
+    whole = dma_all_gather(features, "mp", 0).transpose(1, 0, 2).reshape(rows, width)
     queries = jnp.dot(whole, w_query, preferred_element_type=jnp.float32).astype(jnp.bfloat16)
     keys = jnp.dot(whole, w_key, preferred_element_type=jnp.float32).astype(jnp.bfloat16)
     values = jnp.dot(whole, w_value, preferred_element_type=jnp.float32).astype(jnp.bfloat16)

time: 357 us -> 361 us (1.011)
  waiting for transfers between devices: 104 us -> 37.8 us
  Pallas kernels: 118 us -> 172 us
  local copies, waits for them, and re-layouts: 72.4 us -> 88.1 us
    all_gather x1 -> x0, waiting for transfers between devices: 67.7 us -> none  [per_device(): whole = lax.all_gather(features, 'mp', axis=1, tiled=True)]
    pallas_call x0 -> x1, Pallas kernels: none -> 54 us  [dma_all_gather(): pl.pallas_call(functools.partial(gather_kernel, axis, n), in_specs=[pl.Bl...]
    transpose x0 -> x1, local copies, waits for them, and re-layouts: none -> 4.8 us  [per_device(): dma_all_gather(features, 'mp', 0).transpose(1, 0, 2).reshape(rows, width)]
    unnamed x31 -> x24, local copies, waits for them, and re-layouts: 16.6 us -> 19.8 us
  transfers between devices with their start and end apart: 5 -> 4, of which waited for: 3 -> 1; matrix products, arithmetic and copies ran while one was open for 21% -> 24% of each run, Pallas kernels for 33% -> 33%
where the time goes in v5:
time: 361 us; the launch traced here: 360 us
  Pallas kernels  172 us (48%)
  local copies, waits for them, and re-layouts  88.1 us (24%)
  waiting for transfers between devices  37.8 us (10%)
  matrix products  20.6 us (6%)
  blocking collectives  17 us (5%)
  between operations  13.3 us (4%)
  starting transfers between devices  7.33 us (2%)
  other arithmetic  3.82 us (1%)
    pallas_call x1, Pallas kernels, flash_attention(): pl.pallas_call(functools.partial(flash_kernel, dim), grid=grid, in_specs=...  118 us
    pallas_call x1, Pallas kernels, dma_all_gather(): pl.pallas_call(functools.partial(gather_kernel, axis, n), in_specs=[pl.Bl...  54 us
    all_gather x1, waiting for transfers between devices, per_device(): lax.all_gather(jnp.concatenate([keys, values], axis=1), 'blk', axis=0, ti...  37.3 us
    unnamed x24, local copies, waits for them, and re-layouts  19.8 us
    all_to_all x1, blocking collectives, per_device(): lax.all_to_all(out_parts, 'mp', 0, 0, tiled=False).reshape(rows, cols)  17 us
    all_gather x1, local copies, waits for them, and re-layouts, per_device(): flat_all = lax.all_gather(flat, 'mp', axis=0, tiled=False)  9.58 us
    reshape x2, local copies, waits for them, and re-layouts, per_device(): flat_all[:, offset:offset + size].reshape((n_mp,) + x.shape)  8.11 us
  transfers between devices with their start and end apart: 4, of which 1 were waited for; matrix products, arithmetic and copies ran while one was open for 24% of the time, Pallas kernels for 33%

profile of v5, /device:TPU:0, one launch (start us, length us, event | category | flops | bytes accessed | tf_op | source)
XLA Modules:
  0.0 359.9 jit_solution(14459092247025677868)
XLA Ops:
  6.5 2.0 copy.64.x_ref
  8.6 54.0 %shard_map.118 = bf16[8,2048,96]{2,1,0:T(8,128)(2,1)} custom-call(bf16[2048,96]{1,0:T(8,128)(2,1)} %copy.64.x_ref), custom_call_target="tpu_custom_call" | custom-call | tf_op jit(solution)/shard_map/pallas_call | solution.py:141
  62.6 4.8 %copy.65 = bf16[2048,8,96]{0,2,1:T(8,128)(2,1)S(1)} copy(bf16[2048,8,96]{2,0,1:T(8,128)(2,1)} %bitcast.62) | data formatting | bytes 6291456 | tf_op jit(solution)/shard_map/transpose | solution.py:177
  71.7 2.4 pad_maximum_fusion.1
  76.2 1.9 copy.70
  78.0 2.2 reshape.71
  80.2 1.7 reshape.72
  85.0 1.7 constant_dynamic-update-slice_fusion.3
  89.6 37.3 %all-gather.5.cloned.1.call-done.kv_ref = bf16[32768,128]{1,0:T(8,128)(2,1)} async-done(((bf16[2048,128]{1,0:T(8,128)(2,1)}), bf16[32768,128]{1,0:T(8,128)(2,1)}) %all-gather.5.cloned.1.call-update) | async-done | bytes 8388624 | tf_op jit(solution)/shard_map/all_gather | solution.py:182
  131.0 2.0 copy.80
  135.0 117.8 %shard_map.119 = bf16[2048,64]{1,0:T(8,128)(2,1)} custom-call(bf16[2048,128]{1,0:T(8,128)(2,1)} %concatenate.14.q_ref, bf16[32768,128]{1,0:T(8,128)(2,1)} %all-gather.5.cloned.1.call-done.kv_ref), custom_call_target="tpu_custom_call" | custom-call | flops 34359738368 | bytes 34340864 | tf_op jit(solution)/shard_map/pallas_call | solution.py:75
  254.1 6.5 %copy_bitcast_fusion = bf16[256,128,96]{1,2,0:T(8,128)(2,1)} fusion(bf16[32768,96]{0,1:T(8,128)(2,1)} %all-gather.7.cloned.1.call-done), kind=kLoop, calls=%fused_computation.1 | loop fusion | bytes 12582912 | tf_op jit(solution)/shard_map/reshape | solution.py:21
  260.6 3.6 %gather_fusion = bf16[64,128,96]{1,2,0:T(8,128)(2,1)S(1)} fusion(bf16[256,128,96]{1,2,0:T(8,128)(2,1)} %copy_bitcast_fusion, s32[1024]{0:T(1024)S(1)} %pad_clamp_fusion), kind=kCustom, calls=%fused_computation | custom fusion | bytes 3145984 | tf_op jit(solution)/shard_map/jit(_take)/gather | solution.py:22
  264.3 3.8 %fusion.5 = f32[64,128,96]{1,2,0:T(8,128)S(1)} fusion(s32[64,128,128]{2,1,0:T(8,128)} %param.15, bf16[64,128,96]{1,2,0:T(8,128)(2,1)S(1)} %gather_fusion, pred[64]{0:T(512)(128)(4,1)S(1)} %get-tuple-element.13), kind=kOutput, calls=%fused_computation.11 | convolution fusion | flops 203161600 | bytes 8912960 | tf_op jit(solution)/shard_map/ers,esf->erf/dot_general | solution.py:23
  268.1 2.9 fusion.11
  272.3 7.1 %all-to-all-start = ((bf16[8,256,160]{1,2,0:T(8,128)(2,1)}), bf16[8,256,160]{1,2,0:T(8,128)(2,1)}, u32[]{:S(2)}, u32[]{:S(2)}) async-start(bf16[8,256,160]{1,2,0:T(8,128)(2,1)} %bitcast.56), calls=%async_computation | async-start | bytes 1310720 | tf_op jit(solution)/shard_map/all_to_all | solution.py:211
  279.4 9.6 %reshape.91 = bf16[8,491520]{1,0:T(8,128)(2,1)} reshape(bf16[3932160]{0:T(1024)(128)(2,1)} %all-gather.9.cloned.1.call-done) | data formatting | bytes 15728640 | tf_op jit(solution)/shard_map/all_gather | solution.py:187
  289.0 3.6 %fusion.37 = (bf16[8,147456]{1,0:T(8,128)(2,1)S(1)}, bf16[8,147456]{1,0:T(8,128)(2,1)}) fusion(bf16[8,491520]{1,0:T(8,128)(2,1)} %reshape.91), kind=kLoop, calls=%fused_computation.58 | loop fusion | bytes 9437184 | tf_op jit(solution)/shard_map/slice | solution.py:192
  292.6 1.9 copy-done.2
  296.0 2.9 reshape.96
  298.9 3.7 %reshape.77 = bf16[8,768,96]{2,1,0:T(8,128)(2,1)} reshape(bf16[589824]{0:T(1024)(128)(2,1)} %reshape.96) | data formatting | bytes 2359296 | tf_op jit(solution)/shard_map/reshape | solution.py:192
  302.6 3.6 %copy.76 = bf16[768,8,96]{2,1,0:T(8,128)(2,1)} copy(bf16[768,8,96]{2,0,1:T(8,128)(2,1)} %bitcast.64) | data formatting | bytes 2359296 | tf_op jit(solution)/shard_map/transpose | solution.py:198
  306.2 3.8 %reshape_reshape.9 = bf16[8,96,768]{2,1,0:T(8,128)(2,1)} reshape(bf16[768,8,96]{2,1,0:T(8,128)(2,1)} %copy.76) | data formatting | bytes 2359296 | tf_op jit(solution)/shard_map/reshape;reshape | solution.py:200
  310.0 2.8 reshape_reshape.10
  312.9 2.5 reshape.98
  315.3 4.4 %reshape.79 = bf16[8,768,192]{2,1,0:T(8,128)(2,1)S(1)} reshape(bf16[1179648]{0:T(1024)(128)(2,1)} %reshape.98) | data formatting | bytes 4718592 | tf_op jit(solution)/shard_map/reshape | solution.py:192
  319.8 2.6 copy.77
  322.4 2.8 reshape_reshape.11
  325.3 2.3 convolution_bitcast_fusion
  327.6 4.0 %fusion.36 = (f32[256]{0:T(256)S(1)}, f32[256]{0:T(256)S(1)}, f32[256,768]{1,0:T(8,128)}) fusion(f32[256,768]{1,0:T(8,128)} %convolution_bitcast_fusion, bf16[768,768]{1,0:T(8,128)(2,1)} %reshape_reshape.10, bf16[8,96,768]{2,1,0:T(8,128)(2,1)} %reshape_reshape.9, bf16[8,256,160]{1,2,0:T(8,128)(2,1)} %all-to-all-done, bf16[256,768]{1,0:T(8,128)(2,1)} %copy.80), kind=kOutput, calls=%fused_computation.57 | convolution fusion | flops 605552128 | bytes 4720640 | tf_op jit(solution)/shard_map/dot_general | solution.py:219
  331.6 3.7 %fusion.15 = bf16[256,768]{1,0:T(8,128)(2,1)S(1)} fusion(f32[256,768]{1,0:T(8,128)} %get-tuple-element.21, bf16[1536,768]{1,0:T(8,128)(2,1)S(1)} %reshape_reshape.11, bf16[768,1536]{0,1:T(8,128)(2,1)} %bitcast.67, f32[256]{0:T(256)S(1)} %get-tuple-element.20, f32[256]{0:T(256)S(1)} %get-tuple-element.19), kind=kOutput, calls=%fused_computation.21 | convolution fusion | flops 1209729024 | bytes 5900288 | tf_op jit(solution)/shard_map/dot_general | solution.py:231
  335.5 17.0 %all_to_all.10 = bf16[8,256,96]{1,2,0:T(8,128)(2,1)S(1)} all-to-all(bf16[8,256,96]{1,2,0:T(8,128)(2,1)S(1)} %bitcast.68), channel_id=1, replica_groups=mesh['blk'=16,'mp'=8] {'mp'}, dimensions={0} | all-to-all | bytes 786432 | tf_op jit(solution)/shard_map/all_to_all | solution.py:234
  (51 shorter events, 23.4 us)
Async XLA Ops:
  6.5 60.9 %copy-start = (bf16[768,64]{0,1:T(8,128)(2,1)S(1)}, bf16[768,64]{0,1:T(8,128)(2,1)}, u32[]{:S(2)}) copy-start(bf16[768,64]{0,1:T(8,128)(2,1)} %param.19) | copy-start | bytes 294916
  6.5 120.4 %all-gather.5.cloned.1.call-start = ((), (), s32[]{:S(2)}) async-start(), calls=%async_computation.2 | async-start | bytes 8912896 | tf_op jit(solution)/shard_map/all_gather | solution.py:182
  71.7 10.3 %copy-start.4 = (bf16[64,768]{1,0:T(8,128)(2,1)S(1)}, bf16[64,768]{1,0:T(8,128)(2,1)}, u32[]{:S(2)}) copy-start(bf16[64,768]{1,0:T(8,128)(2,1)} %param.21) | copy-start | bytes 294916
  74.1 180.0 %all-gather.7.cloned.1.call-start = ((), (), s32[]{:S(2)}) async-start(), calls=%async_computation.3 | async-start | bytes 6684672 | tf_op jit(solution)/shard_map/all_gather | solution.py:186
  126.9 152.5 %all-gather.9.cloned.1.call-start = ((), (), s32[]{:S(2)}) async-start(), calls=%async_computation.4 | async-start | bytes 8847360 | tf_op jit(solution)/shard_map/all_gather | solution.py:187
  129.2 5.8 %copy-start.6 = (s32[64]{0:T(128)S(1)}, s32[64]{0:T(128)}, u32[]{:S(2)}) copy-start(s32[64]{0:T(128)} %param.14) | copy-start | bytes 772
  264.3 3.8 %copy-start.5 = (s32[64]{0:T(128)S(1)}, s32[64]{0:T(128)}, u32[]{:S(2)}) copy-start(s32[64]{0:T(128)} %param.13) | copy-start | bytes 772
  268.1 2.9 copy-start.3
  272.3 52.9 %all-to-all-start = ((bf16[8,256,160]{1,2,0:T(8,128)(2,1)}), bf16[8,256,160]{1,2,0:T(8,128)(2,1)}, u32[]{:S(2)}, u32[]{:S(2)}) async-start(bf16[8,256,160]{1,2,0:T(8,128)(2,1)} %bitcast.56), calls=%async_computation | async-start | bytes 1310720 | tf_op jit(solution)/shard_map/all_to_all | solution.py:211
  289.0 5.5 %copy-start.2 = (bf16[8,491520]{1,0:T(8,128)(2,1)S(1)}, bf16[8,491520]{1,0:T(8,128)(2,1)}, u32[]{:S(2)}) copy-start(bf16[8,491520]{1,0:T(8,128)(2,1)} %reshape.91) | copy-start | bytes 23592964
  322.4 2.8 slice-start
  331.6 21.7 %copy-start.1 = (bf16[768,64]{0,1:T(8,128)(2,1)S(1)}, bf16[768,64]{0,1:T(8,128)(2,1)}, u32[]{:S(2)}) copy-start(bf16[768,64]{0,1:T(8,128)(2,1)} %param.19) | copy-start | bytes 294916
Sparse Core Ops, SparseCore 0:
  74.2 52.6 all-gather.4
  128.5 43.1 all-gather.6
  174.1 103.4 all-gather.8

commit v6 on v5

--- a/solution.py
+++ b/solution.py
@@ -174,49 +174,60 @@
     heads = w_query.shape[1] // HEAD_DIM
     scale = 1.0 / math.sqrt(HEAD_DIM)
 
-    whole = dma_all_gather(features, "mp", 0).transpose(1, 0, 2).reshape(rows, width)
-    queries = jnp.dot(whole, w_query, preferred_element_type=jnp.float32).astype(jnp.bfloat16)
-    keys = jnp.dot(whole, w_key, preferred_element_type=jnp.float32).astype(jnp.bfloat16)
-    values = jnp.dot(whole, w_value, preferred_element_type=jnp.float32).astype(jnp.bfloat16)
-    queries = queries * jnp.bfloat16(scale)
-    kv_all = lax.all_gather(jnp.concatenate([keys, values], axis=1), "blk", axis=0, tiled=True)
-    pieces = (gin_in, ffn_in, gin_out, w_attn_out, ffn_out)
-    flat = jnp.concatenate([x.reshape(-1) for x in pieces])
-    kv_all, late_features, flat = lax.optimization_barrier((kv_all, features, flat))
-    all_features = lax.all_gather(late_features, "blk", axis=0, tiled=True)
-    flat_all = lax.all_gather(flat, "mp", axis=0, tiled=False)
+    all_features = lax.all_gather(features, "blk", axis=0, tiled=True)
+    feature_parts = dma_all_gather(features, "mp", 0)
+
+    def project(w):
+        return jnp.einsum(
+            "jrc,jcd->rd",
+            feature_parts,
+            w.reshape(n_mp, cols, w.shape[1]),
+            preferred_element_type=jnp.float32,
+        ).astype(jnp.bfloat16)
+
+    queries = project(w_query) * jnp.bfloat16(scale)
+    keys = project(w_key)
+    values = project(w_value)
+    kv_packed = jnp.concatenate([keys, values], axis=1)
+    kv_packed, all_features = lax.optimization_barrier((kv_packed, all_features))
+    kv_all = lax.all_gather(kv_packed, "blk", axis=0, tiled=True)
+
+    gathered = neighbour_sum(features, edge_dst, edge_src, edge_mask, all_features)
+    local_share = (features.astype(jnp.float32) + gathered * 0.25).astype(jnp.bfloat16)
+
+    pieces = (gin_in.T, ffn_in.T, gin_out, w_attn_out, ffn_out)
+    packed_weights = jnp.concatenate(pieces, axis=0)
+    kv_all, packed_weights = lax.optimization_barrier((kv_all, packed_weights))
+    weight_parts = lax.all_gather(packed_weights, "mp", axis=0, tiled=False)
     unpacked = []
     offset = 0
     for x in pieces:
-        size = x.size
-        unpacked.append(flat_all[:, offset : offset + size].reshape((n_mp,) + x.shape))
-        offset += size
-    gin_in_parts, ffn_in_parts, gin_out_parts, attn_out_parts, ffn_out_parts = unpacked
-
-    def join_columns(parts):
-        count, r, c = parts.shape
-        return parts.transpose(1, 0, 2).reshape(r, count * c)
-
-    gin_in_full = join_columns(gin_in_parts).reshape(n_mp, cols, width)
-    ffn_in_full = join_columns(ffn_in_parts)
-    gin_out_full = gin_out_parts.reshape(width, width)
-    ffn_out_full = ffn_out_parts.reshape(-1, width)
-
-    gathered = neighbour_sum(features, edge_dst, edge_src, edge_mask, all_features)
-    local_share = (features.astype(jnp.float32) + gathered * 0.25).astype(jnp.bfloat16)
+        unpacked.append(weight_parts[:, offset : offset + x.shape[0], :])
+        offset += x.shape[0]
+    gin_in_t, ffn_in_t, gin_out_parts, attn_out_parts, ffn_out_parts = unpacked
 
     attended = flash_attention(queries, kv_all, 0, heads)
 
     mixed_in = jnp.concatenate([local_share, attended], axis=1).reshape(n_mp, share, -1)
     received = lax.all_to_all(mixed_in, "mp", 0, 0, tiled=False)
-    own_rows = lax.dynamic_slice_in_dim(whole, me * share, share, 0).astype(jnp.float32)
+    own_rows = (
+        lax.dynamic_slice_in_dim(feature_parts, me * share, share, 1)
+        .transpose(1, 0, 2)
+        .reshape(share, width)
+        .astype(jnp.float32)
+    )
 
     local_hidden = jax.nn.relu(
-        jnp.einsum("jrc,jcd->rd", received[:, :, :cols], gin_in_full, preferred_element_type=jnp.float32)
+        jnp.einsum(
+            "jrc,pqjc->rpq",
+            received[:, :, :cols],
+            gin_in_t.reshape(n_mp, cols, n_mp, cols),
+            preferred_element_type=jnp.float32,
+        )
     ).astype(jnp.bfloat16)
     mixed = (
         own_rows
-        + jnp.dot(local_hidden, gin_out_full, preferred_element_type=jnp.float32)
+        + jnp.einsum("rjc,jce->re", local_hidden, gin_out_parts, preferred_element_type=jnp.float32)
         + jnp.einsum("jrd,jde->re", received[:, :, cols:], attn_out_parts, preferred_element_type=jnp.float32)
     )
     row_average = jnp.sum(mixed, axis=1, keepdims=True) / width
@@ -225,10 +236,11 @@
         (mixed - row_average) * lax.rsqrt(square_row - row_average * row_average + 1e-05)
     ).astype(jnp.bfloat16)
     ffn_hidden = jax.nn.relu(
-        jnp.dot(normed, ffn_in_full, preferred_element_type=jnp.float32)
+        jnp.einsum("rk,jck->rjc", normed, ffn_in_t, preferred_element_type=jnp.float32)
     ).astype(jnp.bfloat16)
     out_rows = (
-        mixed + jnp.dot(ffn_hidden, ffn_out_full, preferred_element_type=jnp.float32)
+        mixed
+        + jnp.einsum("rjc,jce->re", ffn_hidden, ffn_out_parts, preferred_element_type=jnp.float32)
     ).astype(jnp.bfloat16)
     out_parts = out_rows.reshape(share, n_mp, cols).transpose(1, 0, 2)
     return lax.all_to_all(out_parts, "mp", 0, 0, tiled=False).reshape(rows, cols)

time: 361 us -> 351 us (0.972)
  local copies, waits for them, and re-layouts: 88.1 us -> 23.7 us
  Pallas kernels: 172 us -> 201 us
  waiting for transfers between devices: 37.8 us -> 62 us
  matrix products: 20.6 us -> 28.2 us
  blocking collectives: 17 us -> 13 us
    pallas_call x1, Pallas kernels: 54 us -> 82.7 us  [dma_all_gather(): pl.pallas_call(functools.partial(gather_kernel, axis, n), in_specs=[pl.Bl...]
    unnamed x24 -> x25, local copies, waits for them, and re-layouts: 19.8 us -> 2.14 us
    all_gather x3, waiting for transfers between devices: 37.3 us -> 52.6 us  [the longest x1 52.6 us: per_device(): kv_all = lax.all_gather(kv_packed, 'blk', axis=0, tiled=True)]
    transpose x3 -> x0, local copies, waits for them, and re-layouts: 11.1 us -> none  [the longest x2 6.28 us: join_columns(): return parts.transpose(1, 0, 2).reshape(r, count * c)]
    reshape x7 -> x4, local copies, waits for them, and re-layouts: 14.3 us -> 3.98 us  [the longest x3 2.25 us: project(): w.reshape(n_mp, cols, w.shape[1])]
    all_gather x1 -> x0, local copies, waits for them, and re-layouts: 9.58 us -> none  [per_device(): flat_all = lax.all_gather(flat, 'mp', axis=0, tiled=False)]
    another operation x3 -> x0, local copies, waits for them, and re-layouts: 9.45 us -> none  [the longest x1 3.81 us: per_device(): gin_in_full = join_columns(gin_in_parts).reshape(n_mp, cols, width)]
    all_to_all x1, waiting for transfers between devices: 0.01 us -> 8.68 us  [per_device(): received = lax.all_to_all(mixed_in, 'mp', 0, 0, tiled=False)]
  transfers between devices with their start and end apart: 4 -> 4, of which waited for: 1 -> 2; matrix products, arithmetic and copies ran while one was open for 24% -> 12% of each run, Pallas kernels for 33% -> 57%
where the time goes in v6:
time: 351 us
  Pallas kernels  201 us (57%)
  waiting for transfers between devices  62 us (18%)
  matrix products  28.2 us (8%)
  local copies, waits for them, and re-layouts  23.7 us (7%)
  between operations  13.5 us (4%)
  blocking collectives  13 us (4%)
  starting transfers between devices  7.04 us (2%)
    pallas_call x1, Pallas kernels, flash_attention(): pl.pallas_call(functools.partial(flash_kernel, dim), grid=grid, in_specs=...  118 us
    pallas_call x1, Pallas kernels, dma_all_gather(): pl.pallas_call(functools.partial(gather_kernel, axis, n), in_specs=[pl.Bl...  82.7 us
    all_gather x1, waiting for transfers between devices, per_device(): kv_all = lax.all_gather(kv_packed, 'blk', axis=0, tiled=True)  52.6 us
    all_to_all x1, blocking collectives, per_device(): lax.all_to_all(out_parts, 'mp', 0, 0, tiled=False).reshape(rows, cols)  13 us
    dot_general x3, matrix products, project(): jnp.einsum('jrc,jcd->rd', feature_parts, w.reshape(n_mp, cols, w.shape[1]...  10.7 us
    all_to_all x1, waiting for transfers between devices, per_device(): received = lax.all_to_all(mixed_in, 'mp', 0, 0, tiled=False)  8.68 us
  transfers between devices with their start and end apart: 4, of which 2 were waited for; matrix products, arithmetic and copies ran while one was open for 12% of the time, Pallas kernels for 57%

profile of v6, /device:TPU:0, one launch (start us, length us, event | category | flops | bytes accessed | tf_op | source)
XLA Modules:
  0.0 350.5 jit_solution(4101934096971205571)
XLA Ops:
  6.5 0.7 all-gather.5.cloned.1.call-update
  7.3 2.0 copy.77.x_ref
  9.3 1.0 reshape.54
  10.4 1.1 reshape.55
  11.4 82.7 %shard_map.118 = bf16[8,2048,96]{2,1,0:T(8,128)(2,1)} custom-call(bf16[2048,96]{1,0:T(8,128)(2,1)} %copy.77.x_ref), custom_call_target="tpu_custom_call" | custom-call | tf_op jit(solution)/shard_map/pallas_call | solution.py:141
  94.2 3.6 %fusion.6 = bf16[2048,64]{0,1:T(8,128)(2,1)S(1)} fusion(bf16[8,2048,96]{2,1,0:T(8,128)(2,1)} %shard_map.118, bf16[8,96,64]{1,0,2:T(8,128)(2,1)S(1)} %reshape.54), kind=kOutput, calls=%fused_computation.11 | convolution fusion | flops 201457664 | bytes 3506176 | tf_op jit(solution)/shard_map/jrc,jcd->rd/dot_general | solution.py:181
  97.7 0.3 copy.83
  98.0 3.6 %fusion.7 = bf16[2048,64]{0,1:T(8,128)(2,1)S(1)} fusion(bf16[8,2048,96]{2,1,0:T(8,128)(2,1)} %shard_map.118, bf16[8,96,64]{1,0,2:T(8,128)(2,1)S(1)} %reshape.55), kind=kOutput, calls=%fused_computation.12 | convolution fusion | flops 201457664 | bytes 3506176 | tf_op jit(solution)/shard_map/jrc,jcd->rd/dot_general | solution.py:181
  102.0 1.1 pad_maximum_fusion.1
  103.5 52.6 %all-gather.7.cloned.1.call-done.kv_ref = bf16[32768,128]{1,0:T(8,128)(2,1)} async-done(((bf16[2048,128]{1,0:T(8,128)(2,1)}), bf16[32768,128]{1,0:T(8,128)(2,1)}) %all-gather.7.cloned.1.call-update) | async-done | bytes 8388624 | tf_op jit(solution)/shard_map/all_gather | solution.py:193
  156.3 3.6 %fusion.8 = bf16[2048,64]{0,1:T(8,128)(2,1)S(1)} fusion(bf16[8,2048,96]{2,1,0:T(8,128)(2,1)} %shard_map.118, bf16[8,96,64]{1,0,2:T(8,128)(2,1)S(1)} %reshape.57), kind=kOutput, calls=%fused_computation.13 | convolution fusion | flops 201457664 | bytes 3506176 | tf_op jit(solution)/shard_map/jrc,jcd->rd/dot_general | solution.py:181
  159.9 0.3 copy.89
  160.2 0.9 concatenate.13.q_ref
  161.2 6.5 %copy_bitcast_fusion = bf16[256,128,96]{1,2,0:T(8,128)(2,1)} fusion(bf16[32768,96]{0,1:T(8,128)(2,1)} %all-gather.5.cloned.1.call-done), kind=kLoop, calls=%fused_computation.1 | loop fusion | bytes 12582912 | tf_op jit(solution)/shard_map/reshape | solution.py:21
  167.7 4.3 %gather_fusion = bf16[64,128,96]{1,2,0:T(8,128)(2,1)S(1)} fusion(bf16[256,128,96]{1,2,0:T(8,128)(2,1)} %copy_bitcast_fusion, s32[1024]{0:T(1024)S(1)} %pad_clamp_fusion), kind=kCustom, calls=%fused_computation | custom fusion | bytes 3145984 | tf_op jit(solution)/shard_map/jit(_take)/gather | solution.py:22
  172.0 3.8 %fusion.11 = f32[64,128,96]{1,2,0:T(8,128)S(1)} fusion(s32[64,128,128]{2,1,0:T(8,128)} %param.15, bf16[64,128,96]{1,2,0:T(8,128)(2,1)S(1)} %gather_fusion, pred[64]{0:T(512)(128)(4,1)S(1)} %get-tuple-element.15), kind=kOutput, calls=%fused_computation.16 | convolution fusion | flops 203161600 | bytes 8912960 | tf_op jit(solution)/shard_map/ers,esf->erf/dot_general | solution.py:23
  175.8 2.9 fusion.26
  178.7 0.3 fusion.48
  179.1 117.8 %shard_map.119 = bf16[2048,64]{1,0:T(8,128)(2,1)} custom-call(bf16[2048,128]{1,0:T(8,128)(2,1)} %concatenate.13.q_ref, bf16[32768,128]{1,0:T(8,128)(2,1)} %all-gather.7.cloned.1.call-done.kv_ref), custom_call_target="tpu_custom_call" | custom-call | flops 34359738368 | bytes 34340864 | tf_op jit(solution)/shard_map/pallas_call | solution.py:75
  296.8 1.2 copy.90
  298.1 0.9 copy.129
  299.0 6.8 %all-to-all-start = ((bf16[8,256,160]{1,2,0:T(8,128)(2,1)}), bf16[8,256,160]{1,2,0:T(8,128)(2,1)}, u32[]{:S(2)}, u32[]{:S(2)}) async-start(bf16[8,256,160]{1,2,0:T(8,128)(2,1)} %bitcast.89), calls=%async_computation | async-start | bytes 1310720 | tf_op jit(solution)/shard_map/all_to_all | solution.py:212
  305.8 1.1 convert_bitcast_fusion
  306.9 0.3 copy.78
  307.5 1.4 slice.31
  308.9 1.7 reshape.59
  310.6 8.7 %all-to-all-done = bf16[8,256,160]{1,2,0:T(8,128)(2,1)} async-done(((bf16[8,256,160]{1,2,0:T(8,128)(2,1)}), bf16[8,256,160]{1,2,0:T(8,128)(2,1)}, u32[]{:S(2)}, u32[]{:S(2)}) %all-to-all-start) | async-done | bytes 655392 | tf_op jit(solution)/shard_map/all_to_all | solution.py:212
  319.3 1.6 convolution_bitcast_fusion.3
  320.9 3.8 %fusion.70 = (f32[256]{0:T(256)S(1)}, f32[256]{0:T(256)S(1)}, f32[256,768]{1,0:T(8,128)}) fusion(f32[256,768]{1,0:T(8,128)S(1)} %convolution_bitcast_fusion.3, f32[256,768]{1,0:T(8,128)S(1)} %copy.93, bf16[8,640,768]{2,1,0:T(8,128)(2,1)} %bitcast.97, bf16[8,96,8,96]{3,2,1,0:T(8,128)(2,1)S(1)} %reshape.59, bf16[8,256,160]{1,2,0:T(8,128)(2,1)} %all-to-all-done), kind=kOutput, calls=%fused_computation.71 | convolution fusion | flops 605355520 | bytes 5113856 | tf_op jit(solution)/shard_map/rjc,jce->re/dot_general | solution.py:230
  324.7 5.3 %fusion.37 = bf16[256,768]{1,0:T(8,128)(2,1)S(1)} fusion(f32[256,768]{1,0:T(8,128)} %get-tuple-element.19, bf16[8,640,768]{2,1,0:T(8,128)(2,1)} %bitcast.98, f32[256]{0:T(256)S(1)} %get-tuple-element.18, f32[256]{0:T(256)S(1)} %get-tuple-element.17), kind=kOutput, calls=%fused_computation.31 | convolution fusion | flops 1209729024 | bytes 6686720 | tf_op jit(solution)/shard_map/rjc,jce->re/dot_general | solution.py:243
  330.2 13.0 %all_to_all.10 = bf16[8,256,96]{1,2,0:T(8,128)(2,1)S(1)} all-to-all(bf16[8,256,96]{1,2,0:T(8,128)(2,1)S(1)} %bitcast.93), channel_id=1, replica_groups=mesh['blk'=16,'mp'=8] {'mp'}, dimensions={0} | all-to-all | bytes 786432 | tf_op jit(solution)/shard_map/all_to_all | solution.py:246
  343.2 0.8 copy.102
  (41 shorter events, 1.4 us)
Async XLA Ops:
  6.5 96.6 %all-gather.5.cloned.1.call-start = ((), (), s32[]{:S(2)}) async-start(), calls=%async_computation.2 | async-start | bytes 6684672 | tf_op jit(solution)/shard_map/all_gather | solution.py:177
  7.3 148.8 %all-gather.7.cloned.1.call-start = ((), (), s32[]{:S(2)}) async-start(), calls=%async_computation.3 | async-start | bytes 8912896 | tf_op jit(solution)/shard_map/all_gather | solution.py:193
  98.0 5.3 %copy-start.4 = (bf16[768,96]{0,1:T(8,128)(2,1)S(1)}, bf16[768,96]{0,1:T(8,128)(2,1)}, u32[]{:S(2)}) copy-start(bf16[768,96]{0,1:T(8,128)(2,1)} %param.16) | copy-start | bytes 442372
  101.6 1.7 copy-start.2
  101.7 1.8 copy-start.5
  101.7 1.8 copy-start.7
  101.7 1.8 copy-start.3
  101.7 54.4 %copy-start.6 = (bf16[768,64]{0,1:T(8,128)(2,1)S(1)}, bf16[768,64]{0,1:T(8,128)(2,1)}, u32[]{:S(2)}) copy-start(bf16[768,64]{0,1:T(8,128)(2,1)} %param.18) | copy-start | bytes 294916
  103.1 204.4 %all-gather.9.cloned.1.call-start = ((), (), s32[]{:S(2)}) async-start(), calls=%async_computation.4 | async-start | bytes 8847360 | tf_op jit(solution)/shard_map/all_gather | solution.py:201
  103.5 52.6 %copy-start.1 = (bf16[640,768]{1,0:T(8,128)(2,1)}, bf16[640,768]{1,0:T(8,128)(2,1)S(1)}, u32[]{:S(2)}) copy-start(bf16[640,768]{1,0:T(8,128)(2,1)S(1)} %constant_dynamic-update-slice_fusion) | copy-start | bytes 2949124
  156.3 4.9 %copy-start.9 = (s32[64]{0:T(128)S(1)}, s32[64]{0:T(128)}, u32[]{:S(2)}) copy-start(s32[64]{0:T(128)} %param.14) | copy-start | bytes 772
  172.0 3.8 %copy-start.8 = (s32[64]{0:T(128)S(1)}, s32[64]{0:T(128)}, u32[]{:S(2)}) copy-start(s32[64]{0:T(128)} %param.13) | copy-start | bytes 772
  175.8 2.9 copy-start
  299.0 20.3 %all-to-all-start = ((bf16[8,256,160]{1,2,0:T(8,128)(2,1)}), bf16[8,256,160]{1,2,0:T(8,128)(2,1)}, u32[]{:S(2)}, u32[]{:S(2)}) async-start(bf16[8,256,160]{1,2,0:T(8,128)(2,1)} %bitcast.89), calls=%async_computation | async-start | bytes 1310720 | tf_op jit(solution)/shard_map/all_to_all | solution.py:212
Sparse Core Ops, SparseCore 0:
  9.0 74.2 all-gather.4
  103.2 52.8 all-gather.6
  158.4 103.4 all-gather.8

commit v7 on v6

--- a/solution.py
+++ b/solution.py
@@ -174,7 +174,6 @@
     heads = w_query.shape[1] // HEAD_DIM
     scale = 1.0 / math.sqrt(HEAD_DIM)
 
-    all_features = lax.all_gather(features, "blk", axis=0, tiled=True)
     feature_parts = dma_all_gather(features, "mp", 0)
 
     def project(w):
@@ -188,16 +187,12 @@
     queries = project(w_query) * jnp.bfloat16(scale)
     keys = project(w_key)
     values = project(w_value)
-    kv_packed = jnp.concatenate([keys, values], axis=1)
-    kv_packed, all_features = lax.optimization_barrier((kv_packed, all_features))
-    kv_all = lax.all_gather(kv_packed, "blk", axis=0, tiled=True)
-
-    gathered = neighbour_sum(features, edge_dst, edge_src, edge_mask, all_features)
-    local_share = (features.astype(jnp.float32) + gathered * 0.25).astype(jnp.bfloat16)
+    kv_all = lax.all_gather(jnp.concatenate([keys, values], axis=1), "blk", axis=0, tiled=True)
 
     pieces = (gin_in.T, ffn_in.T, gin_out, w_attn_out, ffn_out)
     packed_weights = jnp.concatenate(pieces, axis=0)
-    kv_all, packed_weights = lax.optimization_barrier((kv_all, packed_weights))
+    kv_all, packed_weights, late_features = lax.optimization_barrier((kv_all, packed_weights, features))
+    all_features = lax.all_gather(late_features, "blk", axis=0, tiled=True)
     weight_parts = lax.all_gather(packed_weights, "mp", axis=0, tiled=False)
     unpacked = []
     offset = 0
@@ -207,6 +202,9 @@
     gin_in_t, ffn_in_t, gin_out_parts, attn_out_parts, ffn_out_parts = unpacked
 
     attended = flash_attention(queries, kv_all, 0, heads)
+
+    gathered = neighbour_sum(features, edge_dst, edge_src, edge_mask, all_features)
+    local_share = (features.astype(jnp.float32) + gathered * 0.25).astype(jnp.bfloat16)
 
     mixed_in = jnp.concatenate([local_share, attended], axis=1).reshape(n_mp, share, -1)
     received = lax.all_to_all(mixed_in, "mp", 0, 0, tiled=False)

time: 351 us -> 320 us (0.912)
  Pallas kernels: 201 us -> 172 us
    pallas_call x1, Pallas kernels: 82.7 us -> 54 us  [dma_all_gather(): pl.pallas_call(functools.partial(gather_kernel, axis, n), in_specs=[pl.Bl...]
  transfers between devices with their start and end apart: 4 -> 4, of which waited for: 2 -> 2; matrix products, arithmetic and copies ran while one was open for 12% -> 9% of each run, Pallas kernels for 57% -> 37%
where the time goes in v7:
time: 320 us; the launch traced here: 319 us
  Pallas kernels  172 us (54%)
  waiting for transfers between devices  61.8 us (19%)
  matrix products  28.3 us (9%)
  local copies, waits for them, and re-layouts  21.3 us (7%)
  between operations  13.5 us (4%)
  blocking collectives  13 us (4%)
  starting transfers between devices  6.89 us (2%)
    pallas_call x1, Pallas kernels, flash_attention(): pl.pallas_call(functools.partial(flash_kernel, dim), grid=grid, in_specs=...  118 us
    pallas_call x1, Pallas kernels, dma_all_gather(): pl.pallas_call(functools.partial(gather_kernel, axis, n), in_specs=[pl.Bl...  54 us
    all_gather x1, waiting for transfers between devices, per_device(): lax.all_gather(jnp.concatenate([keys, values], axis=1), 'blk', axis=0, ti...  52.6 us
    all_to_all x1, blocking collectives, per_device(): lax.all_to_all(out_parts, 'mp', 0, 0, tiled=False).reshape(rows, cols)  13 us
    dot_general x3, matrix products, project(): jnp.einsum('jrc,jcd->rd', feature_parts, w.reshape(n_mp, cols, w.shape[1]...  10.8 us
    all_to_all x1, waiting for transfers between devices, per_device(): received = lax.all_to_all(mixed_in, 'mp', 0, 0, tiled=False)  8.66 us
    all_to_all x1, starting transfers between devices, per_device(): received = lax.all_to_all(mixed_in, 'mp', 0, 0, tiled=False)  6.62 us
    reshape x1, local copies, waits for them, and re-layouts, neighbour_sum(): blocks = all_features.reshape(count, BLOCK, cols)  6.6 us
  transfers between devices with their start and end apart: 4, of which 2 were waited for; matrix products, arithmetic and copies ran while one was open for 9% of the time, Pallas kernels for 37%

profile of v7, /device:TPU:0, one launch (start us, length us, event | category | flops | bytes accessed | tf_op | source)
XLA Modules:
  0.0 319.3 jit_solution(1396303020076345706)
XLA Ops:
  6.5 2.0 copy.77.x_ref
  8.6 54.0 %shard_map.118 = bf16[8,2048,96]{2,1,0:T(8,128)(2,1)} custom-call(bf16[2048,96]{1,0:T(8,128)(2,1)} %copy.77.x_ref), custom_call_target="tpu_custom_call" | custom-call | tf_op jit(solution)/shard_map/pallas_call | solution.py:141
  62.8 3.6 %fusion.6 = bf16[2048,64]{0,1:T(8,128)(2,1)S(1)} fusion(bf16[8,2048,96]{2,1,0:T(8,128)(2,1)} %shard_map.118, bf16[8,96,64]{1,0,2:T(8,128)(2,1)S(1)} %reshape.54), kind=kOutput, calls=%fused_computation.11 | convolution fusion | flops 201457664 | bytes 3506176 | tf_op jit(solution)/shard_map/jrc,jcd->rd/dot_general | solution.py:180
  66.4 0.3 copy.83
  66.9 3.6 %fusion.7 = bf16[2048,64]{0,1:T(8,128)(2,1)S(1)} fusion(bf16[8,2048,96]{2,1,0:T(8,128)(2,1)} %shard_map.118, bf16[8,96,64]{1,0,2:T(8,128)(2,1)S(1)} %reshape.55), kind=kOutput, calls=%fused_computation.12 | convolution fusion | flops 201457664 | bytes 3506176 | tf_op jit(solution)/shard_map/jrc,jcd->rd/dot_general | solution.py:180
  70.5 0.3 copy.84
  70.8 1.2 pad_maximum_fusion.1
  72.2 52.6 %all-gather.5.cloned.1.call-done.kv_ref = bf16[32768,128]{1,0:T(8,128)(2,1)} async-done(((bf16[2048,128]{1,0:T(8,128)(2,1)}), bf16[32768,128]{1,0:T(8,128)(2,1)}) %all-gather.5.cloned.1.call-update) | async-done | bytes 8388624 | tf_op jit(solution)/shard_map/all_gather | solution.py:190
  125.1 0.5 all-gather.9.cloned.1.call-update
  125.8 3.6 %fusion.8 = bf16[2048,64]{0,1:T(8,128)(2,1)S(1)} fusion(bf16[8,2048,96]{2,1,0:T(8,128)(2,1)} %shard_map.118, bf16[8,96,64]{1,0,2:T(8,128)(2,1)S(1)} %reshape.57), kind=kOutput, calls=%fused_computation.13 | convolution fusion | flops 201457664 | bytes 3506176 | tf_op jit(solution)/shard_map/jrc,jcd->rd/dot_general | solution.py:180
  129.3 0.3 copy.89
  129.7 0.9 concatenate.14.q_ref
  130.6 117.8 %shard_map.119 = bf16[2048,64]{1,0:T(8,128)(2,1)} custom-call(bf16[2048,128]{1,0:T(8,128)(2,1)} %concatenate.14.q_ref, bf16[32768,128]{1,0:T(8,128)(2,1)} %all-gather.5.cloned.1.call-done.kv_ref), custom_call_target="tpu_custom_call" | custom-call | flops 34359738368 | bytes 34340864 | tf_op jit(solution)/shard_map/pallas_call | solution.py:75
  248.4 1.2 copy.90
  249.6 6.6 %copy_bitcast_fusion = bf16[256,128,96]{1,2,0:T(8,128)(2,1)} fusion(bf16[32768,96]{0,1:T(8,128)(2,1)} %all-gather.7.cloned.1.call-done), kind=kLoop, calls=%fused_computation.1 | loop fusion | bytes 12582912 | tf_op jit(solution)/shard_map/reshape | solution.py:21
  256.2 3.6 %gather_fusion = bf16[64,128,96]{1,2,0:T(8,128)(2,1)S(1)} fusion(bf16[256,128,96]{1,2,0:T(8,128)(2,1)} %copy_bitcast_fusion, s32[1024]{0:T(1024)S(1)} %pad_clamp_fusion), kind=kCustom, calls=%fused_computation | custom fusion | bytes 3145984 | tf_op jit(solution)/shard_map/jit(_take)/gather | solution.py:22
  259.9 3.9 %fusion.11 = f32[64,128,96]{1,2,0:T(8,128)S(1)} fusion(s32[64,128,128]{2,1,0:T(8,128)} %param.15, bf16[64,128,96]{1,2,0:T(8,128)(2,1)S(1)} %gather_fusion, pred[64]{0:T(512)(128)(4,1)S(1)} %get-tuple-element.13), kind=kOutput, calls=%fused_computation.16 | convolution fusion | flops 203161600 | bytes 8912960 | tf_op jit(solution)/shard_map/ers,esf->erf/dot_general | solution.py:23
  263.8 2.9 fusion.26
  266.8 0.3 fusion.48
  267.1 0.9 copy.129
  268.0 6.6 %all-to-all-start = ((bf16[8,256,160]{1,2,0:T(8,128)(2,1)}), bf16[8,256,160]{1,2,0:T(8,128)(2,1)}, u32[]{:S(2)}, u32[]{:S(2)}) async-start(bf16[8,256,160]{1,2,0:T(8,128)(2,1)} %bitcast.89), calls=%async_computation | async-start | bytes 1310720 | tf_op jit(solution)/shard_map/all_to_all | solution.py:210
  274.6 1.1 convert_bitcast_fusion
  275.8 0.3 copy.78
  276.1 0.3 copy.93
  276.4 1.4 slice.31
  277.7 1.7 reshape.59
  279.5 8.7 %all-to-all-done = bf16[8,256,160]{1,2,0:T(8,128)(2,1)} async-done(((bf16[8,256,160]{1,2,0:T(8,128)(2,1)}), bf16[8,256,160]{1,2,0:T(8,128)(2,1)}, u32[]{:S(2)}, u32[]{:S(2)}) %all-to-all-start) | async-done | bytes 655392 | tf_op jit(solution)/shard_map/all_to_all | solution.py:210
  288.1 1.6 convolution_bitcast_fusion.3
  289.7 3.8 %fusion.70 = (f32[256]{0:T(256)S(1)}, f32[256]{0:T(256)S(1)}, f32[256,768]{1,0:T(8,128)}) fusion(f32[256,768]{1,0:T(8,128)S(1)} %convolution_bitcast_fusion.3, f32[256,768]{1,0:T(8,128)S(1)} %copy.93, bf16[8,640,768]{2,1,0:T(8,128)(2,1)} %bitcast.97, bf16[8,96,8,96]{3,2,1,0:T(8,128)(2,1)S(1)} %reshape.59, bf16[8,256,160]{1,2,0:T(8,128)(2,1)} %all-to-all-done), kind=kOutput, calls=%fused_computation.71 | convolution fusion | flops 605355520 | bytes 5113856 | tf_op jit(solution)/shard_map/rjc,jce->re/dot_general | solution.py:228
  293.6 5.3 %fusion.37 = bf16[256,768]{1,0:T(8,128)(2,1)S(1)} fusion(f32[256,768]{1,0:T(8,128)} %get-tuple-element.17, bf16[8,640,768]{2,1,0:T(8,128)(2,1)} %bitcast.98, f32[256]{0:T(256)S(1)} %get-tuple-element.16, f32[256]{0:T(256)S(1)} %get-tuple-element.15), kind=kOutput, calls=%fused_computation.31 | convolution fusion | flops 1209729024 | bytes 6686720 | tf_op jit(solution)/shard_map/rjc,jce->re/dot_general | solution.py:241
  299.0 13.0 %all_to_all.10 = bf16[8,256,96]{1,2,0:T(8,128)(2,1)S(1)} all-to-all(bf16[8,256,96]{1,2,0:T(8,128)(2,1)S(1)} %bitcast.93), channel_id=1, replica_groups=mesh['blk'=16,'mp'=8] {'mp'}, dimensions={0} | all-to-all | bytes 786432 | tf_op jit(solution)/shard_map/all_to_all | solution.py:244
  312.0 0.8 copy.102
  (45 shorter events, 1.2 us)
Async XLA Ops:
  6.5 56.1 %copy-start.6 = (bf16[768,64]{0,1:T(8,128)(2,1)S(1)}, bf16[768,64]{0,1:T(8,128)(2,1)}, u32[]{:S(2)}) copy-start(bf16[768,64]{0,1:T(8,128)(2,1)} %param.19) | copy-start | bytes 294916
  6.5 118.3 %all-gather.5.cloned.1.call-start = ((), (), s32[]{:S(2)}) async-start(), calls=%async_computation.2 | async-start | bytes 8912896 | tf_op jit(solution)/shard_map/all_gather | solution.py:190
  62.8 3.9 %copy-start.7 = (bf16[768,64]{0,1:T(8,128)(2,1)S(1)}, bf16[768,64]{0,1:T(8,128)(2,1)}, u32[]{:S(2)}) copy-start(bf16[768,64]{0,1:T(8,128)(2,1)} %param.20) | copy-start | bytes 294916
  66.9 5.2 %copy-start.4 = (bf16[768,96]{0,1:T(8,128)(2,1)S(1)}, bf16[768,96]{0,1:T(8,128)(2,1)}, u32[]{:S(2)}) copy-start(bf16[768,96]{0,1:T(8,128)(2,1)} %param.16) | copy-start | bytes 442372
  70.5 1.6 copy-start.2
  70.5 1.6 copy-start.5
  70.5 1.6 copy-start.9
  70.5 1.7 copy-start.3
  70.5 55.0 %copy-start.8 = (bf16[768,64]{0,1:T(8,128)(2,1)S(1)}, bf16[768,64]{0,1:T(8,128)(2,1)}, u32[]{:S(2)}) copy-start(bf16[768,64]{0,1:T(8,128)(2,1)} %param.18) | copy-start | bytes 294916
  72.0 177.6 %all-gather.7.cloned.1.call-start = ((), (), s32[]{:S(2)}) async-start(), calls=%async_computation.3 | async-start | bytes 6684672 | tf_op jit(solution)/shard_map/all_gather | solution.py:195
  72.2 52.9 %copy-start.1 = (bf16[640,768]{1,0:T(8,128)(2,1)}, bf16[640,768]{1,0:T(8,128)(2,1)S(1)}, u32[]{:S(2)}) copy-start(bf16[640,768]{1,0:T(8,128)(2,1)S(1)} %constant_dynamic-update-slice_fusion) | copy-start | bytes 2949124
  124.8 151.5 %all-gather.9.cloned.1.call-start = ((), (), s32[]{:S(2)}) async-start(), calls=%async_computation.4 | async-start | bytes 8847360 | tf_op jit(solution)/shard_map/all_gather | solution.py:196
  125.7 4.8 %copy-start.11 = (s32[64]{0:T(128)S(1)}, s32[64]{0:T(128)}, u32[]{:S(2)}) copy-start(s32[64]{0:T(128)} %param.14) | copy-start | bytes 772
  259.9 3.9 %copy-start.10 = (s32[64]{0:T(128)S(1)}, s32[64]{0:T(128)}, u32[]{:S(2)}) copy-start(s32[64]{0:T(128)} %param.13) | copy-start | bytes 772
  263.8 2.9 copy-start
  268.0 20.1 %all-to-all-start = ((bf16[8,256,160]{1,2,0:T(8,128)(2,1)}), bf16[8,256,160]{1,2,0:T(8,128)(2,1)}, u32[]{:S(2)}, u32[]{:S(2)}) async-start(bf16[8,256,160]{1,2,0:T(8,128)(2,1)} %bitcast.89), calls=%async_computation | async-start | bytes 1310720 | tf_op jit(solution)/shard_map/all_to_all | solution.py:210
Sparse Core Ops, SparseCore 0:
  72.1 52.6 all-gather.4
  126.5 43.1 all-gather.6
  172.0 103.3 all-gather.8

commit v8 on v7

--- a/solution.py
+++ b/solution.py
@@ -48,19 +48,19 @@
     s = lax.dot_general(
         q_ref[...], kv, (((1,), (1,)), ((), ())), preferred_element_type=jnp.float32
     )
-    m_prev = m_ref[...]
+    m_prev = m_ref[:, :1]
     m_new = jnp.maximum(m_prev, jnp.max(s, axis=1, keepdims=True))
     alpha = jnp.exp(m_prev - m_new)
     p = jnp.exp(s - m_new)
-    l_ref[...] = alpha * l_ref[...] + jnp.sum(p, axis=1, keepdims=True)
+    l_ref[...] = jnp.broadcast_to(alpha * l_ref[:, :1] + jnp.sum(p, axis=1, keepdims=True), l_ref.shape)
     acc_ref[...] = alpha * acc_ref[...] + jnp.dot(
         p.astype(jnp.bfloat16), kv, preferred_element_type=jnp.float32
     )
-    m_ref[...] = m_new
+    m_ref[...] = jnp.broadcast_to(m_new, m_ref.shape)
 
     @pl.when(j == pl.num_programs(1) - 1)
     def _():
-        o_ref[...] = (acc_ref[:, dim : 2 * dim] / l_ref[...]).astype(o_ref.dtype)
+        o_ref[...] = (acc_ref[:, dim : 2 * dim] / l_ref[:, :1]).astype(o_ref.dtype)
 
 
 def flash_attention(q, packed_all, head, heads):
@@ -82,8 +82,8 @@
         out_specs=pl.BlockSpec((tq, dim), lambda i, j: (i, 0)),
         out_shape=jax.ShapeDtypeStruct((rows, dim), jnp.bfloat16),
         scratch_shapes=[
-            pltpu.VMEM((tq, 1), jnp.float32),
-            pltpu.VMEM((tq, 1), jnp.float32),
+            pltpu.VMEM((tq, 128), jnp.float32),
+            pltpu.VMEM((tq, 128), jnp.float32),
             pltpu.VMEM((tq, lanes), jnp.float32),
         ],
         compiler_params=pltpu.CompilerParams(
@@ -97,7 +97,7 @@
     )(q_pad, packed_all)
 
 
-def gather_kernel(axis, n, x_ref, out_ref, send_sem, recv_sem, local_sem):
+def exchange_kernel(axis, n, scatter, x_ref, out_ref, send_sem, recv_sem, local_sem):
     me = lax.axis_index(axis)
     mesh_id = pl.DeviceIdType.MESH
     barrier = pltpu.get_barrier_semaphore()
@@ -106,12 +106,15 @@
             barrier, inc=1, device_id={axis: lax.rem(me + k, n)}, device_id_type=mesh_id
         )
     pl.semaphore_wait(barrier, n - 1)
-    local = pltpu.make_async_copy(x_ref, out_ref.at[me], local_sem)
+    def part(device):
+        return x_ref.at[device] if scatter else x_ref
+
+    local = pltpu.make_async_copy(part(me), out_ref.at[me], local_sem)
     local.start()
     sends = []
     for k in range(1, n):
         copy = pltpu.make_async_remote_copy(
-            src_ref=x_ref,
+            src_ref=part(lax.rem(me + k, n)),
             dst_ref=out_ref.at[me],
             send_sem=send_sem.at[k],
             recv_sem=recv_sem.at[k],
@@ -123,7 +126,7 @@
     for k in range(1, n):
         source = lax.rem(me + n - k, n)
         arriving = pltpu.make_async_remote_copy(
-            src_ref=x_ref,
+            src_ref=part(me),
             dst_ref=out_ref.at[source],
             send_sem=send_sem.at[k],
             recv_sem=recv_sem.at[k],
@@ -136,13 +139,14 @@
     local.wait()
 
 
-def dma_all_gather(x, axis, collective_id):
+def dma_exchange(x, axis, collective_id, scatter):
     n = lax.axis_size(axis)
+    out_shape = x.shape if scatter else (n,) + x.shape
     return pl.pallas_call(
-        functools.partial(gather_kernel, axis, n),
+        functools.partial(exchange_kernel, axis, n, scatter),
         in_specs=[pl.BlockSpec(memory_space=pl.ANY)],
         out_specs=pl.BlockSpec(memory_space=pl.ANY),
-        out_shape=jax.ShapeDtypeStruct((n,) + x.shape, x.dtype),
+        out_shape=jax.ShapeDtypeStruct(out_shape, x.dtype),
         scratch_shapes=[
             pltpu.SemaphoreType.DMA((n,)),
             pltpu.SemaphoreType.DMA((n,)),
@@ -174,7 +178,7 @@
     heads = w_query.shape[1] // HEAD_DIM
     scale = 1.0 / math.sqrt(HEAD_DIM)
 
-    feature_parts = dma_all_gather(features, "mp", 0)
+    feature_parts = dma_exchange(features, "mp", 0, False)
 
     def project(w):
         return jnp.einsum(
@@ -207,7 +211,7 @@
     local_share = (features.astype(jnp.float32) + gathered * 0.25).astype(jnp.bfloat16)
 
     mixed_in = jnp.concatenate([local_share, attended], axis=1).reshape(n_mp, share, -1)
-    received = lax.all_to_all(mixed_in, "mp", 0, 0, tiled=False)
+    received = dma_exchange(mixed_in, "mp", 1, True)
     own_rows = (
         lax.dynamic_slice_in_dim(feature_parts, me * share, share, 1)
         .transpose(1, 0, 2)
@@ -241,7 +245,7 @@
         + jnp.einsum("rjc,jce->re", ffn_hidden, ffn_out_parts, preferred_element_type=jnp.float32)
     ).astype(jnp.bfloat16)
     out_parts = out_rows.reshape(share, n_mp, cols).transpose(1, 0, 2)
-    return lax.all_to_all(out_parts, "mp", 0, 0, tiled=False).reshape(rows, cols)
+    return dma_exchange(out_parts, "mp", 2, True).reshape(rows, cols)
 
 
 def solution(mesh):

time: 320 us -> 324 us (1.012)
  Pallas kernels: 172 us -> 200 us
  blocking collectives: 13 us -> 0 us
  waiting for transfers between devices: 61.8 us -> 53.3 us
  starting transfers between devices: 6.89 us -> 0.08 us
    pallas_call x1 -> x3, Pallas kernels: 54 us -> 86.4 us  [dma_exchange(): pl.pallas_call(functools.partial(exchange_kernel, axis, n, scatter), in_s...]
    all_to_all x1 -> x0, blocking collectives: 13 us -> none  [per_device(): lax.all_to_all(out_parts, 'mp', 0, 0, tiled=False).reshape(rows, cols)]
    all_to_all x1 -> x0, waiting for transfers between devices: 8.66 us -> none  [per_device(): received = lax.all_to_all(mixed_in, 'mp', 0, 0, tiled=False)]
    all_to_all x1 -> x0, starting transfers between devices: 6.62 us -> none  [per_device(): received = lax.all_to_all(mixed_in, 'mp', 0, 0, tiled=False)]
    pallas_call x1, Pallas kernels: 118 us -> 113 us  [flash_attention(): pl.pallas_call(functools.partial(flash_kernel, dim), grid=grid, in_specs=...]
  transfers between devices with their start and end apart: 4 -> 3, of which waited for: 2 -> 1; matrix products, arithmetic and copies ran while one was open for 9% -> 8% of each run, Pallas kernels for 37% -> 42%
where the time goes in v8:
time: 324 us; the launch traced here: 323 us
  Pallas kernels  200 us (62%)
  waiting for transfers between devices  53.3 us (16%)
  matrix products  29.8 us (9%)
  local copies, waits for them, and re-layouts  24.1 us (7%)
  between operations  13.5 us (4%)
    pallas_call x1, Pallas kernels, flash_attention(): pl.pallas_call(functools.partial(flash_kernel, dim), grid=grid, in_specs=...  113 us
    pallas_call x3, Pallas kernels, dma_exchange(): pl.pallas_call(functools.partial(exchange_kernel, axis, n, scatter), in_s...  86.4 us
    all_gather x1, waiting for transfers between devices, per_device(): lax.all_gather(jnp.concatenate([keys, values], axis=1), 'blk', axis=0, ti...  52.6 us
    dot_general x3, matrix products, project(): jnp.einsum('jrc,jcd->rd', feature_parts, w.reshape(n_mp, cols, w.shape[1]...  10.7 us
    reshape x1, local copies, waits for them, and re-layouts, neighbour_sum(): blocks = all_features.reshape(count, BLOCK, cols)  6.52 us
  transfers between devices with their start and end apart: 3, of which 1 were waited for; matrix products, arithmetic and copies ran while one was open for 8% of the time, Pallas kernels for 42%

profile of v8, /device:TPU:0, one launch (start us, length us, event | category | flops | bytes accessed | tf_op | source)
XLA Modules:
  0.0 323.2 jit_solution(10125983444170453602)
XLA Ops:
  6.5 2.0 copy.88.x_ref
  8.6 54.0 %shard_map.118 = bf16[8,2048,96]{2,1,0:T(8,128)(2,1)} custom-call(bf16[2048,96]{1,0:T(8,128)(2,1)} %copy.88.x_ref), custom_call_target="tpu_custom_call" | custom-call | tf_op jit(solution)/shard_map/pallas_call | solution.py:145
  62.8 3.6 %fusion.6 = bf16[2048,64]{0,1:T(8,128)(2,1)S(1)} fusion(bf16[8,2048,96]{2,1,0:T(8,128)(2,1)} %shard_map.118, bf16[8,96,64]{1,0,2:T(8,128)(2,1)S(1)} %reshape.54), kind=kOutput, calls=%fused_computation.11 | convolution fusion | flops 201457664 | bytes 3506176 | tf_op jit(solution)/shard_map/jrc,jcd->rd/dot_general | solution.py:184
  66.4 0.3 copy.94
  66.9 3.6 %fusion.7 = bf16[2048,64]{0,1:T(8,128)(2,1)S(1)} fusion(bf16[8,2048,96]{2,1,0:T(8,128)(2,1)} %shard_map.118, bf16[8,96,64]{1,0,2:T(8,128)(2,1)S(1)} %reshape.55), kind=kOutput, calls=%fused_computation.12 | convolution fusion | flops 201457664 | bytes 3506176 | tf_op jit(solution)/shard_map/jrc,jcd->rd/dot_general | solution.py:184
  70.6 0.3 copy.95
  70.8 1.1 pad_maximum_fusion.1
  72.2 52.6 %all-gather.5.cloned.1.call-done.kv_ref = bf16[32768,128]{1,0:T(8,128)(2,1)} async-done(((bf16[2048,128]{1,0:T(8,128)(2,1)}), bf16[32768,128]{1,0:T(8,128)(2,1)}) %all-gather.5.cloned.1.call-update) | async-done | bytes 8388624 | tf_op jit(solution)/shard_map/all_gather | solution.py:194
  124.9 0.7 all-gather.9.cloned.1.call-update
  125.7 3.6 %fusion.8 = bf16[2048,64]{0,1:T(8,128)(2,1)S(1)} fusion(bf16[8,2048,96]{2,1,0:T(8,128)(2,1)} %shard_map.118, bf16[8,96,64]{1,0,2:T(8,128)(2,1)S(1)} %reshape.57), kind=kOutput, calls=%fused_computation.13 | convolution fusion | flops 201457664 | bytes 3506176 | tf_op jit(solution)/shard_map/jrc,jcd->rd/dot_general | solution.py:184
  129.3 0.3 copy.100
  129.6 1.1 convert_bitcast_fusion
  130.7 0.3 copy.89
  131.1 0.3 copy.105
  131.4 0.9 concatenate.14.q_ref
  132.3 113.3 %shard_map.119 = bf16[2048,64]{1,0:T(8,128)(2,1)} custom-call(bf16[2048,128]{1,0:T(8,128)(2,1)} %concatenate.14.q_ref, bf16[32768,128]{1,0:T(8,128)(2,1)} %all-gather.5.cloned.1.call-done.kv_ref), custom_call_target="tpu_custom_call" | custom-call | flops 34359738368 | bytes 34340864 | tf_op jit(solution)/shard_map/pallas_call | solution.py:75
  245.6 1.2 copy.101
  246.9 6.5 %copy_bitcast_fusion = bf16[256,128,96]{1,2,0:T(8,128)(2,1)} fusion(bf16[32768,96]{0,1:T(8,128)(2,1)} %all-gather.7.cloned.1.call-done), kind=kLoop, calls=%fused_computation.1 | loop fusion | bytes 12582912 | tf_op jit(solution)/shard_map/reshape | solution.py:21
  253.4 3.6 %gather_fusion = bf16[64,128,96]{1,2,0:T(8,128)(2,1)S(1)} fusion(bf16[256,128,96]{1,2,0:T(8,128)(2,1)} %copy_bitcast_fusion, s32[1024]{0:T(1024)S(1)} %pad_clamp_fusion), kind=kCustom, calls=%fused_computation | custom fusion | bytes 3145984 | tf_op jit(solution)/shard_map/jit(_take)/gather | solution.py:22
  257.0 3.8 %fusion.11 = f32[64,128,96]{1,2,0:T(8,128)S(1)} fusion(s32[64,128,128]{2,1,0:T(8,128)} %param.15, bf16[64,128,96]{1,2,0:T(8,128)(2,1)S(1)} %gather_fusion, pred[64]{0:T(512)(128)(4,1)S(1)} %get-tuple-element.13), kind=kOutput, calls=%fused_computation.16 | convolution fusion | flops 203161600 | bytes 8912960 | tf_op jit(solution)/shard_map/ers,esf->erf/dot_general | solution.py:23
  260.9 2.9 fusion.26
  263.8 0.3 fusion.48
  264.2 1.3 copy.102
  265.5 21.1 %shard_map.120 = bf16[8,256,160]{2,1,0:T(8,128)(2,1)} custom-call(bf16[8,256,160]{2,1,0:T(8,128)(2,1)} %bitcast.85), custom_call_target="tpu_custom_call" | custom-call | tf_op jit(solution)/shard_map/pallas_call | solution.py:145
  286.6 1.4 slice.30
  288.0 2.9 convolution_bitcast_fusion.3
  290.9 1.9 reshape.59
  292.8 4.1 %fusion.74 = (f32[256]{0:T(256)S(1)}, f32[256]{0:T(256)S(1)}, f32[256,768]{1,0:T(8,128)}) fusion(f32[256,768]{1,0:T(8,128)} %convolution_bitcast_fusion.3, f32[256,768]{1,0:T(8,128)S(1)} %copy.105, bf16[8,640,768]{2,1,0:T(8,128)(2,1)} %bitcast.93, bf16[8,96,8,96]{3,2,1,0:T(8,128)(2,1)S(1)} %reshape.59, bf16[8,256,160]{2,1,0:T(8,128)(2,1)} %shard_map.120), kind=kOutput, calls=%fused_computation.71 | convolution fusion | flops 605355520 | bytes 5244928 | tf_op jit(solution)/shard_map/rjc,jce->re/dot_general | solution.py:232
  296.9 5.3 %fusion.37 = bf16[256,768]{1,0:T(8,128)(2,1)S(1)} fusion(f32[256,768]{1,0:T(8,128)} %get-tuple-element.17, bf16[8,640,768]{2,1,0:T(8,128)(2,1)} %bitcast.94, f32[256]{0:T(256)S(1)} %get-tuple-element.16, f32[256]{0:T(256)S(1)} %get-tuple-element.15), kind=kOutput, calls=%fused_computation.31 | convolution fusion | flops 1209729024 | bytes 6686720 | tf_op jit(solution)/shard_map/rjc,jce->re/dot_general | solution.py:245
  302.4 1.0 copy.108
  303.4 11.3 %shard_map.121 = bf16[8,256,96]{2,1,0:T(8,128)(2,1)} custom-call(bf16[8,256,96]{2,1,0:T(8,128)(2,1)} %bitcast.88), custom_call_target="tpu_custom_call" | custom-call | tf_op jit(solution)/shard_map/pallas_call | solution.py:145
  314.7 2.0 copy.109
  (45 shorter events, 1.1 us)
Async XLA Ops:
  6.5 56.1 %copy-start.6 = (bf16[768,64]{0,1:T(8,128)(2,1)S(1)}, bf16[768,64]{0,1:T(8,128)(2,1)}, u32[]{:S(2)}) copy-start(bf16[768,64]{0,1:T(8,128)(2,1)} %param.19) | copy-start | bytes 294916
  6.5 118.3 %all-gather.5.cloned.1.call-start = ((), (), s32[]{:S(2)}) async-start(), calls=%async_computation | async-start | bytes 8912896 | tf_op jit(solution)/shard_map/all_gather | solution.py:194
  62.8 3.9 %copy-start.7 = (bf16[768,64]{0,1:T(8,128)(2,1)S(1)}, bf16[768,64]{0,1:T(8,128)(2,1)}, u32[]{:S(2)}) copy-start(bf16[768,64]{0,1:T(8,128)(2,1)} %param.20) | copy-start | bytes 294916
  66.9 5.2 %copy-start.4 = (bf16[768,96]{0,1:T(8,128)(2,1)S(1)}, bf16[768,96]{0,1:T(8,128)(2,1)}, u32[]{:S(2)}) copy-start(bf16[768,96]{0,1:T(8,128)(2,1)} %param.16) | copy-start | bytes 442372
  70.5 1.6 copy-start.2
  70.5 1.6 copy-start.5
  70.5 1.6 copy-start.9
  70.5 1.6 copy-start.3
  70.5 55.0 %copy-start.8 = (bf16[768,64]{0,1:T(8,128)(2,1)S(1)}, bf16[768,64]{0,1:T(8,128)(2,1)}, u32[]{:S(2)}) copy-start(bf16[768,64]{0,1:T(8,128)(2,1)} %param.18) | copy-start | bytes 294916
  72.0 174.9 %all-gather.7.cloned.1.call-start = ((), (), s32[]{:S(2)}) async-start(), calls=%async_computation.1 | async-start | bytes 6684672 | tf_op jit(solution)/shard_map/all_gather | solution.py:199
  72.2 52.7 %copy-start.1 = (bf16[640,768]{1,0:T(8,128)(2,1)}, bf16[640,768]{1,0:T(8,128)(2,1)S(1)}, u32[]{:S(2)}) copy-start(bf16[640,768]{1,0:T(8,128)(2,1)S(1)} %constant_dynamic-update-slice_fusion) | copy-start | bytes 2949124
  124.8 161.8 %all-gather.9.cloned.1.call-start = ((), (), s32[]{:S(2)}) async-start(), calls=%async_computation.2 | async-start | bytes 8847360 | tf_op jit(solution)/shard_map/all_gather | solution.py:200
  130.7 1.6 copy-start.11
  257.0 3.8 %copy-start.10 = (s32[64]{0:T(128)S(1)}, s32[64]{0:T(128)}, u32[]{:S(2)}) copy-start(s32[64]{0:T(128)} %param.13) | copy-start | bytes 772
  260.9 2.9 copy-start
Sparse Core Ops, SparseCore 0:
  72.1 52.6 all-gather.4
  126.5 43.1 all-gather.6
  172.0 111.2 all-gather.8

commit v9 on v8

--- a/solution.py
+++ b/solution.py
@@ -211,7 +211,7 @@
     local_share = (features.astype(jnp.float32) + gathered * 0.25).astype(jnp.bfloat16)
 
     mixed_in = jnp.concatenate([local_share, attended], axis=1).reshape(n_mp, share, -1)
-    received = dma_exchange(mixed_in, "mp", 1, True)
+    received = lax.all_to_all(mixed_in, "mp", 0, 0, tiled=False)
     own_rows = (
         lax.dynamic_slice_in_dim(feature_parts, me * share, share, 1)
         .transpose(1, 0, 2)
@@ -245,7 +245,7 @@
         + jnp.einsum("rjc,jce->re", ffn_hidden, ffn_out_parts, preferred_element_type=jnp.float32)
     ).astype(jnp.bfloat16)
     out_parts = out_rows.reshape(share, n_mp, cols).transpose(1, 0, 2)
-    return dma_exchange(out_parts, "mp", 2, True).reshape(rows, cols)
+    return lax.all_to_all(out_parts, "mp", 0, 0, tiled=False).reshape(rows, cols)
 
 
 def solution(mesh):

time: 324 us -> 315 us (0.972)
  Pallas kernels: 200 us -> 167 us
  blocking collectives: 0 us -> 13 us
  waiting for transfers between devices: 53.3 us -> 61.8 us
  starting transfers between devices: 0.08 us -> 7.03 us
    pallas_call x3 -> x1, Pallas kernels: 86.4 us -> 54 us  [dma_exchange(): pl.pallas_call(functools.partial(exchange_kernel, axis, n, scatter), in_s...]
    all_to_all x0 -> x1, blocking collectives: none -> 13 us  [per_device(): lax.all_to_all(out_parts, 'mp', 0, 0, tiled=False).reshape(rows, cols)]
    all_to_all x0 -> x1, starting transfers between devices: none -> 6.77 us  [per_device(): received = lax.all_to_all(mixed_in, 'mp', 0, 0, tiled=False)]
    all_gather x1, waiting for transfers between devices: 0.02 us -> 4.96 us  [per_device(): weight_parts = lax.all_gather(packed_weights, 'mp', axis=0, tiled=False)]
    all_to_all x0 -> x1, waiting for transfers between devices: none -> 3.73 us  [per_device(): received = lax.all_to_all(mixed_in, 'mp', 0, 0, tiled=False)]
  transfers between devices with their start and end apart: 3 -> 4, of which waited for: 1 -> 3; matrix products, arithmetic and copies ran while one was open for 8% -> 9% of each run, Pallas kernels for 42% -> 36%
where the time goes in v9:
time: 315 us
  Pallas kernels  167 us (53%)
  waiting for transfers between devices  61.8 us (20%)
  matrix products  28.2 us (9%)
  local copies, waits for them, and re-layouts  21.3 us (7%)
  between operations  13.5 us (4%)
  blocking collectives  13 us (4%)
  starting transfers between devices  7.03 us (2%)
    pallas_call x1, Pallas kernels, flash_attention(): pl.pallas_call(functools.partial(flash_kernel, dim), grid=grid, in_specs=...  113 us
    pallas_call x1, Pallas kernels, dma_exchange(): pl.pallas_call(functools.partial(exchange_kernel, axis, n, scatter), in_s...  54 us
    all_gather x1, waiting for transfers between devices, per_device(): lax.all_gather(jnp.concatenate([keys, values], axis=1), 'blk', axis=0, ti...  52.6 us
    all_to_all x1, blocking collectives, per_device(): lax.all_to_all(out_parts, 'mp', 0, 0, tiled=False).reshape(rows, cols)  13 us
    dot_general x3, matrix products, project(): jnp.einsum('jrc,jcd->rd', feature_parts, w.reshape(n_mp, cols, w.shape[1]...  10.8 us
    all_to_all x1, starting transfers between devices, per_device(): received = lax.all_to_all(mixed_in, 'mp', 0, 0, tiled=False)  6.77 us
    reshape x1, local copies, waits for them, and re-layouts, neighbour_sum(): blocks = all_features.reshape(count, BLOCK, cols)  6.53 us
  transfers between devices with their start and end apart: 4, of which 3 were waited for; matrix products, arithmetic and copies ran while one was open for 9% of the time, Pallas kernels for 36%

profile of v9, /device:TPU:0, one launch (start us, length us, event | category | flops | bytes accessed | tf_op | source)
XLA Modules:
  0.0 314.6 jit_solution(10936832084654673819)
XLA Ops:
  6.5 2.0 copy.77.x_ref
  8.6 54.0 %shard_map.118 = bf16[8,2048,96]{2,1,0:T(8,128)(2,1)} custom-call(bf16[2048,96]{1,0:T(8,128)(2,1)} %copy.77.x_ref), custom_call_target="tpu_custom_call" | custom-call | tf_op jit(solution)/shard_map/pallas_call | solution.py:145
  62.8 3.6 %fusion.6 = bf16[2048,64]{0,1:T(8,128)(2,1)S(1)} fusion(bf16[8,2048,96]{2,1,0:T(8,128)(2,1)} %shard_map.118, bf16[8,96,64]{1,0,2:T(8,128)(2,1)S(1)} %reshape.54), kind=kOutput, calls=%fused_computation.11 | convolution fusion | flops 201457664 | bytes 3506176 | tf_op jit(solution)/shard_map/jrc,jcd->rd/dot_general | solution.py:184
  66.4 0.3 copy.83
  66.9 3.6 %fusion.7 = bf16[2048,64]{0,1:T(8,128)(2,1)S(1)} fusion(bf16[8,2048,96]{2,1,0:T(8,128)(2,1)} %shard_map.118, bf16[8,96,64]{1,0,2:T(8,128)(2,1)S(1)} %reshape.55), kind=kOutput, calls=%fused_computation.12 | convolution fusion | flops 201457664 | bytes 3506176 | tf_op jit(solution)/shard_map/jrc,jcd->rd/dot_general | solution.py:184
  70.5 0.3 copy.84
  70.8 1.2 pad_maximum_fusion.1
  72.2 52.6 %all-gather.5.cloned.1.call-done.kv_ref = bf16[32768,128]{1,0:T(8,128)(2,1)} async-done(((bf16[2048,128]{1,0:T(8,128)(2,1)}), bf16[32768,128]{1,0:T(8,128)(2,1)}) %all-gather.5.cloned.1.call-update) | async-done | bytes 8388624 | tf_op jit(solution)/shard_map/all_gather | solution.py:194
  125.1 0.5 all-gather.9.cloned.1.call-update
  125.8 3.6 %fusion.8 = bf16[2048,64]{0,1:T(8,128)(2,1)S(1)} fusion(bf16[8,2048,96]{2,1,0:T(8,128)(2,1)} %shard_map.118, bf16[8,96,64]{1,0,2:T(8,128)(2,1)S(1)} %reshape.57), kind=kOutput, calls=%fused_computation.13 | convolution fusion | flops 201457664 | bytes 3506176 | tf_op jit(solution)/shard_map/jrc,jcd->rd/dot_general | solution.py:184
  129.3 0.3 copy.89
  129.7 0.9 concatenate.14.q_ref
  130.6 113.1 %shard_map.119 = bf16[2048,64]{1,0:T(8,128)(2,1)} custom-call(bf16[2048,128]{1,0:T(8,128)(2,1)} %concatenate.14.q_ref, bf16[32768,128]{1,0:T(8,128)(2,1)} %all-gather.5.cloned.1.call-done.kv_ref), custom_call_target="tpu_custom_call" | custom-call | flops 34359738368 | bytes 34340864 | tf_op jit(solution)/shard_map/pallas_call | solution.py:75
  243.7 1.2 copy.90
  245.0 6.5 %copy_bitcast_fusion = bf16[256,128,96]{1,2,0:T(8,128)(2,1)} fusion(bf16[32768,96]{0,1:T(8,128)(2,1)} %all-gather.7.cloned.1.call-done), kind=kLoop, calls=%fused_computation.1 | loop fusion | bytes 12582912 | tf_op jit(solution)/shard_map/reshape | solution.py:21
  251.5 3.6 %gather_fusion = bf16[64,128,96]{1,2,0:T(8,128)(2,1)S(1)} fusion(bf16[256,128,96]{1,2,0:T(8,128)(2,1)} %copy_bitcast_fusion, s32[1024]{0:T(1024)S(1)} %pad_clamp_fusion), kind=kCustom, calls=%fused_computation | custom fusion | bytes 3145984 | tf_op jit(solution)/shard_map/jit(_take)/gather | solution.py:22
  255.2 3.8 %fusion.11 = f32[64,128,96]{1,2,0:T(8,128)S(1)} fusion(s32[64,128,128]{2,1,0:T(8,128)} %param.15, bf16[64,128,96]{1,2,0:T(8,128)(2,1)S(1)} %gather_fusion, pred[64]{0:T(512)(128)(4,1)S(1)} %get-tuple-element.13), kind=kOutput, calls=%fused_computation.16 | convolution fusion | flops 203161600 | bytes 8912960 | tf_op jit(solution)/shard_map/ers,esf->erf/dot_general | solution.py:23
  259.0 2.9 fusion.26
  261.9 0.3 fusion.48
  262.3 0.9 copy.129
  263.2 6.8 %all-to-all-start = ((bf16[8,256,160]{1,2,0:T(8,128)(2,1)}), bf16[8,256,160]{1,2,0:T(8,128)(2,1)}, u32[]{:S(2)}, u32[]{:S(2)}) async-start(bf16[8,256,160]{1,2,0:T(8,128)(2,1)} %bitcast.89), calls=%async_computation | async-start | bytes 1310720 | tf_op jit(solution)/shard_map/all_to_all | solution.py:214
  269.9 1.1 convert_bitcast_fusion
  271.1 0.3 copy.78
  271.7 5.0 %all-gather.9.cloned.1.call-done = bf16[5120,768]{1,0:T(8,128)(2,1)} async-done(((bf16[640,768]{1,0:T(8,128)(2,1)}), bf16[5120,768]{1,0:T(8,128)(2,1)}) %all-gather.9.cloned.1.call-update) | async-done | bytes 7864336 | tf_op jit(solution)/shard_map/all_gather | solution.py:200
  276.6 1.3 slice.31
  278.0 1.7 reshape.59
  279.7 3.7 %all-to-all-done = bf16[8,256,160]{1,2,0:T(8,128)(2,1)} async-done(((bf16[8,256,160]{1,2,0:T(8,128)(2,1)}), bf16[8,256,160]{1,2,0:T(8,128)(2,1)}, u32[]{:S(2)}, u32[]{:S(2)}) %all-to-all-start) | async-done | bytes 655392 | tf_op jit(solution)/shard_map/all_to_all | solution.py:214
  283.4 1.6 convolution_bitcast_fusion.3
  285.0 3.8 %fusion.70 = (f32[256]{0:T(256)S(1)}, f32[256]{0:T(256)S(1)}, f32[256,768]{1,0:T(8,128)}) fusion(f32[256,768]{1,0:T(8,128)S(1)} %convolution_bitcast_fusion.3, f32[256,768]{1,0:T(8,128)S(1)} %copy.93, bf16[8,640,768]{2,1,0:T(8,128)(2,1)} %bitcast.97, bf16[8,96,8,96]{3,2,1,0:T(8,128)(2,1)S(1)} %reshape.59, bf16[8,256,160]{1,2,0:T(8,128)(2,1)} %all-to-all-done), kind=kOutput, calls=%fused_computation.71 | convolution fusion | flops 605355520 | bytes 5113856 | tf_op jit(solution)/shard_map/rjc,jce->re/dot_general | solution.py:232
  288.9 5.3 %fusion.37 = bf16[256,768]{1,0:T(8,128)(2,1)S(1)} fusion(f32[256,768]{1,0:T(8,128)} %get-tuple-element.17, bf16[8,640,768]{2,1,0:T(8,128)(2,1)} %bitcast.98, f32[256]{0:T(256)S(1)} %get-tuple-element.16, f32[256]{0:T(256)S(1)} %get-tuple-element.15), kind=kOutput, calls=%fused_computation.31 | convolution fusion | flops 1209729024 | bytes 6686720 | tf_op jit(solution)/shard_map/rjc,jce->re/dot_general | solution.py:245
  294.3 13.0 %all_to_all.10 = bf16[8,256,96]{1,2,0:T(8,128)(2,1)S(1)} all-to-all(bf16[8,256,96]{1,2,0:T(8,128)(2,1)S(1)} %bitcast.93), channel_id=1, replica_groups=mesh['blk'=16,'mp'=8] {'mp'}, dimensions={0} | all-to-all | bytes 786432 | tf_op jit(solution)/shard_map/all_to_all | solution.py:248
  307.3 0.8 copy.102
  (45 shorter events, 1.5 us)
Async XLA Ops:
  6.5 56.1 %copy-start.6 = (bf16[768,64]{0,1:T(8,128)(2,1)S(1)}, bf16[768,64]{0,1:T(8,128)(2,1)}, u32[]{:S(2)}) copy-start(bf16[768,64]{0,1:T(8,128)(2,1)} %param.19) | copy-start | bytes 294916
  6.5 118.3 %all-gather.5.cloned.1.call-start = ((), (), s32[]{:S(2)}) async-start(), calls=%async_computation.2 | async-start | bytes 8912896 | tf_op jit(solution)/shard_map/all_gather | solution.py:194
  62.8 3.9 %copy-start.7 = (bf16[768,64]{0,1:T(8,128)(2,1)S(1)}, bf16[768,64]{0,1:T(8,128)(2,1)}, u32[]{:S(2)}) copy-start(bf16[768,64]{0,1:T(8,128)(2,1)} %param.20) | copy-start | bytes 294916
  66.9 5.2 %copy-start.4 = (bf16[768,96]{0,1:T(8,128)(2,1)S(1)}, bf16[768,96]{0,1:T(8,128)(2,1)}, u32[]{:S(2)}) copy-start(bf16[768,96]{0,1:T(8,128)(2,1)} %param.16) | copy-start | bytes 442372
  70.5 1.6 copy-start.2
  70.5 1.6 copy-start.5
  70.5 1.6 copy-start.9
  70.5 1.7 copy-start.3
  70.5 55.0 %copy-start.8 = (bf16[768,64]{0,1:T(8,128)(2,1)S(1)}, bf16[768,64]{0,1:T(8,128)(2,1)}, u32[]{:S(2)}) copy-start(bf16[768,64]{0,1:T(8,128)(2,1)} %param.18) | copy-start | bytes 294916
  72.0 173.0 %all-gather.7.cloned.1.call-start = ((), (), s32[]{:S(2)}) async-start(), calls=%async_computation.3 | async-start | bytes 6684672 | tf_op jit(solution)/shard_map/all_gather | solution.py:199
  72.2 52.9 %copy-start.1 = (bf16[640,768]{1,0:T(8,128)(2,1)}, bf16[640,768]{1,0:T(8,128)(2,1)S(1)}, u32[]{:S(2)}) copy-start(bf16[640,768]{1,0:T(8,128)(2,1)S(1)} %constant_dynamic-update-slice_fusion) | copy-start | bytes 2949124
  124.8 151.8 %all-gather.9.cloned.1.call-start = ((), (), s32[]{:S(2)}) async-start(), calls=%async_computation.4 | async-start | bytes 8847360 | tf_op jit(solution)/shard_map/all_gather | solution.py:200
  125.7 4.8 %copy-start.11 = (s32[64]{0:T(128)S(1)}, s32[64]{0:T(128)}, u32[]{:S(2)}) copy-start(s32[64]{0:T(128)} %param.14) | copy-start | bytes 772
  255.2 3.8 %copy-start.10 = (s32[64]{0:T(128)S(1)}, s32[64]{0:T(128)}, u32[]{:S(2)}) copy-start(s32[64]{0:T(128)} %param.13) | copy-start | bytes 772
  259.0 2.9 copy-start
  263.2 20.3 %all-to-all-start = ((bf16[8,256,160]{1,2,0:T(8,128)(2,1)}), bf16[8,256,160]{1,2,0:T(8,128)(2,1)}, u32[]{:S(2)}, u32[]{:S(2)}) async-start(bf16[8,256,160]{1,2,0:T(8,128)(2,1)} %bitcast.89), calls=%async_computation | async-start | bytes 1310720 | tf_op jit(solution)/shard_map/all_to_all | solution.py:214
Sparse Core Ops, SparseCore 0:
  72.1 52.6 all-gather.4
  126.5 43.1 all-gather.6
  172.0 104.5 all-gather.8

commit v10 on v9

--- a/solution.py
+++ b/solution.py
@@ -10,7 +10,7 @@
 
 HEAD_DIM = 64
 BLOCK = 128
-Q_TILE = 512
+Q_TILE = 1024
 K_TILE = 4096
 
 
@@ -144,7 +144,7 @@
     out_shape = x.shape if scatter else (n,) + x.shape
     return pl.pallas_call(
         functools.partial(exchange_kernel, axis, n, scatter),
-        in_specs=[pl.BlockSpec(memory_space=pl.ANY)],
+        in_specs=[pl.BlockSpec(memory_space=pltpu.VMEM)],
         out_specs=pl.BlockSpec(memory_space=pl.ANY),
         out_shape=jax.ShapeDtypeStruct(out_shape, x.dtype),
         scratch_shapes=[

time: 315 us -> 318 us (level)
  waiting for transfers between devices: 61.8 us -> 68.4 us
    all_gather x1, waiting for transfers between devices: 4.96 us -> 15.1 us  [per_device(): weight_parts = lax.all_gather(packed_weights, 'mp', axis=0, tiled=False)]
    pallas_call x1, Pallas kernels: 113 us -> 109 us  [flash_attention(): pl.pallas_call(functools.partial(flash_kernel, dim), grid=grid, in_specs=...]
    all_to_all x1, waiting for transfers between devices: 3.73 us -> 0.01 us  [per_device(): received = lax.all_to_all(mixed_in, 'mp', 0, 0, tiled=False)]
  transfers between devices with their start and end apart: 4 -> 4, of which waited for: 3 -> 2; matrix products, arithmetic and copies ran while one was open for 9% -> 9% of each run, Pallas kernels for 36% -> 34%
where the time goes in v10:
time: 318 us; the launch traced here: 317 us
  Pallas kernels  164 us (52%)
  waiting for transfers between devices  68.4 us (22%)
  matrix products  28.2 us (9%)
  local copies, waits for them, and re-layouts  21.3 us (7%)
  between operations  13.5 us (4%)
  blocking collectives  12.6 us (4%)
  starting transfers between devices  6.84 us (2%)
    pallas_call x1, Pallas kernels, flash_attention(): pl.pallas_call(functools.partial(flash_kernel, dim), grid=grid, in_specs=...  109 us
    pallas_call x1, Pallas kernels, dma_exchange(): pl.pallas_call(functools.partial(exchange_kernel, axis, n, scatter), in_s...  54.9 us
    all_gather x1, waiting for transfers between devices, per_device(): lax.all_gather(jnp.concatenate([keys, values], axis=1), 'blk', axis=0, ti...  52.6 us
    all_gather x1, waiting for transfers between devices, per_device(): weight_parts = lax.all_gather(packed_weights, 'mp', axis=0, tiled=False)  15.1 us
    all_to_all x1, blocking collectives, per_device(): lax.all_to_all(out_parts, 'mp', 0, 0, tiled=False).reshape(rows, cols)  12.6 us
    dot_general x3, matrix products, project(): jnp.einsum('jrc,jcd->rd', feature_parts, w.reshape(n_mp, cols, w.shape[1]...  10.8 us
    all_to_all x1, starting transfers between devices, per_device(): received = lax.all_to_all(mixed_in, 'mp', 0, 0, tiled=False)  6.75 us
    reshape x1, local copies, waits for them, and re-layouts, neighbour_sum(): blocks = all_features.reshape(count, BLOCK, cols)  6.57 us
  transfers between devices with their start and end apart: 4, of which 2 were waited for; matrix products, arithmetic and copies ran while one was open for 9% of the time, Pallas kernels for 34%

profile of v10, /device:TPU:0, one launch (start us, length us, event | category | flops | bytes accessed | tf_op | source)
XLA Modules:
  0.0 317.2 jit_solution(637784759052968686)
XLA Ops:
  6.5 2.0 copy.77.x_ref
  8.6 54.9 %shard_map.118 = bf16[8,2048,96]{2,1,0:T(8,128)(2,1)} custom-call(bf16[2048,96]{1,0:T(8,128)(2,1)} %copy.77.x_ref), custom_call_target="tpu_custom_call" | custom-call | tf_op jit(solution)/shard_map/pallas_call | solution.py:145
  63.6 3.6 %fusion.6 = bf16[2048,64]{0,1:T(8,128)(2,1)S(1)} fusion(bf16[8,2048,96]{2,1,0:T(8,128)(2,1)} %shard_map.118, bf16[8,96,64]{1,0,2:T(8,128)(2,1)S(1)} %reshape.54), kind=kOutput, calls=%fused_computation.11 | convolution fusion | flops 201457664 | bytes 3506176 | tf_op jit(solution)/shard_map/jrc,jcd->rd/dot_general | solution.py:184
  67.2 0.3 copy.83
  67.7 3.6 %fusion.7 = bf16[2048,64]{0,1:T(8,128)(2,1)S(1)} fusion(bf16[8,2048,96]{2,1,0:T(8,128)(2,1)} %shard_map.118, bf16[8,96,64]{1,0,2:T(8,128)(2,1)S(1)} %reshape.55), kind=kOutput, calls=%fused_computation.12 | convolution fusion | flops 201457664 | bytes 3506176 | tf_op jit(solution)/shard_map/jrc,jcd->rd/dot_general | solution.py:184
  71.4 0.3 copy.84
  71.7 1.2 pad_maximum_fusion.1
  73.1 52.6 %all-gather.5.cloned.1.call-done.kv_ref = bf16[32768,128]{1,0:T(8,128)(2,1)} async-done(((bf16[2048,128]{1,0:T(8,128)(2,1)}), bf16[32768,128]{1,0:T(8,128)(2,1)}) %all-gather.5.cloned.1.call-update) | async-done | bytes 8388624 | tf_op jit(solution)/shard_map/all_gather | solution.py:194
  125.7 0.7 all-gather.9.cloned.1.call-update
  126.6 3.6 %fusion.8 = bf16[2048,64]{0,1:T(8,128)(2,1)S(1)} fusion(bf16[8,2048,96]{2,1,0:T(8,128)(2,1)} %shard_map.118, bf16[8,96,64]{1,0,2:T(8,128)(2,1)S(1)} %reshape.57), kind=kOutput, calls=%fused_computation.13 | convolution fusion | flops 201457664 | bytes 3506176 | tf_op jit(solution)/shard_map/jrc,jcd->rd/dot_general | solution.py:184
  130.2 0.3 copy.89
  130.5 0.9 concatenate.14.q_ref
  131.4 108.8 %shard_map.119 = bf16[2048,64]{1,0:T(8,128)(2,1)} custom-call(bf16[2048,128]{1,0:T(8,128)(2,1)} %concatenate.14.q_ref, bf16[32768,128]{1,0:T(8,128)(2,1)} %all-gather.5.cloned.1.call-done.kv_ref), custom_call_target="tpu_custom_call" | custom-call | flops 34359738368 | bytes 17563648 | tf_op jit(solution)/shard_map/pallas_call | solution.py:75
  240.2 1.2 copy.90
  241.5 6.6 %copy_bitcast_fusion = bf16[256,128,96]{1,2,0:T(8,128)(2,1)} fusion(bf16[32768,96]{0,1:T(8,128)(2,1)} %all-gather.7.cloned.1.call-done), kind=kLoop, calls=%fused_computation.1 | loop fusion | bytes 12582912 | tf_op jit(solution)/shard_map/reshape | solution.py:21
  248.0 3.6 %gather_fusion = bf16[64,128,96]{1,2,0:T(8,128)(2,1)S(1)} fusion(bf16[256,128,96]{1,2,0:T(8,128)(2,1)} %copy_bitcast_fusion, s32[1024]{0:T(1024)S(1)} %pad_clamp_fusion), kind=kCustom, calls=%fused_computation | custom fusion | bytes 3145984 | tf_op jit(solution)/shard_map/jit(_take)/gather | solution.py:22
  251.7 3.9 %fusion.11 = f32[64,128,96]{1,2,0:T(8,128)S(1)} fusion(s32[64,128,128]{2,1,0:T(8,128)} %param.15, bf16[64,128,96]{1,2,0:T(8,128)(2,1)S(1)} %gather_fusion, pred[64]{0:T(512)(128)(4,1)S(1)} %get-tuple-element.13), kind=kOutput, calls=%fused_computation.16 | convolution fusion | flops 203161600 | bytes 8912960 | tf_op jit(solution)/shard_map/ers,esf->erf/dot_general | solution.py:23
  255.6 2.9 fusion.26
  258.5 0.3 fusion.48
  258.9 0.9 copy.129
  259.7 6.8 %all-to-all-start = ((bf16[8,256,160]{1,2,0:T(8,128)(2,1)}), bf16[8,256,160]{1,2,0:T(8,128)(2,1)}, u32[]{:S(2)}, u32[]{:S(2)}) async-start(bf16[8,256,160]{1,2,0:T(8,128)(2,1)} %bitcast.89), calls=%async_computation | async-start | bytes 1310720 | tf_op jit(solution)/shard_map/all_to_all | solution.py:214
  266.5 1.1 convert_bitcast_fusion
  267.6 0.3 copy.78
  267.9 0.3 copy.93
  268.2 15.1 %all-gather.9.cloned.1.call-done = bf16[5120,768]{1,0:T(8,128)(2,1)} async-done(((bf16[640,768]{1,0:T(8,128)(2,1)}), bf16[5120,768]{1,0:T(8,128)(2,1)}) %all-gather.9.cloned.1.call-update) | async-done | bytes 7864336 | tf_op jit(solution)/shard_map/all_gather | solution.py:200
  283.3 1.3 slice.31
  284.6 1.7 reshape.59
  286.4 1.6 convolution_bitcast_fusion.3
  288.0 3.8 %fusion.70 = (f32[256]{0:T(256)S(1)}, f32[256]{0:T(256)S(1)}, f32[256,768]{1,0:T(8,128)}) fusion(f32[256,768]{1,0:T(8,128)S(1)} %convolution_bitcast_fusion.3, f32[256,768]{1,0:T(8,128)S(1)} %copy.93, bf16[8,640,768]{2,1,0:T(8,128)(2,1)} %bitcast.97, bf16[8,96,8,96]{3,2,1,0:T(8,128)(2,1)S(1)} %reshape.59, bf16[8,256,160]{1,2,0:T(8,128)(2,1)} %all-to-all-done), kind=kOutput, calls=%fused_computation.71 | convolution fusion | flops 605355520 | bytes 5113856 | tf_op jit(solution)/shard_map/rjc,jce->re/dot_general | solution.py:232
  291.8 5.3 %fusion.37 = bf16[256,768]{1,0:T(8,128)(2,1)S(1)} fusion(f32[256,768]{1,0:T(8,128)} %get-tuple-element.17, bf16[8,640,768]{2,1,0:T(8,128)(2,1)} %bitcast.98, f32[256]{0:T(256)S(1)} %get-tuple-element.16, f32[256]{0:T(256)S(1)} %get-tuple-element.15), kind=kOutput, calls=%fused_computation.31 | convolution fusion | flops 1209729024 | bytes 6686720 | tf_op jit(solution)/shard_map/rjc,jce->re/dot_general | solution.py:245
  297.3 12.6 %all_to_all.10 = bf16[8,256,96]{1,2,0:T(8,128)(2,1)S(1)} all-to-all(bf16[8,256,96]{1,2,0:T(8,128)(2,1)S(1)} %bitcast.93), channel_id=1, replica_groups=mesh['blk'=16,'mp'=8] {'mp'}, dimensions={0} | all-to-all | bytes 786432 | tf_op jit(solution)/shard_map/all_to_all | solution.py:248
  309.9 0.8 copy.102
  (45 shorter events, 1.0 us)
Async XLA Ops:
  6.5 56.9 %copy-start.6 = (bf16[768,64]{0,1:T(8,128)(2,1)S(1)}, bf16[768,64]{0,1:T(8,128)(2,1)}, u32[]{:S(2)}) copy-start(bf16[768,64]{0,1:T(8,128)(2,1)} %param.19) | copy-start | bytes 294916
  6.5 119.1 %all-gather.5.cloned.1.call-start = ((), (), s32[]{:S(2)}) async-start(), calls=%async_computation.2 | async-start | bytes 8912896 | tf_op jit(solution)/shard_map/all_gather | solution.py:194
  63.6 3.9 %copy-start.7 = (bf16[768,64]{0,1:T(8,128)(2,1)S(1)}, bf16[768,64]{0,1:T(8,128)(2,1)}, u32[]{:S(2)}) copy-start(bf16[768,64]{0,1:T(8,128)(2,1)} %param.20) | copy-start | bytes 294916
  67.7 5.2 %copy-start.4 = (bf16[768,96]{0,1:T(8,128)(2,1)S(1)}, bf16[768,96]{0,1:T(8,128)(2,1)}, u32[]{:S(2)}) copy-start(bf16[768,96]{0,1:T(8,128)(2,1)} %param.16) | copy-start | bytes 442372
  71.3 1.6 copy-start.2
  71.3 1.6 copy-start.5
  71.3 1.6 copy-start.9
  71.3 1.7 copy-start.3
  71.4 55.1 %copy-start.8 = (bf16[768,64]{0,1:T(8,128)(2,1)S(1)}, bf16[768,64]{0,1:T(8,128)(2,1)}, u32[]{:S(2)}) copy-start(bf16[768,64]{0,1:T(8,128)(2,1)} %param.18) | copy-start | bytes 294916
  72.8 168.6 %all-gather.7.cloned.1.call-start = ((), (), s32[]{:S(2)}) async-start(), calls=%async_computation.3 | async-start | bytes 6684672 | tf_op jit(solution)/shard_map/all_gather | solution.py:199
  73.0 52.7 %copy-start.1 = (bf16[640,768]{1,0:T(8,128)(2,1)}, bf16[640,768]{1,0:T(8,128)(2,1)S(1)}, u32[]{:S(2)}) copy-start(bf16[640,768]{1,0:T(8,128)(2,1)S(1)} %constant_dynamic-update-slice_fusion) | copy-start | bytes 2949124
  125.7 157.6 %all-gather.9.cloned.1.call-start = ((), (), s32[]{:S(2)}) async-start(), calls=%async_computation.4 | async-start | bytes 8847360 | tf_op jit(solution)/shard_map/all_gather | solution.py:200
  126.6 4.8 %copy-start.11 = (s32[64]{0:T(128)S(1)}, s32[64]{0:T(128)}, u32[]{:S(2)}) copy-start(s32[64]{0:T(128)} %param.14) | copy-start | bytes 772
  251.7 3.9 %copy-start.10 = (s32[64]{0:T(128)S(1)}, s32[64]{0:T(128)}, u32[]{:S(2)}) copy-start(s32[64]{0:T(128)} %param.13) | copy-start | bytes 772
  255.6 2.9 copy-start
  259.7 26.6 %all-to-all-start = ((bf16[8,256,160]{1,2,0:T(8,128)(2,1)}), bf16[8,256,160]{1,2,0:T(8,128)(2,1)}, u32[]{:S(2)}, u32[]{:S(2)}) async-start(bf16[8,256,160]{1,2,0:T(8,128)(2,1)} %bitcast.89), calls=%async_computation | async-start | bytes 1310720 | tf_op jit(solution)/shard_map/all_to_all | solution.py:214
Sparse Core Ops, SparseCore 0:
  73.0 52.6 all-gather.4
  127.3 43.1 all-gather.6
  172.8 110.4 all-gather.8

commit v11 on v10

--- a/solution.py
+++ b/solution.py
@@ -195,17 +195,23 @@
 
     pieces = (gin_in.T, ffn_in.T, gin_out, w_attn_out, ffn_out)
     packed_weights = jnp.concatenate(pieces, axis=0)
-    kv_all, packed_weights, late_features = lax.optimization_barrier((kv_all, packed_weights, features))
+    packed_weights, _ = lax.optimization_barrier((packed_weights, feature_parts))
+    by_offset = [packed_weights] + [
+        lax.ppermute(packed_weights, "mp", [(i, (i + k) % n_mp) for i in range(n_mp)])
+        for k in range(1, n_mp)
+    ]
+    kv_all, late_features = lax.optimization_barrier((kv_all, features))
     all_features = lax.all_gather(late_features, "blk", axis=0, tiled=True)
-    weight_parts = lax.all_gather(packed_weights, "mp", axis=0, tiled=False)
+    attended = flash_attention(queries, kv_all, 0, heads)
+    attended, by_offset = lax.optimization_barrier((attended, by_offset))
+    source_order = (me - jnp.arange(n_mp, dtype=jnp.int32)) % n_mp
+    weight_parts = jnp.take(jnp.stack(by_offset), source_order, axis=0)
     unpacked = []
     offset = 0
     for x in pieces:
         unpacked.append(weight_parts[:, offset : offset + x.shape[0], :])
         offset += x.shape[0]
     gin_in_t, ffn_in_t, gin_out_parts, attn_out_parts, ffn_out_parts = unpacked
-
-    attended = flash_attention(queries, kv_all, 0, heads)
 
     gathered = neighbour_sum(features, edge_dst, edge_src, edge_mask, all_features)
     local_share = (features.astype(jnp.float32) + gathered * 0.25).astype(jnp.bfloat16)

time: 318 us -> 418 us (1.31)
  starting transfers between devices: 6.84 us -> 63 us
  local copies, waits for them, and re-layouts: 21.3 us -> 49.9 us
  waiting for transfers between devices: 68.4 us -> 80.2 us
    ppermute x0 -> x7, starting transfers between devices: none -> 57.9 us  [per_device(): lax.ppermute(packed_weights, 'mp', [(i, (i + k) % n_mp) for i in range(n_...]
    ppermute x0 -> x7, waiting for transfers between devices: none -> 25.2 us  [per_device(): lax.ppermute(packed_weights, 'mp', [(i, (i + k) % n_mp) for i in range(n_...]
    unnamed x29 -> x36, local copies, waits for them, and re-layouts: 2.16 us -> 18.4 us
    all_gather x1 -> x0, waiting for transfers between devices: 15.1 us -> none  [per_device(): weight_parts = lax.all_gather(packed_weights, 'mp', axis=0, tiled=False)]
    gather x0 -> x1, local copies, waits for them, and re-layouts: none -> 7.68 us  [per_device(): weight_parts = jnp.take(jnp.stack(by_offset), source_order, axis=0)]
  transfers between devices with their start and end apart: 4 -> 10, of which waited for: 2 -> 3; matrix products, arithmetic and copies ran while one was open for 9% -> 9% of each run, Pallas kernels for 34% -> 26%
where the time goes in v11:
time: 418 us; the launch traced here: 417 us
  Pallas kernels  164 us (39%)
  waiting for transfers between devices  80.2 us (19%)
  starting transfers between devices  63 us (15%)
  local copies, waits for them, and re-layouts  49.9 us (12%)
  matrix products  25.4 us (6%)
  blocking collectives  14.4 us (3%)
  between operations  13.8 us (3%)
  other arithmetic  6.85 us (2%)
    pallas_call x1, Pallas kernels, flash_attention(): pl.pallas_call(functools.partial(flash_kernel, dim), grid=grid, in_specs=...  109 us
    ppermute x7, starting transfers between devices, per_device(): lax.ppermute(packed_weights, 'mp', [(i, (i + k) % n_mp) for i in range(n_...  57.9 us
    pallas_call x1, Pallas kernels, dma_exchange(): pl.pallas_call(functools.partial(exchange_kernel, axis, n, scatter), in_s...  54.9 us
    all_gather x1, waiting for transfers between devices, per_device(): lax.all_gather(jnp.concatenate([keys, values], axis=1), 'blk', axis=0, ti...  52.8 us
    ppermute x7, waiting for transfers between devices, per_device(): lax.ppermute(packed_weights, 'mp', [(i, (i + k) % n_mp) for i in range(n_...  25.2 us
    unnamed x36, local copies, waits for them, and re-layouts  18.4 us
    all_to_all x1, blocking collectives, per_device(): lax.all_to_all(out_parts, 'mp', 0, 0, tiled=False).reshape(rows, cols)  14.4 us
    dot_general x3, matrix products, project(): jnp.einsum('jrc,jcd->rd', feature_parts, w.reshape(n_mp, cols, w.shape[1]...  8.65 us
  transfers between devices with their start and end apart: 10, of which 3 were waited for; matrix products, arithmetic and copies ran while one was open for 9% of the time, Pallas kernels for 26%

profile of v11, /device:TPU:0, one launch (start us, length us, event | category | flops | bytes accessed | tf_op | source)
XLA Modules:
  0.0 417.1 jit_solution(8512900594132582130)
XLA Ops:
  8.7 2.0 copy.77.x_ref
  10.7 54.9 %shard_map.118 = bf16[8,2048,96]{2,1,0:T(8,128)(2,1)} custom-call(bf16[2048,96]{1,0:T(8,128)(2,1)} %copy.77.x_ref), custom_call_target="tpu_custom_call" | custom-call | tf_op jit(solution)/shard_map/pallas_call | solution.py:145
  65.6 3.7 fusion.7
  69.3 1.4 fusion.6
  72.5 52.8 %all-gather.3.cloned.1.call-done.kv_ref = bf16[32768,128]{1,0:T(8,128)(2,1)} async-done(((bf16[2048,128]{1,0:T(8,128)(2,1)}), bf16[32768,128]{1,0:T(8,128)(2,1)}) %all-gather.3.cloned.1.call-update) | async-done | bytes 8388624 | tf_op jit(solution)/shard_map/all_gather | solution.py:194
  125.5 5.4 %collective-permute-start.6 = (bf16[640,768]{1,0:T(8,128)(2,1)S(1)}, bf16[640,768]{1,0:T(8,128)(2,1)}, u32[]{:S(2)}, u32[]{:S(2)}) collective-permute-start(bf16[640,768]{1,0:T(8,128)(2,1)S(1)} %constant_dynamic-update-slice_fusion), channel_id=1, source_target_pairs={{0,7},{1,0},{2,1},{3,2},{4,3},{5,4},{6,5},{7,6},{8,15},{9,8},{10,9... | collective-permute-start | bytes 2949128 | tf_op jit(solution)/shard_map/ppermute | solution.py:200
  132.1 2.9 collective-permute-start.3
  138.9 3.6 fusion.8
  143.9 25.1 %collective-permute-done.6 = bf16[640,768]{1,0:T(8,128)(2,1)} collective-permute-done((bf16[640,768]{1,0:T(8,128)(2,1)S(1)}, bf16[640,768]{1,0:T(8,128)(2,1)}, u32[]{:S(2)}, u32[]{:S(2)}) %collective-permute-start.6) | collective-permute-done | bytes 983072 | tf_op jit(solution)/shard_map/ppermute | solution.py:200
  169.0 47.3 %collective-permute-start = (bf16[640,768]{1,0:T(8,128)(2,1)S(1)}, bf16[640,768]{1,0:T(8,128)(2,1)}, u32[]{:S(2)}, u32[]{:S(2)}) collective-permute-start(bf16[640,768]{1,0:T(8,128)(2,1)S(1)} %constant_dynamic-update-slice_fusion), channel_id=1, source_target_pairs={{0,1},{1,2},{2,3},{3,4},{4,5},{5,6},{6,7},{7,0},{8,9},{9,10},{10,1... | collective-permute-start | bytes 2949128 | tf_op jit(solution)/shard_map/ppermute | solution.py:200
  216.4 108.7 %shard_map.119 = bf16[2048,64]{1,0:T(8,128)(2,1)} custom-call(bf16[2048,128]{1,0:T(8,128)(2,1)} %concatenate.13.q_ref, bf16[32768,128]{1,0:T(8,128)(2,1)} %all-gather.3.cloned.1.call-done.kv_ref), custom_call_target="tpu_custom_call" | custom-call | flops 34359738368 | bytes 17563648 | tf_op jit(solution)/shard_map/pallas_call | solution.py:75
  325.1 1.2 copy.90
  327.5 2.2 bitcast_dynamic-update-slice_fusion.6
  330.7 2.2 bitcast_dynamic-update-slice_fusion.4
  332.9 2.2 bitcast_dynamic-update-slice_fusion.3
  335.1 2.2 bitcast_dynamic-update-slice_fusion.2
  337.4 2.2 bitcast_dynamic-update-slice_fusion.1
  339.6 2.2 bitcast_dynamic-update-slice_fusion
  341.8 7.7 %gather_fusion.1 = bf16[8,640,768]{2,1,0:T(8,128)(2,1)} fusion(bf16[8,640,768]{2,1,0:T(8,128)(2,1)} %bitcast_dynamic-update-slice_fusion, s32[1024]{0:T(1024)S(1)} %pad_clamp_fusion), kind=kCustom, calls=%fused_computation.1 | custom fusion | bytes 15728672 | tf_op jit(solution)/shard_map/jit(_take)/gather | solution.py:208
  349.5 6.6 %copy_bitcast_fusion = bf16[256,128,96]{1,2,0:T(8,128)(2,1)} fusion(bf16[32768,96]{0,1:T(8,128)(2,1)} %all-gather.5.cloned.1.call-done), kind=kLoop, calls=%fused_computation.3 | loop fusion | bytes 12582912 | tf_op jit(solution)/shard_map/reshape | solution.py:21
  356.1 3.6 gather_fusion
  359.7 3.8 fusion.11
  363.6 2.9 fusion.26
  367.8 5.1 %all-to-all-start = ((bf16[8,256,160]{1,2,0:T(8,128)(2,1)}), bf16[8,256,160]{1,2,0:T(8,128)(2,1)}, u32[]{:S(2)}, u32[]{:S(2)}) async-start(bf16[8,256,160]{1,2,0:T(8,128)(2,1)} %bitcast.106), calls=%async_computation | async-start | bytes 1310720 | tf_op jit(solution)/shard_map/all_to_all | solution.py:220
  372.9 4.1 broadcast_select_fusion
  376.9 3.0 copy-done.1
  380.0 2.6 reshape.113
  382.7 2.3 all-to-all-done
  384.9 1.6 convolution_bitcast_fusion.3
  386.6 3.5 fusion.73
  390.1 4.9 %fusion.37 = bf16[256,768]{1,0:T(8,128)(2,1)S(1)} fusion(f32[256,768]{1,0:T(8,128)S(1)} %get-tuple-element.35, bf16[8,640,768]{2,1,0:T(8,128)(2,1)} %copy-done.1, f32[256]{0:T(256)S(1)} %get-tuple-element.34, f32[256]{0:T(256)S(1)} %get-tuple-element.33), kind=kOutput, calls=%fused_computation.33 | convolution fusion | flops 1209729024 | bytes 6686720 | tf_op jit(solution)/shard_map/rjc,jce->re/dot_general | solution.py:251
  395.2 14.4 %all_to_all.10 = bf16[8,256,96]{1,2,0:T(8,128)(2,1)S(1)} all-to-all(bf16[8,256,96]{1,2,0:T(8,128)(2,1)S(1)} %bitcast.110), channel_id=1, replica_groups=mesh['blk'=16,'mp'=8] {'mp'}, dimensions={0} | all-to-all | bytes 786432 | tf_op jit(solution)/shard_map/all_to_all | solution.py:254
  (69 shorter events, 14.9 us)
Async XLA Ops:
  6.5 118.8 %all-gather.3.cloned.1.call-start = ((), (), s32[]{:S(2)}) async-start(), calls=%async_computation.2 | async-start | bytes 8912896 | tf_op jit(solution)/shard_map/all_gather | solution.py:194
  65.5 3.7 copy-start
  69.3 56.0 %copy-start.6 = (bf16[768,96]{0,1:T(8,128)(2,1)S(1)}, bf16[768,96]{0,1:T(8,128)(2,1)}, u32[]{:S(2)}) copy-start(bf16[768,96]{0,1:T(8,128)(2,1)} %param.16) | copy-start | bytes 442372
  69.3 56.0 %copy-start.4 = (bf16[768,192]{0,1:T(8,128)(2,1)S(1)}, bf16[768,192]{0,1:T(8,128)(2,1)}, u32[]{:S(2)}) copy-start(bf16[768,192]{0,1:T(8,128)(2,1)} %param.22) | copy-start | bytes 884740
  69.3 56.1 %copy-start.7 = (bf16[96,768]{1,0:T(8,128)(2,1)S(1)}, bf16[96,768]{1,0:T(8,128)(2,1)}, u32[]{:S(2)}) copy-start(bf16[96,768]{1,0:T(8,128)(2,1)} %param.17) | copy-start | bytes 442372
  70.7 54.7 %copy-start.9 = (bf16[64,768]{1,0:T(8,128)(2,1)S(1)}, bf16[64,768]{1,0:T(8,128)(2,1)}, u32[]{:S(2)}) copy-start(bf16[64,768]{1,0:T(8,128)(2,1)} %param.21) | copy-start | bytes 294916
  70.7 54.7 %copy-start.5 = (bf16[192,768]{1,0:T(8,128)(2,1)S(1)}, bf16[192,768]{1,0:T(8,128)(2,1)}, u32[]{:S(2)}) copy-start(bf16[192,768]{1,0:T(8,128)(2,1)} %param.23) | copy-start | bytes 884740
  70.7 65.3 %copy-start.8 = (bf16[768,64]{0,1:T(8,128)(2,1)S(1)}, bf16[768,64]{0,1:T(8,128)(2,1)}, u32[]{:S(2)}) copy-start(bf16[768,64]{0,1:T(8,128)(2,1)} %param.18) | copy-start | bytes 294916
  72.5 277.1 %all-gather.5.cloned.1.call-start = ((), (), s32[]{:S(2)}) async-start(), calls=%async_computation.3 | async-start | bytes 6684672 | tf_op jit(solution)/shard_map/all_gather | solution.py:204
  125.5 43.6 %collective-permute-start.6 = (bf16[640,768]{1,0:T(8,128)(2,1)S(1)}, bf16[640,768]{1,0:T(8,128)(2,1)}, u32[]{:S(2)}, u32[]{:S(2)}) collective-permute-start(bf16[640,768]{1,0:T(8,128)(2,1)S(1)} %constant_dynamic-update-slice_fusion), channel_id=1, source_target_pairs={{0,7},{1,0},{2,1},{3,2},{4,3},{5,4},{6,5},{7,6},{8,15},{9,8},{10,9... | collective-permute-start | bytes 2949128 | tf_op jit(solution)/shard_map/ppermute | solution.py:200
  130.9 38.2 %collective-permute-start.5 = (bf16[640,768]{1,0:T(8,128)(2,1)S(1)}, bf16[640,768]{1,0:T(8,128)(2,1)}, u32[]{:S(2)}, u32[]{:S(2)}) collective-permute-start(bf16[640,768]{1,0:T(8,128)(2,1)S(1)} %constant_dynamic-update-slice_fusion), channel_id=1, source_target_pairs={{0,6},{1,7},{2,0},{3,1},{4,2},{5,3},{6,4},{7,5},{8,14},{9,15},{10,... | collective-permute-start | bytes 2949128 | tf_op jit(solution)/shard_map/ppermute | solution.py:200
  131.6 193.5 %collective-permute-start.4 = (bf16[640,768]{1,0:T(8,128)(2,1)S(1)}, bf16[640,768]{1,0:T(8,128)(2,1)}, u32[]{:S(2)}, u32[]{:S(2)}) collective-permute-start(bf16[640,768]{1,0:T(8,128)(2,1)S(1)} %constant_dynamic-update-slice_fusion), channel_id=1, source_target_pairs={{0,5},{1,6},{2,7},{3,0},{4,1},{5,2},{6,3},{7,4},{8,13},{9,14},{10,... | collective-permute-start | bytes 2949128 | tf_op jit(solution)/shard_map/ppermute | solution.py:200
  132.1 193.0 %collective-permute-start.3 = (bf16[640,768]{1,0:T(8,128)(2,1)S(1)}, bf16[640,768]{1,0:T(8,128)(2,1)}, u32[]{:S(2)}, u32[]{:S(2)}) collective-permute-start(bf16[640,768]{1,0:T(8,128)(2,1)S(1)} %constant_dynamic-update-slice_fusion), channel_id=1, source_target_pairs={{0,4},{1,5},{2,6},{3,7},{4,0},{5,1},{6,2},{7,3},{8,12},{9,13},{10,... | collective-permute-start | bytes 2949128 | tf_op jit(solution)/shard_map/ppermute | solution.py:200
  135.0 190.1 %collective-permute-start.2 = (bf16[640,768]{1,0:T(8,128)(2,1)S(1)}, bf16[640,768]{1,0:T(8,128)(2,1)}, u32[]{:S(2)}, u32[]{:S(2)}) collective-permute-start(bf16[640,768]{1,0:T(8,128)(2,1)S(1)} %constant_dynamic-update-slice_fusion), channel_id=1, source_target_pairs={{0,3},{1,4},{2,5},{3,6},{4,7},{5,0},{6,1},{7,2},{8,11},{9,12},{10,... | collective-permute-start | bytes 2949128 | tf_op jit(solution)/shard_map/ppermute | solution.py:200
  138.9 4.9 %copy-start.11 = (s32[64]{0:T(128)S(1)}, s32[64]{0:T(128)}, u32[]{:S(2)}) copy-start(s32[64]{0:T(128)} %param.14) | copy-start | bytes 772
  169.0 156.1 %collective-permute-start.1 = (bf16[640,768]{1,0:T(8,128)(2,1)S(1)}, bf16[640,768]{1,0:T(8,128)(2,1)S(1)}, u32[]{:S(2)}, u32[]{:S(2)}) collective-permute-start(bf16[640,768]{1,0:T(8,128)(2,1)S(1)} %constant_dynamic-update-slice_fusion), channel_id=1, source_target_pairs={{0,2},{1,3},{2,4},{3,5},{4,6},{5,7},{6,0},{7,1},{8,10},{9,11},{10,... | collective-permute-start | bytes 2949128 | tf_op jit(solution)/shard_map/ppermute | solution.py:200
  169.0 156.1 %collective-permute-start = (bf16[640,768]{1,0:T(8,128)(2,1)S(1)}, bf16[640,768]{1,0:T(8,128)(2,1)}, u32[]{:S(2)}, u32[]{:S(2)}) collective-permute-start(bf16[640,768]{1,0:T(8,128)(2,1)S(1)} %constant_dynamic-update-slice_fusion), channel_id=1, source_target_pairs={{0,1},{1,2},{2,3},{3,4},{4,5},{5,6},{6,7},{7,0},{8,9},{9,10},{10,1... | collective-permute-start | bytes 2949128 | tf_op jit(solution)/shard_map/ppermute | solution.py:200
  359.7 3.8 copy-start.10
  363.6 2.9 copy-start.2
  367.8 17.2 %all-to-all-start = ((bf16[8,256,160]{1,2,0:T(8,128)(2,1)}), bf16[8,256,160]{1,2,0:T(8,128)(2,1)}, u32[]{:S(2)}, u32[]{:S(2)}) async-start(bf16[8,256,160]{1,2,0:T(8,128)(2,1)} %bitcast.106), calls=%async_computation | async-start | bytes 1310720 | tf_op jit(solution)/shard_map/all_to_all | solution.py:220
  376.9 3.0 copy-start.1
  380.0 6.6 %copy-start.3 = (f32[256,768]{1,0:T(8,128)S(1)}, f32[256,768]{1,0:T(8,128)}, u32[]{:S(2)}) copy-start(f32[256,768]{1,0:T(8,128)} %copy.93) | copy-start | bytes 2359300
Sparse Core Ops, SparseCore 0:
  72.6 52.6 all-gather.2
  126.9 72.7 all-gather.4

commit v12 on v9

--- a/solution.py
+++ b/solution.py
@@ -188,10 +188,9 @@
             preferred_element_type=jnp.float32,
         ).astype(jnp.bfloat16)
 
-    queries = project(w_query) * jnp.bfloat16(scale)
-    keys = project(w_key)
-    values = project(w_value)
-    kv_all = lax.all_gather(jnp.concatenate([keys, values], axis=1), "blk", axis=0, tiled=True)
+    projected = project(jnp.concatenate([w_query, w_key, w_value], axis=1))
+    queries = projected[:, : HEAD_DIM * heads] * jnp.bfloat16(scale)
+    kv_all = lax.all_gather(projected[:, HEAD_DIM * heads :], "blk", axis=0, tiled=True)
 
     pieces = (gin_in.T, ffn_in.T, gin_out, w_attn_out, ffn_out)
     packed_weights = jnp.concatenate(pieces, axis=0)

time: 315 us -> 314 us (level)
  matrix products: 28.2 us -> 21.2 us
  waiting for transfers between devices: 61.8 us -> 66.1 us
    all_gather x1, waiting for transfers between devices: 4.96 us -> 14.7 us  [per_device(): weight_parts = lax.all_gather(packed_weights, 'mp', axis=0, tiled=False)]
    dot_general x3 -> x1, matrix products: 10.8 us -> 3.73 us  [project(): jnp.einsum('jrc,jcd->rd', feature_parts, w.reshape(n_mp, cols, w.shape[1]...]
    all_to_all x1, waiting for transfers between devices: 3.73 us -> 0.01 us  [per_device(): received = lax.all_to_all(mixed_in, 'mp', 0, 0, tiled=False)]
  transfers between devices with their start and end apart: 4 -> 4, of which waited for: 3 -> 2; matrix products, arithmetic and copies ran while one was open for 9% -> 9% of each run, Pallas kernels for 36% -> 36%
where the time goes in v12:
time: 314 us
  Pallas kernels  167 us (53%)
  waiting for transfers between devices  66.1 us (21%)
  local copies, waits for them, and re-layouts  23.7 us (8%)
  matrix products  21.2 us (7%)
  between operations  13.4 us (4%)
  blocking collectives  12.5 us (4%)
  starting transfers between devices  7.07 us (2%)
    pallas_call x1, Pallas kernels, flash_attention(): pl.pallas_call(functools.partial(flash_kernel, dim), grid=grid, in_specs=...  113 us
    pallas_call x1, Pallas kernels, dma_exchange(): pl.pallas_call(functools.partial(exchange_kernel, axis, n, scatter), in_s...  54 us
    all_gather x1, waiting for transfers between devices, per_device(): lax.all_gather(projected[:, HEAD_DIM * heads:], 'blk', axis=0, tiled=True)  50.8 us
    all_gather x1, waiting for transfers between devices, per_device(): weight_parts = lax.all_gather(packed_weights, 'mp', axis=0, tiled=False)  14.7 us
    all_to_all x1, blocking collectives, per_device(): lax.all_to_all(out_parts, 'mp', 0, 0, tiled=False).reshape(rows, cols)  12.5 us
    all_to_all x1, starting transfers between devices, per_device(): received = lax.all_to_all(mixed_in, 'mp', 0, 0, tiled=False)  6.81 us
    reshape x1, local copies, waits for them, and re-layouts, neighbour_sum(): blocks = all_features.reshape(count, BLOCK, cols)  6.53 us
  transfers between devices with their start and end apart: 4, of which 2 were waited for; matrix products, arithmetic and copies ran while one was open for 9% of the time, Pallas kernels for 36%

profile of v12, /device:TPU:0, one launch (start us, length us, event | category | flops | bytes accessed | tf_op | source)
XLA Modules:
  0.0 313.7 jit_solution(11941538611932857663)
XLA Ops:
  6.5 1.0 pad_maximum_fusion.1
  7.5 0.4 reshape.48
  8.0 2.0 copy.52.x_ref
  10.0 54.0 %shard_map.118 = bf16[8,2048,96]{2,1,0:T(8,128)(2,1)} custom-call(bf16[2048,96]{1,0:T(8,128)(2,1)} %copy.52.x_ref), custom_call_target="tpu_custom_call" | custom-call | tf_op jit(solution)/shard_map/pallas_call | solution.py:145
  64.1 3.7 %fusion.2 = bf16[192,2048]{1,0:T(8,128)(2,1)S(1)} fusion(bf16[8,2048,96]{2,1,0:T(8,128)(2,1)} %shard_map.118, bf16[8,96,192]{1,0,2:T(8,128)(2,1)S(1)} %reshape.48), kind=kOutput, calls=%fused_computation.5 | convolution fusion | flops 604372992 | bytes 4227072 | tf_op jit(solution)/shard_map/jrc,jcd->rd/dot_general | solution.py:184
  67.8 0.5 copy.56
  68.3 1.1 slice.38
  69.5 0.9 constant_dynamic-update-slice_fusion.2
  70.5 0.9 constant_dynamic-update-slice_fusion.1
  71.4 50.8 %all-gather.5.cloned.1.call-done.kv_ref = bf16[32768,128]{1,0:T(8,128)(2,1)} async-done(((bf16[2048,128]{1,0:T(8,128)(2,1)}), bf16[32768,128]{1,0:T(8,128)(2,1)}) %all-gather.5.cloned.1.call-update) | async-done | bytes 8388624 | tf_op jit(solution)/shard_map/all_gather | solution.py:193
  122.5 0.5 all-gather.9.cloned.1.call-update
  123.1 0.9 concatenate.14.q_ref
  124.0 113.1 %shard_map.119 = bf16[2048,64]{1,0:T(8,128)(2,1)} custom-call(bf16[2048,128]{1,0:T(8,128)(2,1)} %concatenate.14.q_ref, bf16[32768,128]{1,0:T(8,128)(2,1)} %all-gather.5.cloned.1.call-done.kv_ref), custom_call_target="tpu_custom_call" | custom-call | flops 34359738368 | bytes 34340864 | tf_op jit(solution)/shard_map/pallas_call | solution.py:75
  237.1 1.2 copy.59
  238.4 6.5 %copy_bitcast_fusion = bf16[256,128,96]{1,2,0:T(8,128)(2,1)} fusion(bf16[32768,96]{0,1:T(8,128)(2,1)} %all-gather.7.cloned.1.call-done), kind=kLoop, calls=%fused_computation.1 | loop fusion | bytes 12582912 | tf_op jit(solution)/shard_map/reshape | solution.py:21
  244.9 3.6 %gather_fusion = bf16[64,128,96]{1,2,0:T(8,128)(2,1)S(1)} fusion(bf16[256,128,96]{1,2,0:T(8,128)(2,1)} %copy_bitcast_fusion, s32[1024]{0:T(1024)S(1)} %pad_clamp_fusion), kind=kCustom, calls=%fused_computation | custom fusion | bytes 3145984 | tf_op jit(solution)/shard_map/jit(_take)/gather | solution.py:22
  248.5 3.8 %fusion.9 = f32[64,128,96]{1,2,0:T(8,128)S(1)} fusion(s32[64,128,128]{2,1,0:T(8,128)} %param.15, bf16[64,128,96]{1,2,0:T(8,128)(2,1)S(1)} %gather_fusion, pred[64]{0:T(512)(128)(4,1)S(1)} %get-tuple-element.13), kind=kOutput, calls=%fused_computation.12 | convolution fusion | flops 203161600 | bytes 8912960 | tf_op jit(solution)/shard_map/ers,esf->erf/dot_general | solution.py:23
  252.4 2.9 fusion.24
  255.3 0.3 fusion.46
  255.7 0.9 copy.92
  256.6 6.8 %all-to-all-start = ((bf16[8,256,160]{1,2,0:T(8,128)(2,1)}), bf16[8,256,160]{1,2,0:T(8,128)(2,1)}, u32[]{:S(2)}, u32[]{:S(2)}) async-start(bf16[8,256,160]{1,2,0:T(8,128)(2,1)} %bitcast.76), calls=%async_computation | async-start | bytes 1310720 | tf_op jit(solution)/shard_map/all_to_all | solution.py:213
  263.4 1.1 convert_bitcast_fusion
  264.5 0.3 copy.53
  264.9 0.3 copy.62
  265.1 14.7 %all-gather.9.cloned.1.call-done = bf16[5120,768]{1,0:T(8,128)(2,1)} async-done(((bf16[640,768]{1,0:T(8,128)(2,1)}), bf16[5120,768]{1,0:T(8,128)(2,1)}) %all-gather.9.cloned.1.call-update) | async-done | bytes 7864336 | tf_op jit(solution)/shard_map/all_gather | solution.py:199
  279.8 1.3 slice.41
  281.2 1.7 reshape.51
  282.9 1.6 convolution_bitcast_fusion.1
  284.6 3.8 %fusion.66 = (f32[256]{0:T(256)S(1)}, f32[256]{0:T(256)S(1)}, f32[256,768]{1,0:T(8,128)}) fusion(f32[256,768]{1,0:T(8,128)S(1)} %convolution_bitcast_fusion.1, f32[256,768]{1,0:T(8,128)S(1)} %copy.62, bf16[8,640,768]{2,1,0:T(8,128)(2,1)} %bitcast.86, bf16[8,96,8,96]{3,2,1,0:T(8,128)(2,1)S(1)} %reshape.51, bf16[8,256,160]{1,2,0:T(8,128)(2,1)} %all-to-all-done), kind=kOutput, calls=%fused_computation.65 | convolution fusion | flops 605355520 | bytes 5113856 | tf_op jit(solution)/shard_map/rjc,jce->re/dot_general | solution.py:231
  288.4 5.3 %fusion.35 = bf16[256,768]{1,0:T(8,128)(2,1)S(1)} fusion(f32[256,768]{1,0:T(8,128)} %get-tuple-element.17, bf16[8,640,768]{2,1,0:T(8,128)(2,1)} %bitcast.87, f32[256]{0:T(256)S(1)} %get-tuple-element.16, f32[256]{0:T(256)S(1)} %get-tuple-element.15), kind=kOutput, calls=%fused_computation.27 | convolution fusion | flops 1209729024 | bytes 6686720 | tf_op jit(solution)/shard_map/rjc,jce->re/dot_general | solution.py:244
  293.9 12.5 %all_to_all.10 = bf16[8,256,96]{1,2,0:T(8,128)(2,1)S(1)} all-to-all(bf16[8,256,96]{1,2,0:T(8,128)(2,1)S(1)} %bitcast.82), channel_id=1, replica_groups=mesh['blk'=16,'mp'=8] {'mp'}, dimensions={0} | all-to-all | bytes 786432 | tf_op jit(solution)/shard_map/all_to_all | solution.py:247
  306.4 0.8 copy.69
  (30 shorter events, 0.7 us)
Async XLA Ops:
  6.5 115.7 %all-gather.5.cloned.1.call-start = ((), (), s32[]{:S(2)}) async-start(), calls=%async_computation.2 | async-start | bytes 8912896 | tf_op jit(solution)/shard_map/all_gather | solution.py:193
  64.0 5.4 %copy-start.4 = (bf16[768,96]{0,1:T(8,128)(2,1)S(1)}, bf16[768,96]{0,1:T(8,128)(2,1)}, u32[]{:S(2)}) copy-start(bf16[768,96]{0,1:T(8,128)(2,1)} %param.16) | copy-start | bytes 442372
  67.8 1.7 copy-start.2
  67.8 3.6 %copy-start.3 = (bf16[192,768]{1,0:T(8,128)(2,1)S(1)}, bf16[192,768]{1,0:T(8,128)(2,1)}, u32[]{:S(2)}) copy-start(bf16[192,768]{1,0:T(8,128)(2,1)} %param.23) | copy-start | bytes 884740
  69.4 54.6 %copy-start.6 = (s32[64]{0:T(128)S(1)}, s32[64]{0:T(128)}, u32[]{:S(2)}) copy-start(s32[64]{0:T(128)} %param.14) | copy-start | bytes 772
  69.4 168.9 %all-gather.7.cloned.1.call-start = ((), (), s32[]{:S(2)}) async-start(), calls=%async_computation.3 | async-start | bytes 6684672 | tf_op jit(solution)/shard_map/all_gather | solution.py:198
  71.4 51.1 %copy-start.1 = (bf16[640,768]{1,0:T(8,128)(2,1)}, bf16[640,768]{1,0:T(8,128)(2,1)S(1)}, u32[]{:S(2)}) copy-start(bf16[640,768]{1,0:T(8,128)(2,1)S(1)} %constant_dynamic-update-slice_fusion) | copy-start | bytes 2949124
  122.3 157.6 %all-gather.9.cloned.1.call-start = ((), (), s32[]{:S(2)}) async-start(), calls=%async_computation.4 | async-start | bytes 8847360 | tf_op jit(solution)/shard_map/all_gather | solution.py:199
  248.5 3.9 %copy-start.5 = (s32[64]{0:T(128)S(1)}, s32[64]{0:T(128)}, u32[]{:S(2)}) copy-start(s32[64]{0:T(128)} %param.13) | copy-start | bytes 772
  252.4 2.9 copy-start
  256.6 26.3 %all-to-all-start = ((bf16[8,256,160]{1,2,0:T(8,128)(2,1)}), bf16[8,256,160]{1,2,0:T(8,128)(2,1)}, u32[]{:S(2)}, u32[]{:S(2)}) async-start(bf16[8,256,160]{1,2,0:T(8,128)(2,1)} %bitcast.76), calls=%async_computation | async-start | bytes 1310720 | tf_op jit(solution)/shard_map/all_to_all | solution.py:213
Sparse Core Ops, SparseCore 0:
  69.5 52.6 all-gather.4
  123.9 43.1 all-gather.6
  169.4 110.3 all-gather.8

commit v13 on v12

--- a/solution.py
+++ b/solution.py
@@ -194,9 +194,15 @@
 
     pieces = (gin_in.T, ffn_in.T, gin_out, w_attn_out, ffn_out)
     packed_weights = jnp.concatenate(pieces, axis=0)
-    kv_all, packed_weights, late_features = lax.optimization_barrier((kv_all, packed_weights, features))
+    n_blk = lax.axis_size("blk")
+    piece_rows = packed_weights.shape[0] // n_blk
+    piece = lax.dynamic_slice_in_dim(
+        packed_weights, lax.axis_index("blk") * piece_rows, piece_rows, 0
+    )
+    piece_parts = lax.all_gather(piece, "mp", axis=0, tiled=False)
+    kv_all, piece_parts, late_features = lax.optimization_barrier((kv_all, piece_parts, features))
     all_features = lax.all_gather(late_features, "blk", axis=0, tiled=True)
-    weight_parts = lax.all_gather(packed_weights, "mp", axis=0, tiled=False)
+    weight_parts = lax.all_gather(piece_parts, "blk", axis=1, tiled=True)
     unpacked = []
     offset = 0
     for x in pieces:

time: 314 us -> 315 us (level)
  blocking collectives: 12.5 us -> 52.9 us
  waiting for transfers between devices: 66.1 us -> 28.6 us
    all_gather x0 -> x1, blocking collectives: none -> 39.9 us  [per_device(): piece_parts = lax.all_gather(piece, 'mp', axis=0, tiled=False)]
    all_gather x1, waiting for transfers between devices: 50.8 us -> 19.3 us  [per_device(): lax.all_gather(projected[:, HEAD_DIM * heads:], 'blk', axis=0, tiled=True)]
    all_gather x1, waiting for transfers between devices: 14.7 us -> 0.02 us  [per_device(): weight_parts = lax.all_gather(piece_parts, 'blk', axis=1, tiled=True)]
    all_to_all x1, waiting for transfers between devices: 0.01 us -> 8.79 us  [per_device(): received = lax.all_to_all(mixed_in, 'mp', 0, 0, tiled=False)]
  transfers between devices with their start and end apart: 4 -> 4, of which waited for: 2 -> 2; matrix products, arithmetic and copies ran while one was open for 9% -> 8% of each run, Pallas kernels for 36% -> 36%
where the time goes in v13:
time: 315 us; the launch traced here: 314 us
  Pallas kernels  167 us (53%)
  blocking collectives  52.9 us (17%)
  waiting for transfers between devices  28.6 us (9%)
  local copies, waits for them, and re-layouts  21.9 us (7%)
  matrix products  21.2 us (7%)
  between operations  13.4 us (4%)
  starting transfers between devices  6.52 us (2%)
    pallas_call x1, Pallas kernels, flash_attention(): pl.pallas_call(functools.partial(flash_kernel, dim), grid=grid, in_specs=...  113 us
    pallas_call x1, Pallas kernels, dma_exchange(): pl.pallas_call(functools.partial(exchange_kernel, axis, n, scatter), in_s...  54 us
    all_gather x1, blocking collectives, per_device(): piece_parts = lax.all_gather(piece, 'mp', axis=0, tiled=False)  39.9 us
    all_gather x1, waiting for transfers between devices, per_device(): lax.all_gather(projected[:, HEAD_DIM * heads:], 'blk', axis=0, tiled=True)  19.3 us
    all_to_all x1, blocking collectives, per_device(): lax.all_to_all(out_parts, 'mp', 0, 0, tiled=False).reshape(rows, cols)  13 us
    all_to_all x1, waiting for transfers between devices, per_device(): received = lax.all_to_all(mixed_in, 'mp', 0, 0, tiled=False)  8.79 us
    reshape x1, local copies, waits for them, and re-layouts, neighbour_sum(): blocks = all_features.reshape(count, BLOCK, cols)  6.52 us
  transfers between devices with their start and end apart: 4, of which 2 were waited for; matrix products, arithmetic and copies ran while one was open for 8% of the time, Pallas kernels for 36%

profile of v13, /device:TPU:0, one launch (start us, length us, event | category | flops | bytes accessed | tf_op | source)
XLA Modules:
  0.0 314.2 jit_solution(8501338503169670564)
XLA Ops:
  6.5 1.0 pad_maximum_fusion.1
  7.5 0.4 reshape.48
  8.0 2.0 copy.52.x_ref
  10.0 54.0 %shard_map.118 = bf16[8,2048,96]{2,1,0:T(8,128)(2,1)} custom-call(bf16[2048,96]{1,0:T(8,128)(2,1)} %copy.52.x_ref), custom_call_target="tpu_custom_call" | custom-call | tf_op jit(solution)/shard_map/pallas_call | solution.py:145
  64.1 3.7 %fusion.2 = bf16[192,2048]{1,0:T(8,128)(2,1)S(1)} fusion(bf16[8,2048,96]{2,1,0:T(8,128)(2,1)} %shard_map.118, bf16[8,96,192]{1,0,2:T(8,128)(2,1)S(1)} %reshape.48), kind=kOutput, calls=%fused_computation.5 | convolution fusion | flops 604372992 | bytes 4227072 | tf_op jit(solution)/shard_map/jrc,jcd->rd/dot_general | solution.py:184
  67.9 0.5 copy.56
  68.4 1.1 slice.38
  69.7 39.9 %all-gather = bf16[320,768]{1,0:T(8,128)(2,1)} all-gather(bf16[40,768]{1,0:T(8,128)(2,1)S(1)} %constant_dynamic-slice_fusion), channel_id=2, replica_groups=mesh['blk'=16,'mp'=8] {'mp'}, dimensions={0}, use_global_device_ids=true | all-gather | bytes 552960 | tf_op jit(solution)/shard_map/all_gather | solution.py:202
  109.6 19.3 %all-gather.5.cloned.1.call-done.kv_ref = bf16[32768,128]{1,0:T(8,128)(2,1)} async-done(((bf16[2048,128]{1,0:T(8,128)(2,1)}), bf16[32768,128]{1,0:T(8,128)(2,1)}) %all-gather.5.cloned.1.call-update) | async-done | bytes 8388624 | tf_op jit(solution)/shard_map/all_gather | solution.py:193
  128.9 0.2 all-gather.9.cloned.1.call-start
  129.1 0.5 all-gather.9.cloned.1.call-update
  129.7 0.9 concatenate.14.q_ref
  130.6 113.1 %shard_map.119 = bf16[2048,64]{1,0:T(8,128)(2,1)} custom-call(bf16[2048,128]{1,0:T(8,128)(2,1)} %concatenate.14.q_ref, bf16[32768,128]{1,0:T(8,128)(2,1)} %all-gather.5.cloned.1.call-done.kv_ref), custom_call_target="tpu_custom_call" | custom-call | flops 34359738368 | bytes 34340864 | tf_op jit(solution)/shard_map/pallas_call | solution.py:75
  243.7 1.2 copy.59
  245.0 6.5 %copy_bitcast_fusion = bf16[256,128,96]{1,2,0:T(8,128)(2,1)} fusion(bf16[32768,96]{0,1:T(8,128)(2,1)} %all-gather.7.cloned.1.call-done), kind=kLoop, calls=%fused_computation.1 | loop fusion | bytes 12582912 | tf_op jit(solution)/shard_map/reshape | solution.py:21
  251.5 3.6 %gather_fusion = bf16[64,128,96]{1,2,0:T(8,128)(2,1)S(1)} fusion(bf16[256,128,96]{1,2,0:T(8,128)(2,1)} %copy_bitcast_fusion, s32[1024]{0:T(1024)S(1)} %pad_clamp_fusion), kind=kCustom, calls=%fused_computation | custom fusion | bytes 3145984 | tf_op jit(solution)/shard_map/jit(_take)/gather | solution.py:22
  255.2 3.8 %fusion.9 = f32[64,128,96]{1,2,0:T(8,128)S(1)} fusion(s32[64,128,128]{2,1,0:T(8,128)} %param.15, bf16[64,128,96]{1,2,0:T(8,128)(2,1)S(1)} %gather_fusion, pred[64]{0:T(512)(128)(4,1)S(1)} %get-tuple-element.13), kind=kOutput, calls=%fused_computation.12 | convolution fusion | flops 203161600 | bytes 8912960 | tf_op jit(solution)/shard_map/ers,esf->erf/dot_general | solution.py:23
  259.0 2.9 fusion.24
  261.9 0.3 fusion.46
  262.3 0.9 copy.92
  263.2 6.3 %all-to-all-start = ((bf16[8,256,160]{1,2,0:T(8,128)(2,1)}), bf16[8,256,160]{1,2,0:T(8,128)(2,1)}, u32[]{:S(2)}, u32[]{:S(2)}) async-start(bf16[8,256,160]{1,2,0:T(8,128)(2,1)} %bitcast.76), calls=%async_computation | async-start | bytes 1310720 | tf_op jit(solution)/shard_map/all_to_all | solution.py:219
  269.4 1.1 convert_bitcast_fusion
  270.6 0.3 copy.53
  270.9 0.3 copy.62
  271.2 1.3 slice-done
  272.5 1.7 reshape.51
  274.2 8.8 %all-to-all-done = bf16[8,256,160]{1,2,0:T(8,128)(2,1)} async-done(((bf16[8,256,160]{1,2,0:T(8,128)(2,1)}), bf16[8,256,160]{1,2,0:T(8,128)(2,1)}, u32[]{:S(2)}, u32[]{:S(2)}) %all-to-all-start) | async-done | bytes 655392 | tf_op jit(solution)/shard_map/all_to_all | solution.py:219
  283.0 1.6 convolution_bitcast_fusion.1
  284.6 3.8 %fusion.66 = (f32[256]{0:T(256)S(1)}, f32[256]{0:T(256)S(1)}, f32[256,768]{1,0:T(8,128)}) fusion(f32[256,768]{1,0:T(8,128)S(1)} %convolution_bitcast_fusion.1, f32[256,768]{1,0:T(8,128)S(1)} %copy.62, bf16[8,640,768]{2,1,0:T(8,128)(2,1)} %all-gather.9.cloned.1.call-done, bf16[8,96,8,96]{3,2,1,0:T(8,128)(2,1)S(1)} %reshape.51, ...), kind=kOutput, calls=%fused_computation.66 | convolution fusion | flops 605355520 | bytes 5113856 | tf_op jit(solution)/shard_map/rjc,jce->re/dot_general | solution.py:237
  288.4 5.3 %fusion.35 = bf16[256,768]{1,0:T(8,128)(2,1)S(1)} fusion(f32[256,768]{1,0:T(8,128)} %get-tuple-element.17, bf16[8,640,768]{2,1,0:T(8,128)(2,1)} %all-gather.9.cloned.1.call-done, f32[256]{0:T(256)S(1)} %get-tuple-element.16, f32[256]{0:T(256)S(1)} %get-tuple-element.15), kind=kOutput, calls=%fused_computation.27 | convolution fusion | flops 1209729024 | bytes 6686720 | tf_op jit(solution)/shard_map/rjc,jce->re/dot_general | solution.py:250
  293.9 13.0 %all_to_all.10 = bf16[8,256,96]{1,2,0:T(8,128)(2,1)S(1)} all-to-all(bf16[8,256,96]{1,2,0:T(8,128)(2,1)S(1)} %bitcast.83), channel_id=1, replica_groups=mesh['blk'=16,'mp'=8] {'mp'}, dimensions={0} | all-to-all | bytes 786432 | tf_op jit(solution)/shard_map/all_to_all | solution.py:253
  306.9 0.8 copy.69
  (35 shorter events, 0.6 us)
Async XLA Ops:
  6.5 122.3 %all-gather.5.cloned.1.call-start = ((), (), s32[]{:S(2)}) async-start(), calls=%async_computation.2 | async-start | bytes 8912896 | tf_op jit(solution)/shard_map/all_gather | solution.py:193
  64.1 5.5 %copy-start.3 = (bf16[768,96]{0,1:T(8,128)(2,1)S(1)}, bf16[768,96]{0,1:T(8,128)(2,1)}, u32[]{:S(2)}) copy-start(bf16[768,96]{0,1:T(8,128)(2,1)} %param.16) | copy-start | bytes 442372
  67.8 1.7 copy-start.1
  67.8 1.8 copy-start.4
  67.8 1.8 copy-start.5
  67.8 1.8 copy-start.2
  69.4 61.2 %copy-start.7 = (s32[64]{0:T(128)S(1)}, s32[64]{0:T(128)}, u32[]{:S(2)}) copy-start(s32[64]{0:T(128)} %param.14) | copy-start | bytes 772
  69.5 175.5 %all-gather.7.cloned.1.call-start = ((), (), s32[]{:S(2)}) async-start(), calls=%async_computation.3 | async-start | bytes 6684672 | tf_op jit(solution)/shard_map/all_gather | solution.py:204
  128.9 142.3 %all-gather.9.cloned.1.call-start = ((), (), s32[]{:S(2)}) async-start(), calls=%async_computation.4 | async-start | bytes 8355840 | tf_op jit(solution)/shard_map/all_gather | solution.py:205
  255.2 3.8 %copy-start.6 = (s32[64]{0:T(128)S(1)}, s32[64]{0:T(128)}, u32[]{:S(2)}) copy-start(s32[64]{0:T(128)} %param.13) | copy-start | bytes 772
  259.0 2.9 copy-start
  263.2 19.8 %all-to-all-start = ((bf16[8,256,160]{1,2,0:T(8,128)(2,1)}), bf16[8,256,160]{1,2,0:T(8,128)(2,1)}, u32[]{:S(2)}, u32[]{:S(2)}) async-start(bf16[8,256,160]{1,2,0:T(8,128)(2,1)} %bitcast.76), calls=%async_computation | async-start | bytes 1310720 | tf_op jit(solution)/shard_map/all_to_all | solution.py:219
  271.2 1.3 slice-start
Sparse Core Ops, SparseCore 0:
  69.6 59.2 all-gather.4
  130.5 42.6 all-gather.6
  174.9 50.4 all-gather.8

commit v14 on v13

--- a/solution.py
+++ b/solution.py
@@ -10,15 +10,15 @@
 
 HEAD_DIM = 64
 BLOCK = 128
-Q_TILE = 512
+Q_TILE = 1024
 K_TILE = 4096
 
 
 def neighbour_sum(features, edge_dst, edge_src, edge_mask, all_features):
     rows, cols = features.shape
     local_blocks = rows // BLOCK
-    count = all_features.shape[0] // BLOCK
-    blocks = all_features.reshape(count, BLOCK, cols)
+    count = all_features.shape[0]
+    blocks = all_features
     pulled = jnp.take(blocks, jnp.clip(edge_src, 0, count - 1), axis=0)
     summand_terms = jnp.einsum(
         "ers,esf->erf",
@@ -201,7 +201,9 @@
     )
     piece_parts = lax.all_gather(piece, "mp", axis=0, tiled=False)
     kv_all, piece_parts, late_features = lax.optimization_barrier((kv_all, piece_parts, features))
-    all_features = lax.all_gather(late_features, "blk", axis=0, tiled=True)
+    all_features = lax.all_gather(
+        late_features.reshape(rows // BLOCK, BLOCK, cols), "blk", axis=0, tiled=True
+    )
     weight_parts = lax.all_gather(piece_parts, "blk", axis=1, tiled=True)
     unpacked = []
     offset = 0

time: 315 us -> 305 us (0.968)
  local copies, waits for them, and re-layouts: 21.9 us -> 16.2 us
  Pallas kernels: 167 us -> 163 us
    reshape x1, local copies, waits for them, and re-layouts: 6.52 us -> 0.81 us  [per_device(): late_features.reshape(rows // BLOCK, BLOCK, cols)]
    pallas_call x1, Pallas kernels: 113 us -> 109 us  [flash_attention(): pl.pallas_call(functools.partial(flash_kernel, dim), grid=grid, in_specs=...]
  transfers between devices with their start and end apart: 4 -> 4, of which waited for: 2 -> 2; matrix products, arithmetic and copies ran while one was open for 8% -> 6% of each run, Pallas kernels for 36% -> 36%
where the time goes in v14:
time: 305 us; the launch traced here: 304 us
  Pallas kernels  163 us (53%)
  blocking collectives  52.9 us (17%)
  waiting for transfers between devices  28.8 us (9%)
  matrix products  21.1 us (7%)
  local copies, waits for them, and re-layouts  16.2 us (5%)
  between operations  13.4 us (4%)
  starting transfers between devices  6.34 us (2%)
    pallas_call x1, Pallas kernels, flash_attention(): pl.pallas_call(functools.partial(flash_kernel, dim), grid=grid, in_specs=...  109 us
    pallas_call x1, Pallas kernels, dma_exchange(): pl.pallas_call(functools.partial(exchange_kernel, axis, n, scatter), in_s...  54 us
    all_gather x1, blocking collectives, per_device(): piece_parts = lax.all_gather(piece, 'mp', axis=0, tiled=False)  39.9 us
    all_gather x1, waiting for transfers between devices, per_device(): lax.all_gather(projected[:, HEAD_DIM * heads:], 'blk', axis=0, tiled=True)  19.2 us
    all_to_all x1, blocking collectives, per_device(): lax.all_to_all(out_parts, 'mp', 0, 0, tiled=False).reshape(rows, cols)  13 us
    all_to_all x1, waiting for transfers between devices, per_device(): received = lax.all_to_all(mixed_in, 'mp', 0, 0, tiled=False)  8.8 us
    all_to_all x1, starting transfers between devices, per_device(): received = lax.all_to_all(mixed_in, 'mp', 0, 0, tiled=False)  6.25 us
  transfers between devices with their start and end apart: 4, of which 2 were waited for; matrix products, arithmetic and copies ran while one was open for 6% of the time, Pallas kernels for 36%

profile of v14, /device:TPU:0, one launch (start us, length us, event | category | flops | bytes accessed | tf_op | source)
XLA Modules:
  0.0 304.3 jit_solution(12293781318301571063)
XLA Ops:
  6.5 1.0 pad_maximum_fusion.1
  7.5 0.4 reshape.48
  8.0 2.0 copy.65.x_ref
  10.0 54.0 %shard_map.118 = bf16[8,2048,96]{2,1,0:T(8,128)(2,1)} custom-call(bf16[2048,96]{1,0:T(8,128)(2,1)} %copy.65.x_ref), custom_call_target="tpu_custom_call" | custom-call | tf_op jit(solution)/shard_map/pallas_call | solution.py:145
  64.1 3.7 %fusion.2 = bf16[192,2048]{1,0:T(8,128)(2,1)S(1)} fusion(bf16[8,2048,96]{2,1,0:T(8,128)(2,1)} %shard_map.118, bf16[8,96,192]{1,0,2:T(8,128)(2,1)S(1)} %reshape.48), kind=kOutput, calls=%fused_computation.4 | convolution fusion | flops 604372992 | bytes 4227072 | tf_op jit(solution)/shard_map/jrc,jcd->rd/dot_general | solution.py:184
  67.8 0.5 copy.69
  68.4 1.1 slice.38
  69.7 39.9 %all-gather = bf16[320,768]{1,0:T(8,128)(2,1)} all-gather(bf16[40,768]{1,0:T(8,128)(2,1)S(1)} %constant_dynamic-slice_fusion), channel_id=2, replica_groups=mesh['blk'=16,'mp'=8] {'mp'}, dimensions={0}, use_global_device_ids=true | all-gather | bytes 552960 | tf_op jit(solution)/shard_map/all_gather | solution.py:202
  109.6 19.2 %all-gather.5.cloned.1.call-done.kv_ref = bf16[32768,128]{1,0:T(8,128)(2,1)} async-done(((bf16[2048,128]{1,0:T(8,128)(2,1)}), bf16[32768,128]{1,0:T(8,128)(2,1)}) %all-gather.5.cloned.1.call-update) | async-done | bytes 8388624 | tf_op jit(solution)/shard_map/all_gather | solution.py:193
  128.8 0.8 copy_bitcast_fusion.1
  129.7 0.7 all-gather.9.cloned.1.call-update
  130.5 0.9 concatenate.14.q_ref
  131.4 109.0 %shard_map.119 = bf16[2048,64]{1,0:T(8,128)(2,1)} custom-call(bf16[2048,128]{1,0:T(8,128)(2,1)} %concatenate.14.q_ref, bf16[32768,128]{1,0:T(8,128)(2,1)} %all-gather.5.cloned.1.call-done.kv_ref), custom_call_target="tpu_custom_call" | custom-call | flops 34359738368 | bytes 17563648 | tf_op jit(solution)/shard_map/pallas_call | solution.py:75
  240.4 1.2 copy.72
  241.7 3.6 %gather_fusion = bf16[64,128,96]{1,2,0:T(8,128)(2,1)S(1)} fusion(bf16[256,128,96]{1,2,0:T(8,128)(2,1)} %all-gather.7.cloned.1.call-done, s32[1024]{0:T(1024)S(1)} %pad_clamp_fusion), kind=kCustom, calls=%fused_computation | custom fusion | bytes 3145984 | tf_op jit(solution)/shard_map/jit(_take)/gather | solution.py:22
  245.3 3.8 %fusion.9 = f32[64,128,96]{1,2,0:T(8,128)S(1)} fusion(s32[64,128,128]{2,1,0:T(8,128)} %param.15, bf16[64,128,96]{1,2,0:T(8,128)(2,1)S(1)} %gather_fusion, pred[64]{0:T(512)(128)(4,1)S(1)} %get-tuple-element.13), kind=kOutput, calls=%fused_computation.11 | convolution fusion | flops 203161600 | bytes 8912960 | tf_op jit(solution)/shard_map/ers,esf->erf/dot_general | solution.py:23
  249.1 2.9 fusion.24
  252.0 0.3 fusion.46
  252.4 0.9 copy.105
  253.3 6.3 %all-to-all-start = ((bf16[8,256,160]{1,2,0:T(8,128)(2,1)}), bf16[8,256,160]{1,2,0:T(8,128)(2,1)}, u32[]{:S(2)}, u32[]{:S(2)}) async-start(bf16[8,256,160]{1,2,0:T(8,128)(2,1)} %bitcast.76), calls=%async_computation | async-start | bytes 1310720 | tf_op jit(solution)/shard_map/all_to_all | solution.py:221
  259.6 1.1 convert_bitcast_fusion
  260.7 0.3 copy.66
  261.0 0.3 copy.75
  261.3 1.3 slice-done
  262.6 1.7 reshape.51
  264.3 8.8 %all-to-all-done = bf16[8,256,160]{1,2,0:T(8,128)(2,1)} async-done(((bf16[8,256,160]{1,2,0:T(8,128)(2,1)}), bf16[8,256,160]{1,2,0:T(8,128)(2,1)}, u32[]{:S(2)}, u32[]{:S(2)}) %all-to-all-start) | async-done | bytes 655392 | tf_op jit(solution)/shard_map/all_to_all | solution.py:221
  273.1 1.6 convolution_bitcast_fusion.1
  274.7 3.8 %fusion.66 = (f32[256]{0:T(256)S(1)}, f32[256]{0:T(256)S(1)}, f32[256,768]{1,0:T(8,128)}) fusion(f32[256,768]{1,0:T(8,128)S(1)} %convolution_bitcast_fusion.1, f32[256,768]{1,0:T(8,128)S(1)} %copy.75, bf16[8,640,768]{2,1,0:T(8,128)(2,1)} %all-gather.9.cloned.1.call-done, bf16[8,96,8,96]{3,2,1,0:T(8,128)(2,1)S(1)} %reshape.51, ...), kind=kOutput, calls=%fused_computation.66 | convolution fusion | flops 605355520 | bytes 5113856 | tf_op jit(solution)/shard_map/rjc,jce->re/dot_general | solution.py:239
  278.5 5.3 %fusion.35 = bf16[256,768]{1,0:T(8,128)(2,1)S(1)} fusion(f32[256,768]{1,0:T(8,128)} %get-tuple-element.17, bf16[8,640,768]{2,1,0:T(8,128)(2,1)} %all-gather.9.cloned.1.call-done, f32[256]{0:T(256)S(1)} %get-tuple-element.16, f32[256]{0:T(256)S(1)} %get-tuple-element.15), kind=kOutput, calls=%fused_computation.26 | convolution fusion | flops 1209729024 | bytes 6686720 | tf_op jit(solution)/shard_map/rjc,jce->re/dot_general | solution.py:252
  283.8 0.2 copy.76
  284.0 13.0 %all_to_all.10 = bf16[8,256,96]{1,2,0:T(8,128)(2,1)S(1)} all-to-all(bf16[8,256,96]{1,2,0:T(8,128)(2,1)S(1)} %bitcast.83), channel_id=1, replica_groups=mesh['blk'=16,'mp'=8] {'mp'}, dimensions={0} | all-to-all | bytes 786432 | tf_op jit(solution)/shard_map/all_to_all | solution.py:255
  297.0 0.8 copy.82
  (35 shorter events, 0.4 us)
Async XLA Ops:
  6.5 122.3 %all-gather.5.cloned.1.call-start = ((), (), s32[]{:S(2)}) async-start(), calls=%async_computation.2 | async-start | bytes 8912896 | tf_op jit(solution)/shard_map/all_gather | solution.py:193
  67.8 1.7 copy-start.3
  67.8 1.7 copy-start.1
  67.8 1.8 copy-start.4
  67.8 1.8 copy-start.5
  67.8 1.8 copy-start.2
  68.3 60.5 %copy-start = (bf16[2048,96]{0,1:T(8,128)(2,1)S(1)}, bf16[2048,96]{0,1:T(8,128)(2,1)}, u32[]{:S(2)}) copy-start(bf16[2048,96]{0,1:T(8,128)(2,1)} %param.12) | copy-start | bytes 1179652
  69.4 172.2 %all-gather.7.cloned.1.call-start = ((), (), s32[]{:S(2)}) async-start(), calls=%async_computation.3 | async-start | bytes 6684672 | tf_op jit(solution)/shard_map/all_gather | solution.py:204
  69.7 61.7 %copy-start.7 = (s32[64]{0:T(128)S(1)}, s32[64]{0:T(128)}, u32[]{:S(2)}) copy-start(s32[64]{0:T(128)} %param.14) | copy-start | bytes 772
  129.7 131.6 %all-gather.9.cloned.1.call-start = ((), (), s32[]{:S(2)}) async-start(), calls=%async_computation.4 | async-start | bytes 8355840 | tf_op jit(solution)/shard_map/all_gather | solution.py:207
  245.3 3.8 %copy-start.6 = (s32[64]{0:T(128)S(1)}, s32[64]{0:T(128)}, u32[]{:S(2)}) copy-start(s32[64]{0:T(128)} %param.13) | copy-start | bytes 772
  253.3 19.8 %all-to-all-start = ((bf16[8,256,160]{1,2,0:T(8,128)(2,1)}), bf16[8,256,160]{1,2,0:T(8,128)(2,1)}, u32[]{:S(2)}, u32[]{:S(2)}) async-start(bf16[8,256,160]{1,2,0:T(8,128)(2,1)} %bitcast.76), calls=%async_computation | async-start | bytes 1310720 | tf_op jit(solution)/shard_map/all_to_all | solution.py:221
  261.3 1.3 slice-start
Sparse Core Ops, SparseCore 0:
  69.6 59.2 all-gather.4
  130.5 42.6 all-gather.6
  174.9 50.4 all-gather.8

commit v15 on v14

--- a/solution.py
+++ b/solution.py
@@ -178,7 +178,9 @@
     heads = w_query.shape[1] // HEAD_DIM
     scale = 1.0 / math.sqrt(HEAD_DIM)
 
-    feature_parts = dma_exchange(features, "mp", 0, False)
+    feature_parts = dma_exchange(
+        features.reshape(rows * cols // 128, 128), "mp", 0, False
+    ).reshape(n_mp, rows, cols)
 
     def project(w):
         return jnp.einsum(

time: 305 us -> 302 us (level)
  Pallas kernels: 163 us -> 152 us
  local copies, waits for them, and re-layouts: 16.2 us -> 24.3 us
    pallas_call x1, Pallas kernels: 54 us -> 42.8 us  [dma_exchange(): pl.pallas_call(functools.partial(exchange_kernel, axis, n, scatter), in_s...]
    reshape x0 -> x2, local copies, waits for them, and re-layouts: none -> 8.91 us  [the longest x1 7.45 us: per_device(): feature_parts = dma_exchange(features.reshape(rows * cols // 128, 128), '...]
where the time goes in v15:
time: 302 us; the launch traced here: 301 us
  Pallas kernels  152 us (50%)
  blocking collectives  52.9 us (18%)
  waiting for transfers between devices  28.8 us (10%)
  local copies, waits for them, and re-layouts  24.3 us (8%)
  matrix products  21.1 us (7%)
  between operations  13.4 us (4%)
  starting transfers between devices  6.35 us (2%)
    pallas_call x1, Pallas kernels, flash_attention(): pl.pallas_call(functools.partial(flash_kernel, dim), grid=grid, in_specs=...  109 us
    pallas_call x1, Pallas kernels, dma_exchange(): pl.pallas_call(functools.partial(exchange_kernel, axis, n, scatter), in_s...  42.8 us
    all_gather x1, blocking collectives, per_device(): piece_parts = lax.all_gather(piece, 'mp', axis=0, tiled=False)  39.9 us
    all_gather x1, waiting for transfers between devices, per_device(): lax.all_gather(projected[:, HEAD_DIM * heads:], 'blk', axis=0, tiled=True)  19.2 us
    all_to_all x1, blocking collectives, per_device(): lax.all_to_all(out_parts, 'mp', 0, 0, tiled=False).reshape(rows, cols)  13 us
    all_to_all x1, waiting for transfers between devices, per_device(): received = lax.all_to_all(mixed_in, 'mp', 0, 0, tiled=False)  8.79 us
    reshape x1, local copies, waits for them, and re-layouts, per_device(): feature_parts = dma_exchange(features.reshape(rows * cols // 128, 128), '...  7.45 us
    all_to_all x1, starting transfers between devices, per_device(): received = lax.all_to_all(mixed_in, 'mp', 0, 0, tiled=False)  6.26 us
  transfers between devices with their start and end apart: 4, of which 2 were waited for; matrix products, arithmetic and copies ran while one was open for 6% of the time, Pallas kernels for 36%

profile of v15, /device:TPU:0, one launch (start us, length us, event | category | flops | bytes accessed | tf_op | source)
XLA Modules:
  0.0 301.3 jit_solution(10866256200694265867)
XLA Ops:
  6.5 1.0 pad_maximum_fusion.1
  7.5 0.4 reshape.56
  8.0 1.3 copy.66
  9.3 1.5 reshape.54.x_ref
  10.7 42.8 %shard_map.118 = bf16[8,1536,128]{2,1,0:T(8,128)(2,1)} custom-call(bf16[1536,128]{1,0:T(8,128)(2,1)} %reshape.54.x_ref), custom_call_target="tpu_custom_call" | custom-call | tf_op jit(solution)/shard_map/pallas_call | solution.py:145
  53.5 7.5 %reshape.55 = bf16[8,2048,96]{2,1,0:T(8,128)(2,1)} reshape(bf16[8,1536,128]{2,1,0:T(8,128)(2,1)} %shard_map.118) | data formatting | bytes 6291456 | tf_op jit(solution)/shard_map/reshape | solution.py:183
  61.0 3.7 %fusion.2 = bf16[192,2048]{1,0:T(8,128)(2,1)S(1)} fusion(bf16[8,2048,96]{2,1,0:T(8,128)(2,1)} %reshape.55, bf16[8,96,192]{1,0,2:T(8,128)(2,1)S(1)} %reshape.56), kind=kOutput, calls=%fused_computation.4 | convolution fusion | flops 604372992 | bytes 4227072 | tf_op jit(solution)/shard_map/jrc,jcd->rd/dot_general | solution.py:186
  64.8 0.5 copy.70
  65.3 1.1 slice.38
  66.6 39.9 %all-gather = bf16[320,768]{1,0:T(8,128)(2,1)} all-gather(bf16[40,768]{1,0:T(8,128)(2,1)S(1)} %constant_dynamic-slice_fusion), channel_id=2, replica_groups=mesh['blk'=16,'mp'=8] {'mp'}, dimensions={0}, use_global_device_ids=true | all-gather | bytes 552960 | tf_op jit(solution)/shard_map/all_gather | solution.py:204
  106.5 19.2 %all-gather.5.cloned.1.call-done.kv_ref = bf16[32768,128]{1,0:T(8,128)(2,1)} async-done(((bf16[2048,128]{1,0:T(8,128)(2,1)}), bf16[32768,128]{1,0:T(8,128)(2,1)}) %all-gather.5.cloned.1.call-update) | async-done | bytes 8388624 | tf_op jit(solution)/shard_map/all_gather | solution.py:195
  125.8 0.8 copy_bitcast_fusion.1
  126.7 0.7 all-gather.9.cloned.1.call-update
  127.4 0.9 concatenate.14.q_ref
  128.4 109.0 %shard_map.119 = bf16[2048,64]{1,0:T(8,128)(2,1)} custom-call(bf16[2048,128]{1,0:T(8,128)(2,1)} %concatenate.14.q_ref, bf16[32768,128]{1,0:T(8,128)(2,1)} %all-gather.5.cloned.1.call-done.kv_ref), custom_call_target="tpu_custom_call" | custom-call | flops 34359738368 | bytes 17563648 | tf_op jit(solution)/shard_map/pallas_call | solution.py:75
  237.3 1.2 copy.73
  238.6 3.6 %gather_fusion = bf16[64,128,96]{1,2,0:T(8,128)(2,1)S(1)} fusion(bf16[256,128,96]{1,2,0:T(8,128)(2,1)} %all-gather.7.cloned.1.call-done, s32[1024]{0:T(1024)S(1)} %pad_clamp_fusion), kind=kCustom, calls=%fused_computation | custom fusion | bytes 3145984 | tf_op jit(solution)/shard_map/jit(_take)/gather | solution.py:22
  242.2 3.8 %fusion.9 = f32[64,128,96]{1,2,0:T(8,128)S(1)} fusion(s32[64,128,128]{2,1,0:T(8,128)} %param.15, bf16[64,128,96]{1,2,0:T(8,128)(2,1)S(1)} %gather_fusion, pred[64]{0:T(512)(128)(4,1)S(1)} %get-tuple-element.13), kind=kOutput, calls=%fused_computation.11 | convolution fusion | flops 203161600 | bytes 8912960 | tf_op jit(solution)/shard_map/ers,esf->erf/dot_general | solution.py:23
  246.1 2.9 fusion.24
  249.0 0.3 fusion.46
  249.4 0.9 copy.106
  250.3 6.3 %all-to-all-start = ((bf16[8,256,160]{1,2,0:T(8,128)(2,1)}), bf16[8,256,160]{1,2,0:T(8,128)(2,1)}, u32[]{:S(2)}, u32[]{:S(2)}) async-start(bf16[8,256,160]{1,2,0:T(8,128)(2,1)} %bitcast.76), calls=%async_computation | async-start | bytes 1310720 | tf_op jit(solution)/shard_map/all_to_all | solution.py:223
  256.5 1.1 convert_bitcast_fusion
  257.6 0.3 copy.67
  258.3 1.3 slice-done
  259.5 1.7 reshape.59
  261.2 8.8 %all-to-all-done = bf16[8,256,160]{1,2,0:T(8,128)(2,1)} async-done(((bf16[8,256,160]{1,2,0:T(8,128)(2,1)}), bf16[8,256,160]{1,2,0:T(8,128)(2,1)}, u32[]{:S(2)}, u32[]{:S(2)}) %all-to-all-start) | async-done | bytes 655392 | tf_op jit(solution)/shard_map/all_to_all | solution.py:223
  270.0 1.6 convolution_bitcast_fusion.1
  271.6 3.8 %fusion.66 = (f32[256]{0:T(256)S(1)}, f32[256]{0:T(256)S(1)}, f32[256,768]{1,0:T(8,128)}) fusion(f32[256,768]{1,0:T(8,128)S(1)} %convolution_bitcast_fusion.1, f32[256,768]{1,0:T(8,128)S(1)} %copy.76, bf16[8,640,768]{2,1,0:T(8,128)(2,1)} %all-gather.9.cloned.1.call-done, bf16[8,96,8,96]{3,2,1,0:T(8,128)(2,1)S(1)} %reshape.59, ...), kind=kOutput, calls=%fused_computation.66 | convolution fusion | flops 605355520 | bytes 5113856 | tf_op jit(solution)/shard_map/rjc,jce->re/dot_general | solution.py:241
  275.5 5.3 %fusion.35 = bf16[256,768]{1,0:T(8,128)(2,1)S(1)} fusion(f32[256,768]{1,0:T(8,128)} %get-tuple-element.17, bf16[8,640,768]{2,1,0:T(8,128)(2,1)} %all-gather.9.cloned.1.call-done, f32[256]{0:T(256)S(1)} %get-tuple-element.16, f32[256]{0:T(256)S(1)} %get-tuple-element.15), kind=kOutput, calls=%fused_computation.26 | convolution fusion | flops 1209729024 | bytes 6686720 | tf_op jit(solution)/shard_map/rjc,jce->re/dot_general | solution.py:254
  281.0 13.0 %all_to_all.10 = bf16[8,256,96]{1,2,0:T(8,128)(2,1)S(1)} all-to-all(bf16[8,256,96]{1,2,0:T(8,128)(2,1)S(1)} %bitcast.83), channel_id=1, replica_groups=mesh['blk'=16,'mp'=8] {'mp'}, dimensions={0} | all-to-all | bytes 786432 | tf_op jit(solution)/shard_map/all_to_all | solution.py:257
  294.0 0.8 copy.83
  (37 shorter events, 0.9 us)
Async XLA Ops:
  6.5 119.2 %all-gather.5.cloned.1.call-start = ((), (), s32[]{:S(2)}) async-start(), calls=%async_computation.2 | async-start | bytes 8912896 | tf_op jit(solution)/shard_map/all_gather | solution.py:195
  64.7 1.7 copy-start.3
  64.7 1.7 copy-start.1
  64.7 1.8 copy-start.4
  64.7 1.8 copy-start.5
  64.7 1.8 copy-start.2
  65.3 60.5 %copy-start = (bf16[2048,96]{0,1:T(8,128)(2,1)S(1)}, bf16[2048,96]{0,1:T(8,128)(2,1)}, u32[]{:S(2)}) copy-start(bf16[2048,96]{0,1:T(8,128)(2,1)} %param.12) | copy-start | bytes 1179652
  66.4 172.2 %all-gather.7.cloned.1.call-start = ((), (), s32[]{:S(2)}) async-start(), calls=%async_computation.3 | async-start | bytes 6684672 | tf_op jit(solution)/shard_map/all_gather | solution.py:206
  66.6 61.7 %copy-start.7 = (s32[64]{0:T(128)S(1)}, s32[64]{0:T(128)}, u32[]{:S(2)}) copy-start(s32[64]{0:T(128)} %param.14) | copy-start | bytes 772
  126.6 131.7 %all-gather.9.cloned.1.call-start = ((), (), s32[]{:S(2)}) async-start(), calls=%async_computation.4 | async-start | bytes 8355840 | tf_op jit(solution)/shard_map/all_gather | solution.py:209
  242.2 3.8 %copy-start.6 = (s32[64]{0:T(128)S(1)}, s32[64]{0:T(128)}, u32[]{:S(2)}) copy-start(s32[64]{0:T(128)} %param.13) | copy-start | bytes 772
  250.3 19.8 %all-to-all-start = ((bf16[8,256,160]{1,2,0:T(8,128)(2,1)}), bf16[8,256,160]{1,2,0:T(8,128)(2,1)}, u32[]{:S(2)}, u32[]{:S(2)}) async-start(bf16[8,256,160]{1,2,0:T(8,128)(2,1)} %bitcast.76), calls=%async_computation | async-start | bytes 1310720 | tf_op jit(solution)/shard_map/all_to_all | solution.py:223
  258.3 1.3 slice-start
Sparse Core Ops, SparseCore 0:
  66.5 59.2 all-gather.4
  127.5 42.6 all-gather.6
  171.8 50.4 all-gather.8

commit v16 on v14

--- a/solution.py
+++ b/solution.py
@@ -178,12 +178,12 @@
     heads = w_query.shape[1] // HEAD_DIM
     scale = 1.0 / math.sqrt(HEAD_DIM)
 
-    feature_parts = dma_exchange(features, "mp", 0, False)
+    feature_parts_t = dma_exchange(features.T, "mp", 0, False)
 
     def project(w):
         return jnp.einsum(
-            "jrc,jcd->rd",
-            feature_parts,
+            "jcr,jcd->rd",
+            feature_parts_t,
             w.reshape(n_mp, cols, w.shape[1]),
             preferred_element_type=jnp.float32,
         ).astype(jnp.bfloat16)
@@ -220,8 +220,8 @@
     mixed_in = jnp.concatenate([local_share, attended], axis=1).reshape(n_mp, share, -1)
     received = lax.all_to_all(mixed_in, "mp", 0, 0, tiled=False)
     own_rows = (
-        lax.dynamic_slice_in_dim(feature_parts, me * share, share, 1)
-        .transpose(1, 0, 2)
+        lax.dynamic_slice_in_dim(feature_parts_t, me * share, share, 2)
+        .transpose(2, 0, 1)
         .reshape(share, width)
         .astype(jnp.float32)
     )

time: 305 us -> 291 us (0.954)
  Pallas kernels: 163 us -> 152 us
    pallas_call x1, Pallas kernels: 54 us -> 42.9 us  [dma_exchange(): pl.pallas_call(functools.partial(exchange_kernel, axis, n, scatter), in_s...]
  transfers between devices with their start and end apart: 4 -> 4, of which waited for: 2 -> 2; matrix products, arithmetic and copies ran while one was open for 6% -> 6% of each run, Pallas kernels for 36% -> 38%
where the time goes in v16:
time: 291 us; the launch traced here: 290 us
  Pallas kernels  152 us (52%)
  blocking collectives  52.9 us (18%)
  waiting for transfers between devices  29.1 us (10%)
  matrix products  20.2 us (7%)
  local copies, waits for them, and re-layouts  13.8 us (5%)
  between operations  13.4 us (5%)
  starting transfers between devices  6.35 us (2%)
    pallas_call x1, Pallas kernels, flash_attention(): pl.pallas_call(functools.partial(flash_kernel, dim), grid=grid, in_specs=...  109 us
    pallas_call x1, Pallas kernels, dma_exchange(): pl.pallas_call(functools.partial(exchange_kernel, axis, n, scatter), in_s...  42.9 us
    all_gather x1, blocking collectives, per_device(): piece_parts = lax.all_gather(piece, 'mp', axis=0, tiled=False)  39.9 us
    all_gather x1, waiting for transfers between devices, per_device(): lax.all_gather(projected[:, HEAD_DIM * heads:], 'blk', axis=0, tiled=True)  19.2 us
    all_to_all x1, blocking collectives, per_device(): lax.all_to_all(out_parts, 'mp', 0, 0, tiled=False).reshape(rows, cols)  13 us
    all_to_all x1, waiting for transfers between devices, per_device(): received = lax.all_to_all(mixed_in, 'mp', 0, 0, tiled=False)  9.18 us
    all_to_all x1, starting transfers between devices, per_device(): received = lax.all_to_all(mixed_in, 'mp', 0, 0, tiled=False)  6.27 us
  transfers between devices with their start and end apart: 4, of which 2 were waited for; matrix products, arithmetic and copies ran while one was open for 6% of the time, Pallas kernels for 38%

profile of v16, /device:TPU:0, one launch (start us, length us, event | category | flops | bytes accessed | tf_op | source)
XLA Modules:
  0.0 290.2 jit_solution(5752537423451476258)
XLA Ops:
  6.5 1.0 pad_maximum_fusion.1
  7.5 0.4 reshape.48
  8.0 42.9 %shard_map.118 = bf16[8,96,2048]{2,1,0:T(8,128)(2,1)} custom-call(bf16[96,2048]{1,0:T(8,128)(2,1)} %bitcast.80), custom_call_target="tpu_custom_call" | custom-call | tf_op jit(solution)/shard_map/pallas_call | solution.py:145
  50.9 2.7 fusion.2
  53.7 0.5 copy.53
  54.3 1.1 slice.38
  55.6 39.9 %all-gather = bf16[320,768]{1,0:T(8,128)(2,1)} all-gather(bf16[40,768]{1,0:T(8,128)(2,1)S(1)} %constant_dynamic-slice_fusion), channel_id=2, replica_groups=mesh['blk'=16,'mp'=8] {'mp'}, dimensions={0}, use_global_device_ids=true | all-gather | bytes 552960 | tf_op jit(solution)/shard_map/all_gather | solution.py:202
  95.5 19.2 %all-gather.5.cloned.1.call-done.kv_ref = bf16[32768,128]{1,0:T(8,128)(2,1)} async-done(((bf16[2048,128]{1,0:T(8,128)(2,1)}), bf16[32768,128]{1,0:T(8,128)(2,1)}) %all-gather.5.cloned.1.call-update) | async-done | bytes 8388624 | tf_op jit(solution)/shard_map/all_gather | solution.py:193
  114.7 0.8 copy_bitcast_fusion.1
  115.5 0.0 all-gather.9.cloned.1.call-start
  115.6 0.7 all-gather.9.cloned.1.call-update
  116.3 0.1 slice_multiply_fusion
  116.4 0.9 concatenate.14.q_ref
  117.3 108.9 %shard_map.119 = bf16[2048,64]{1,0:T(8,128)(2,1)} custom-call(bf16[2048,128]{1,0:T(8,128)(2,1)} %concatenate.14.q_ref, bf16[32768,128]{1,0:T(8,128)(2,1)} %all-gather.5.cloned.1.call-done.kv_ref), custom_call_target="tpu_custom_call" | custom-call | flops 34359738368 | bytes 17563648 | tf_op jit(solution)/shard_map/pallas_call | solution.py:75
  226.2 1.2 copy.56
  227.5 3.6 %gather_fusion = bf16[64,128,96]{1,2,0:T(8,128)(2,1)S(1)} fusion(bf16[256,128,96]{1,2,0:T(8,128)(2,1)} %all-gather.7.cloned.1.call-done, s32[1024]{0:T(1024)S(1)} %pad_clamp_fusion), kind=kCustom, calls=%fused_computation | custom fusion | bytes 3145984 | tf_op jit(solution)/shard_map/jit(_take)/gather | solution.py:22
  231.2 3.8 %fusion.9 = f32[64,128,96]{1,2,0:T(8,128)S(1)} fusion(s32[64,128,128]{2,1,0:T(8,128)} %param.15, bf16[64,128,96]{1,2,0:T(8,128)(2,1)S(1)} %gather_fusion, pred[64]{0:T(512)(128)(4,1)S(1)} %get-tuple-element.13), kind=kOutput, calls=%fused_computation.11 | convolution fusion | flops 203161600 | bytes 8912960 | tf_op jit(solution)/shard_map/ers,esf->erf/dot_general | solution.py:23
  235.0 2.9 %fusion.24 = f32[16,128,96]{1,0,2:T(8,128)S(1)} fusion(f32[64,128,96]{1,2,0:T(8,128)S(1)} %fusion.9, s32[64]{0:T(128)S(1)} %copy-done.6), kind=kOutput, calls=%fused_computation.21 | convolution fusion | flops 151192576 | bytes 3932416 | tf_op jit(solution)/shard_map/cy,cla->yla/dot_general | solution.py:32
  237.9 0.3 fusion.46
  238.3 0.9 copy.88
  239.2 6.3 %all-to-all-start = ((bf16[8,256,160]{1,2,0:T(8,128)(2,1)}), bf16[8,256,160]{1,2,0:T(8,128)(2,1)}, u32[]{:S(2)}, u32[]{:S(2)}) async-start(bf16[8,256,160]{1,2,0:T(8,128)(2,1)} %bitcast.77), calls=%async_computation | async-start | bytes 1310720 | tf_op jit(solution)/shard_map/all_to_all | solution.py:221
  245.4 1.1 dynamic-slice_convert_fusion
  246.5 0.3 copy.59
  246.8 1.3 slice-done
  248.1 1.7 reshape.51
  249.8 9.2 %all-to-all-done = bf16[8,256,160]{1,2,0:T(8,128)(2,1)} async-done(((bf16[8,256,160]{1,2,0:T(8,128)(2,1)}), bf16[8,256,160]{1,2,0:T(8,128)(2,1)}, u32[]{:S(2)}, u32[]{:S(2)}) %all-to-all-start) | async-done | bytes 655392 | tf_op jit(solution)/shard_map/all_to_all | solution.py:221
  259.0 1.6 convolution_bitcast_fusion.1
  260.6 3.8 %fusion.66 = (f32[256]{0:T(256)S(1)}, f32[256]{0:T(256)S(1)}, f32[256,768]{1,0:T(8,128)}) fusion(f32[256,768]{1,0:T(8,128)S(1)} %convolution_bitcast_fusion.1, f32[256,768]{1,0:T(8,128)S(1)} %copy.59, bf16[8,640,768]{2,1,0:T(8,128)(2,1)} %all-gather.9.cloned.1.call-done, bf16[8,96,8,96]{3,2,1,0:T(8,128)(2,1)S(1)} %reshape.51, ...), kind=kOutput, calls=%fused_computation.66 | convolution fusion | flops 605355520 | bytes 5113856 | tf_op jit(solution)/shard_map/rjc,jce->re/dot_general | solution.py:239
  264.4 5.3 %fusion.35 = bf16[256,768]{1,0:T(8,128)(2,1)S(1)} fusion(f32[256,768]{1,0:T(8,128)} %get-tuple-element.17, bf16[8,640,768]{2,1,0:T(8,128)(2,1)} %all-gather.9.cloned.1.call-done, f32[256]{0:T(256)S(1)} %get-tuple-element.16, f32[256]{0:T(256)S(1)} %get-tuple-element.15), kind=kOutput, calls=%fused_computation.26 | convolution fusion | flops 1209729024 | bytes 6686720 | tf_op jit(solution)/shard_map/rjc,jce->re/dot_general | solution.py:252
  269.7 0.2 copy.60
  269.9 13.0 %all_to_all.10 = bf16[8,256,96]{1,2,0:T(8,128)(2,1)S(1)} all-to-all(bf16[8,256,96]{1,2,0:T(8,128)(2,1)S(1)} %bitcast.85), channel_id=1, replica_groups=mesh['blk'=16,'mp'=8] {'mp'}, dimensions={0} | all-to-all | bytes 786432 | tf_op jit(solution)/shard_map/all_to_all | solution.py:255
  282.9 0.8 copy.65
  (33 shorter events, 0.3 us)
Async XLA Ops:
  6.5 108.2 %all-gather.5.cloned.1.call-start = ((), (), s32[]{:S(2)}) async-start(), calls=%async_computation.2 | async-start | bytes 8912896 | tf_op jit(solution)/shard_map/all_gather | solution.py:193
  53.7 1.7 copy-start.3
  53.7 1.7 copy-start.1
  53.7 1.8 copy-start.4
  53.7 1.8 copy-start.5
  53.7 1.8 copy-start.2
  54.3 60.4 %copy-start = (bf16[2048,96]{0,1:T(8,128)(2,1)S(1)}, bf16[2048,96]{0,1:T(8,128)(2,1)}, u32[]{:S(2)}) copy-start(bf16[2048,96]{0,1:T(8,128)(2,1)} %param.12) | copy-start | bytes 1179652
  55.3 172.1 %all-gather.7.cloned.1.call-start = ((), (), s32[]{:S(2)}) async-start(), calls=%async_computation.3 | async-start | bytes 6684672 | tf_op jit(solution)/shard_map/all_gather | solution.py:204
  55.6 61.7 %copy-start.7 = (s32[64]{0:T(128)S(1)}, s32[64]{0:T(128)}, u32[]{:S(2)}) copy-start(s32[64]{0:T(128)} %param.14) | copy-start | bytes 772
  115.5 131.3 %all-gather.9.cloned.1.call-start = ((), (), s32[]{:S(2)}) async-start(), calls=%async_computation.4 | async-start | bytes 8355840 | tf_op jit(solution)/shard_map/all_gather | solution.py:207
  231.1 3.8 %copy-start.6 = (s32[64]{0:T(128)S(1)}, s32[64]{0:T(128)}, u32[]{:S(2)}) copy-start(s32[64]{0:T(128)} %param.13) | copy-start | bytes 772
  239.2 19.8 %all-to-all-start = ((bf16[8,256,160]{1,2,0:T(8,128)(2,1)}), bf16[8,256,160]{1,2,0:T(8,128)(2,1)}, u32[]{:S(2)}, u32[]{:S(2)}) async-start(bf16[8,256,160]{1,2,0:T(8,128)(2,1)} %bitcast.77), calls=%async_computation | async-start | bytes 1310720 | tf_op jit(solution)/shard_map/all_to_all | solution.py:221
  246.8 1.3 slice-start
Sparse Core Ops, SparseCore 0:
  55.5 59.1 all-gather.4
  116.4 42.6 all-gather.6
  160.8 50.4 all-gather.8

commit v17 on v16

--- a/solution.py
+++ b/solution.py
@@ -217,7 +217,11 @@
     gathered = neighbour_sum(features, edge_dst, edge_src, edge_mask, all_features)
     local_share = (features.astype(jnp.float32) + gathered * 0.25).astype(jnp.bfloat16)
 
-    mixed_in = jnp.concatenate([local_share, attended], axis=1).reshape(n_mp, share, -1)
+    mixed_in = (
+        jnp.concatenate([local_share, attended], axis=1)
+        .T.reshape(-1, n_mp, share)
+        .transpose(1, 0, 2)
+    )
     received = lax.all_to_all(mixed_in, "mp", 0, 0, tiled=False)
     own_rows = (
         lax.dynamic_slice_in_dim(feature_parts_t, me * share, share, 2)
@@ -228,8 +232,8 @@
 
     local_hidden = jax.nn.relu(
         jnp.einsum(
-            "jrc,pqjc->rpq",
-            received[:, :, :cols],
+            "jcr,pqjc->rpq",
+            received[:, :cols, :],
             gin_in_t.reshape(n_mp, cols, n_mp, cols),
             preferred_element_type=jnp.float32,
         )
@@ -237,7 +241,7 @@
     mixed = (
         own_rows
         + jnp.einsum("rjc,jce->re", local_hidden, gin_out_parts, preferred_element_type=jnp.float32)
-        + jnp.einsum("jrd,jde->re", received[:, :, cols:], attn_out_parts, preferred_element_type=jnp.float32)
+        + jnp.einsum("jdr,jde->re", received[:, cols:, :], attn_out_parts, preferred_element_type=jnp.float32)
     )
     row_average = jnp.sum(mixed, axis=1, keepdims=True) / width
     square_row = jnp.sum(mixed * mixed, axis=1, keepdims=True) / width

time: 291 us -> 291 us (level)
  no operation moved by 1% of the time
where the time goes in v17:
time: 291 us; the launch traced here: 290 us
  Pallas kernels  152 us (52%)
  blocking collectives  52.9 us (18%)
  waiting for transfers between devices  29.1 us (10%)
  matrix products  20.2 us (7%)
  local copies, waits for them, and re-layouts  13.8 us (5%)
  between operations  13.4 us (5%)
  starting transfers between devices  6.35 us (2%)
    pallas_call x1, Pallas kernels, flash_attention(): pl.pallas_call(functools.partial(flash_kernel, dim), grid=grid, in_specs=...  109 us
    pallas_call x1, Pallas kernels, dma_exchange(): pl.pallas_call(functools.partial(exchange_kernel, axis, n, scatter), in_s...  42.9 us
    all_gather x1, blocking collectives, per_device(): piece_parts = lax.all_gather(piece, 'mp', axis=0, tiled=False)  39.9 us
    all_gather x1, waiting for transfers between devices, per_device(): lax.all_gather(projected[:, HEAD_DIM * heads:], 'blk', axis=0, tiled=True)  19.2 us
    all_to_all x1, blocking collectives, per_device(): lax.all_to_all(out_parts, 'mp', 0, 0, tiled=False).reshape(rows, cols)  13 us
    all_to_all x1, waiting for transfers between devices, per_device(): received = lax.all_to_all(mixed_in, 'mp', 0, 0, tiled=False)  9.18 us
    all_to_all x1, starting transfers between devices, per_device(): received = lax.all_to_all(mixed_in, 'mp', 0, 0, tiled=False)  6.27 us
  transfers between devices with their start and end apart: 4, of which 2 were waited for; matrix products, arithmetic and copies ran while one was open for 6% of the time, Pallas kernels for 38%

profile of v17, /device:TPU:0, one launch (start us, length us, event | category | flops | bytes accessed | tf_op | source)
XLA Modules:
  0.0 290.2 jit_solution(9367323557734309994)
XLA Ops:
  6.5 1.0 pad_maximum_fusion.1
  7.5 0.4 reshape.48
  8.0 42.9 %shard_map.118 = bf16[8,96,2048]{2,1,0:T(8,128)(2,1)} custom-call(bf16[96,2048]{1,0:T(8,128)(2,1)} %bitcast.84), custom_call_target="tpu_custom_call" | custom-call | tf_op jit(solution)/shard_map/pallas_call | solution.py:145
  50.9 2.7 fusion.2
  53.7 0.5 copy.53
  54.3 1.1 slice.38
  55.6 39.9 %all-gather = bf16[320,768]{1,0:T(8,128)(2,1)} all-gather(bf16[40,768]{1,0:T(8,128)(2,1)S(1)} %constant_dynamic-slice_fusion), channel_id=2, replica_groups=mesh['blk'=16,'mp'=8] {'mp'}, dimensions={0}, use_global_device_ids=true | all-gather | bytes 552960 | tf_op jit(solution)/shard_map/all_gather | solution.py:202
  95.5 19.2 %all-gather.5.cloned.1.call-done.kv_ref = bf16[32768,128]{1,0:T(8,128)(2,1)} async-done(((bf16[2048,128]{1,0:T(8,128)(2,1)}), bf16[32768,128]{1,0:T(8,128)(2,1)}) %all-gather.5.cloned.1.call-update) | async-done | bytes 8388624 | tf_op jit(solution)/shard_map/all_gather | solution.py:193
  114.7 0.8 copy_bitcast_fusion
  115.5 0.0 all-gather.9.cloned.1.call-start
  115.6 0.7 all-gather.9.cloned.1.call-update
  116.3 0.1 slice_multiply_fusion
  116.4 0.9 concatenate.14.q_ref
  117.3 108.9 %shard_map.119 = bf16[2048,64]{1,0:T(8,128)(2,1)} custom-call(bf16[2048,128]{1,0:T(8,128)(2,1)} %concatenate.14.q_ref, bf16[32768,128]{1,0:T(8,128)(2,1)} %all-gather.5.cloned.1.call-done.kv_ref), custom_call_target="tpu_custom_call" | custom-call | flops 34359738368 | bytes 17563648 | tf_op jit(solution)/shard_map/pallas_call | solution.py:75
  226.2 1.2 copy.56
  227.5 3.6 %gather_fusion = bf16[64,128,96]{1,2,0:T(8,128)(2,1)S(1)} fusion(bf16[256,128,96]{1,2,0:T(8,128)(2,1)} %all-gather.7.cloned.1.call-done, s32[1024]{0:T(1024)S(1)} %pad_clamp_fusion), kind=kCustom, calls=%fused_computation | custom fusion | bytes 3145984 | tf_op jit(solution)/shard_map/jit(_take)/gather | solution.py:22
  231.2 3.8 %fusion.9 = f32[64,128,96]{1,2,0:T(8,128)S(1)} fusion(s32[64,128,128]{2,1,0:T(8,128)} %param.15, bf16[64,128,96]{1,2,0:T(8,128)(2,1)S(1)} %gather_fusion, pred[64]{0:T(512)(128)(4,1)S(1)} %get-tuple-element.13), kind=kOutput, calls=%fused_computation.11 | convolution fusion | flops 203161600 | bytes 8912960 | tf_op jit(solution)/shard_map/ers,esf->erf/dot_general | solution.py:23
  235.0 2.9 %fusion.24 = f32[16,128,96]{1,0,2:T(8,128)S(1)} fusion(f32[64,128,96]{1,2,0:T(8,128)S(1)} %fusion.9, s32[64]{0:T(128)S(1)} %copy-done.6), kind=kOutput, calls=%fused_computation.21 | convolution fusion | flops 151192576 | bytes 3932416 | tf_op jit(solution)/shard_map/cy,cla->yla/dot_general | solution.py:32
  237.9 0.3 fusion.46
  238.3 0.9 copy.88
  239.2 6.3 %all-to-all-start = ((bf16[8,160,256]{2,1,0:T(8,128)(2,1)}), bf16[8,160,256]{2,1,0:T(8,128)(2,1)}, u32[]{:S(2)}, u32[]{:S(2)}) async-start(bf16[8,160,256]{2,1,0:T(8,128)(2,1)} %bitcast.81), calls=%async_computation | async-start | bytes 1310720 | tf_op jit(solution)/shard_map/all_to_all | solution.py:225
  245.4 1.1 dynamic-slice_convert_fusion
  246.5 0.3 copy.59
  246.8 1.3 slice-done
  248.1 1.7 reshape.51
  249.8 9.2 %all-to-all-done = bf16[8,160,256]{2,1,0:T(8,128)(2,1)} async-done(((bf16[8,160,256]{2,1,0:T(8,128)(2,1)}), bf16[8,160,256]{2,1,0:T(8,128)(2,1)}, u32[]{:S(2)}, u32[]{:S(2)}) %all-to-all-start) | async-done | bytes 655392 | tf_op jit(solution)/shard_map/all_to_all | solution.py:225
  259.0 1.6 convolution_bitcast_fusion.1
  260.6 3.8 %fusion.66 = (f32[256]{0:T(256)S(1)}, f32[256]{0:T(256)S(1)}, f32[256,768]{1,0:T(8,128)}) fusion(f32[256,768]{1,0:T(8,128)S(1)} %convolution_bitcast_fusion.1, f32[256,768]{1,0:T(8,128)S(1)} %copy.59, bf16[8,640,768]{2,1,0:T(8,128)(2,1)} %all-gather.9.cloned.1.call-done, bf16[8,96,8,96]{3,2,1,0:T(8,128)(2,1)S(1)} %reshape.51, ...), kind=kOutput, calls=%fused_computation.66 | convolution fusion | flops 605355520 | bytes 5113856 | tf_op jit(solution)/shard_map/rjc,jce->re/dot_general | solution.py:243
  264.4 5.3 %fusion.35 = bf16[256,768]{1,0:T(8,128)(2,1)S(1)} fusion(f32[256,768]{1,0:T(8,128)} %get-tuple-element.17, bf16[8,640,768]{2,1,0:T(8,128)(2,1)} %all-gather.9.cloned.1.call-done, f32[256]{0:T(256)S(1)} %get-tuple-element.16, f32[256]{0:T(256)S(1)} %get-tuple-element.15), kind=kOutput, calls=%fused_computation.26 | convolution fusion | flops 1209729024 | bytes 6686720 | tf_op jit(solution)/shard_map/rjc,jce->re/dot_general | solution.py:256
  269.7 0.2 copy.60
  269.9 13.0 %all_to_all.10 = bf16[8,256,96]{1,2,0:T(8,128)(2,1)S(1)} all-to-all(bf16[8,256,96]{1,2,0:T(8,128)(2,1)S(1)} %bitcast.89), channel_id=1, replica_groups=mesh['blk'=16,'mp'=8] {'mp'}, dimensions={0} | all-to-all | bytes 786432 | tf_op jit(solution)/shard_map/all_to_all | solution.py:259
  282.9 0.8 copy.65
  (33 shorter events, 0.3 us)
Async XLA Ops:
  6.5 108.2 %all-gather.5.cloned.1.call-start = ((), (), s32[]{:S(2)}) async-start(), calls=%async_computation.2 | async-start | bytes 8912896 | tf_op jit(solution)/shard_map/all_gather | solution.py:193
  53.7 1.7 copy-start.3
  53.7 1.7 copy-start.1
  53.7 1.8 copy-start.4
  53.7 1.8 copy-start.5
  53.7 1.8 copy-start.2
  54.3 60.4 %copy-start = (bf16[2048,96]{0,1:T(8,128)(2,1)S(1)}, bf16[2048,96]{0,1:T(8,128)(2,1)}, u32[]{:S(2)}) copy-start(bf16[2048,96]{0,1:T(8,128)(2,1)} %param.12) | copy-start | bytes 1179652
  55.3 172.1 %all-gather.7.cloned.1.call-start = ((), (), s32[]{:S(2)}) async-start(), calls=%async_computation.3 | async-start | bytes 6684672 | tf_op jit(solution)/shard_map/all_gather | solution.py:204
  55.6 61.7 %copy-start.7 = (s32[64]{0:T(128)S(1)}, s32[64]{0:T(128)}, u32[]{:S(2)}) copy-start(s32[64]{0:T(128)} %param.14) | copy-start | bytes 772
  115.5 131.3 %all-gather.9.cloned.1.call-start = ((), (), s32[]{:S(2)}) async-start(), calls=%async_computation.4 | async-start | bytes 8355840 | tf_op jit(solution)/shard_map/all_gather | solution.py:207
  231.1 3.8 %copy-start.6 = (s32[64]{0:T(128)S(1)}, s32[64]{0:T(128)}, u32[]{:S(2)}) copy-start(s32[64]{0:T(128)} %param.13) | copy-start | bytes 772
  239.2 19.8 %all-to-all-start = ((bf16[8,160,256]{2,1,0:T(8,128)(2,1)}), bf16[8,160,256]{2,1,0:T(8,128)(2,1)}, u32[]{:S(2)}, u32[]{:S(2)}) async-start(bf16[8,160,256]{2,1,0:T(8,128)(2,1)} %bitcast.81), calls=%async_computation | async-start | bytes 1310720 | tf_op jit(solution)/shard_map/all_to_all | solution.py:225
  246.8 1.3 slice-start
Sparse Core Ops, SparseCore 0:
  55.5 59.1 all-gather.4
  116.4 42.6 all-gather.6
  160.8 50.4 all-gather.8

commit v18 on v17

--- a/solution.py
+++ b/solution.py
@@ -255,8 +255,9 @@
         mixed
         + jnp.einsum("rjc,jce->re", ffn_hidden, ffn_out_parts, preferred_element_type=jnp.float32)
     ).astype(jnp.bfloat16)
-    out_parts = out_rows.reshape(share, n_mp, cols).transpose(1, 0, 2)
-    return lax.all_to_all(out_parts, "mp", 0, 0, tiled=False).reshape(rows, cols)
+    out_parts = out_rows.T.reshape(n_mp, cols, share)
+    received_out = lax.all_to_all(out_parts, "mp", 0, 0, tiled=False)
+    return received_out.transpose(1, 0, 2).reshape(cols, rows).T
 
 
 def solution(mesh):

time: 291 us -> 291 us (level)
  no operation moved by 1% of the time
where the time goes in v18:
time: 291 us; the launch traced here: 290 us
  Pallas kernels  152 us (52%)
  blocking collectives  52.9 us (18%)
  waiting for transfers between devices  29.1 us (10%)
  matrix products  20.2 us (7%)
  local copies, waits for them, and re-layouts  13.8 us (5%)
  between operations  13.4 us (5%)
  starting transfers between devices  6.35 us (2%)
    pallas_call x1, Pallas kernels, flash_attention(): pl.pallas_call(functools.partial(flash_kernel, dim), grid=grid, in_specs=...  109 us
    pallas_call x1, Pallas kernels, dma_exchange(): pl.pallas_call(functools.partial(exchange_kernel, axis, n, scatter), in_s...  42.9 us
    all_gather x1, blocking collectives, per_device(): piece_parts = lax.all_gather(piece, 'mp', axis=0, tiled=False)  39.9 us
    all_gather x1, waiting for transfers between devices, per_device(): lax.all_gather(projected[:, HEAD_DIM * heads:], 'blk', axis=0, tiled=True)  19.2 us
    all_to_all x1, blocking collectives, per_device(): received_out = lax.all_to_all(out_parts, 'mp', 0, 0, tiled=False)  13 us
    all_to_all x1, waiting for transfers between devices, per_device(): received = lax.all_to_all(mixed_in, 'mp', 0, 0, tiled=False)  9.18 us
    all_to_all x1, starting transfers between devices, per_device(): received = lax.all_to_all(mixed_in, 'mp', 0, 0, tiled=False)  6.27 us
  transfers between devices with their start and end apart: 4, of which 2 were waited for; matrix products, arithmetic and copies ran while one was open for 6% of the time, Pallas kernels for 38%

profile of v18, /device:TPU:0, one launch (start us, length us, event | category | flops | bytes accessed | tf_op | source)
XLA Modules:
  0.0 290.2 jit_solution(9367323557734309994)
XLA Ops:
  6.5 1.0 pad_maximum_fusion.1
  7.5 0.4 reshape.48
  8.0 42.9 %shard_map.118 = bf16[8,96,2048]{2,1,0:T(8,128)(2,1)} custom-call(bf16[96,2048]{1,0:T(8,128)(2,1)} %bitcast.89), custom_call_target="tpu_custom_call" | custom-call | tf_op jit(solution)/shard_map/pallas_call | solution.py:145
  50.9 2.7 fusion.2
  53.7 0.5 copy.53
  54.3 1.1 slice.38
  55.6 39.9 %all-gather = bf16[320,768]{1,0:T(8,128)(2,1)} all-gather(bf16[40,768]{1,0:T(8,128)(2,1)S(1)} %constant_dynamic-slice_fusion), channel_id=2, replica_groups=mesh['blk'=16,'mp'=8] {'mp'}, dimensions={0}, use_global_device_ids=true | all-gather | bytes 552960 | tf_op jit(solution)/shard_map/all_gather | solution.py:202
  95.5 19.2 %all-gather.5.cloned.1.call-done.kv_ref = bf16[32768,128]{1,0:T(8,128)(2,1)} async-done(((bf16[2048,128]{1,0:T(8,128)(2,1)}), bf16[32768,128]{1,0:T(8,128)(2,1)}) %all-gather.5.cloned.1.call-update) | async-done | bytes 8388624 | tf_op jit(solution)/shard_map/all_gather | solution.py:193
  114.7 0.8 copy_bitcast_fusion
  115.5 0.0 all-gather.9.cloned.1.call-start
  115.6 0.7 all-gather.9.cloned.1.call-update
  116.3 0.1 slice_multiply_fusion
  116.4 0.9 concatenate.14.q_ref
  117.3 108.9 %shard_map.119 = bf16[2048,64]{1,0:T(8,128)(2,1)} custom-call(bf16[2048,128]{1,0:T(8,128)(2,1)} %concatenate.14.q_ref, bf16[32768,128]{1,0:T(8,128)(2,1)} %all-gather.5.cloned.1.call-done.kv_ref), custom_call_target="tpu_custom_call" | custom-call | flops 34359738368 | bytes 17563648 | tf_op jit(solution)/shard_map/pallas_call | solution.py:75
  226.2 1.2 copy.56
  227.5 3.6 %gather_fusion = bf16[64,128,96]{1,2,0:T(8,128)(2,1)S(1)} fusion(bf16[256,128,96]{1,2,0:T(8,128)(2,1)} %all-gather.7.cloned.1.call-done, s32[1024]{0:T(1024)S(1)} %pad_clamp_fusion), kind=kCustom, calls=%fused_computation | custom fusion | bytes 3145984 | tf_op jit(solution)/shard_map/jit(_take)/gather | solution.py:22
  231.2 3.8 %fusion.9 = f32[64,128,96]{1,2,0:T(8,128)S(1)} fusion(s32[64,128,128]{2,1,0:T(8,128)} %param.15, bf16[64,128,96]{1,2,0:T(8,128)(2,1)S(1)} %gather_fusion, pred[64]{0:T(512)(128)(4,1)S(1)} %get-tuple-element.13), kind=kOutput, calls=%fused_computation.11 | convolution fusion | flops 203161600 | bytes 8912960 | tf_op jit(solution)/shard_map/ers,esf->erf/dot_general | solution.py:23
  235.0 2.9 %fusion.24 = f32[16,128,96]{1,0,2:T(8,128)S(1)} fusion(f32[64,128,96]{1,2,0:T(8,128)S(1)} %fusion.9, s32[64]{0:T(128)S(1)} %copy-done.6), kind=kOutput, calls=%fused_computation.21 | convolution fusion | flops 151192576 | bytes 3932416 | tf_op jit(solution)/shard_map/cy,cla->yla/dot_general | solution.py:32
  237.9 0.3 fusion.49
  238.3 0.9 copy.88
  239.2 6.3 %all-to-all-start = ((bf16[8,160,256]{2,1,0:T(8,128)(2,1)}), bf16[8,160,256]{2,1,0:T(8,128)(2,1)}, u32[]{:S(2)}, u32[]{:S(2)}) async-start(bf16[8,160,256]{2,1,0:T(8,128)(2,1)} %bitcast.86), calls=%async_computation | async-start | bytes 1310720 | tf_op jit(solution)/shard_map/all_to_all | solution.py:225
  245.4 1.1 dynamic-slice_convert_fusion
  246.5 0.3 copy.59
  246.8 1.3 slice-done
  248.1 1.7 reshape.51
  249.8 9.2 %all-to-all-done = bf16[8,160,256]{2,1,0:T(8,128)(2,1)} async-done(((bf16[8,160,256]{2,1,0:T(8,128)(2,1)}), bf16[8,160,256]{2,1,0:T(8,128)(2,1)}, u32[]{:S(2)}, u32[]{:S(2)}) %all-to-all-start) | async-done | bytes 655392 | tf_op jit(solution)/shard_map/all_to_all | solution.py:225
  259.0 1.6 convolution_bitcast_fusion.1
  260.6 3.8 %fusion.69 = (f32[256]{0:T(256)S(1)}, f32[256]{0:T(256)S(1)}, f32[256,768]{1,0:T(8,128)}) fusion(f32[256,768]{1,0:T(8,128)S(1)} %convolution_bitcast_fusion.1, f32[256,768]{1,0:T(8,128)S(1)} %copy.59, bf16[8,640,768]{2,1,0:T(8,128)(2,1)} %all-gather.9.cloned.1.call-done, bf16[8,96,8,96]{3,2,1,0:T(8,128)(2,1)S(1)} %reshape.51, ...), kind=kOutput, calls=%fused_computation.67 | convolution fusion | flops 605355520 | bytes 5113856 | tf_op jit(solution)/shard_map/rjc,jce->re/dot_general | solution.py:243
  264.4 5.3 %fusion.41 = bf16[768,256]{0,1:T(8,128)(2,1)S(1)} fusion(f32[256,768]{1,0:T(8,128)} %get-tuple-element.17, bf16[8,640,768]{2,1,0:T(8,128)(2,1)} %all-gather.9.cloned.1.call-done, f32[256]{0:T(256)S(1)} %get-tuple-element.16, f32[256]{0:T(256)S(1)} %get-tuple-element.15), kind=kOutput, calls=%fused_computation.28 | convolution fusion | flops 1209729024 | bytes 6686720 | tf_op jit(solution)/shard_map/rjc,jce->re/dot_general | solution.py:256
  269.7 0.2 copy.60
  269.9 13.0 %all_to_all.10 = bf16[8,96,256]{2,1,0:T(8,128)(2,1)S(1)} all-to-all(bf16[8,96,256]{2,1,0:T(8,128)(2,1)S(1)} %bitcast.94), channel_id=1, replica_groups=mesh['blk'=16,'mp'=8] {'mp'}, dimensions={0} | all-to-all | bytes 786432 | tf_op jit(solution)/shard_map/all_to_all | solution.py:259
  282.9 0.8 copy.65
  (33 shorter events, 0.3 us)
Async XLA Ops:
  6.5 108.2 %all-gather.5.cloned.1.call-start = ((), (), s32[]{:S(2)}) async-start(), calls=%async_computation.2 | async-start | bytes 8912896 | tf_op jit(solution)/shard_map/all_gather | solution.py:193
  53.7 1.7 copy-start.3
  53.7 1.7 copy-start.1
  53.7 1.8 copy-start.4
  53.7 1.8 copy-start.5
  53.7 1.8 copy-start.2
  54.3 60.4 %copy-start = (bf16[2048,96]{0,1:T(8,128)(2,1)S(1)}, bf16[2048,96]{0,1:T(8,128)(2,1)}, u32[]{:S(2)}) copy-start(bf16[2048,96]{0,1:T(8,128)(2,1)} %param.12) | copy-start | bytes 1179652
  55.3 172.1 %all-gather.7.cloned.1.call-start = ((), (), s32[]{:S(2)}) async-start(), calls=%async_computation.3 | async-start | bytes 6684672 | tf_op jit(solution)/shard_map/all_gather | solution.py:204
  55.6 61.7 %copy-start.7 = (s32[64]{0:T(128)S(1)}, s32[64]{0:T(128)}, u32[]{:S(2)}) copy-start(s32[64]{0:T(128)} %param.14) | copy-start | bytes 772
  115.5 131.3 %all-gather.9.cloned.1.call-start = ((), (), s32[]{:S(2)}) async-start(), calls=%async_computation.4 | async-start | bytes 8355840 | tf_op jit(solution)/shard_map/all_gather | solution.py:207
  231.1 3.8 %copy-start.6 = (s32[64]{0:T(128)S(1)}, s32[64]{0:T(128)}, u32[]{:S(2)}) copy-start(s32[64]{0:T(128)} %param.13) | copy-start | bytes 772
  239.2 19.8 %all-to-all-start = ((bf16[8,160,256]{2,1,0:T(8,128)(2,1)}), bf16[8,160,256]{2,1,0:T(8,128)(2,1)}, u32[]{:S(2)}, u32[]{:S(2)}) async-start(bf16[8,160,256]{2,1,0:T(8,128)(2,1)} %bitcast.86), calls=%async_computation | async-start | bytes 1310720 | tf_op jit(solution)/shard_map/all_to_all | solution.py:225
  246.8 1.3 slice-start
Sparse Core Ops, SparseCore 0:
  55.5 59.1 all-gather.4
  116.4 42.6 all-gather.6
  160.8 50.4 all-gather.8
